TPU v7x, 512 devices: a whole 4x4x16 slice. The times are simulated.
512 devices in a mesh: tm: 16 (over x, z_hi, core), rep: 32 (over y, z_lo).
Axes of the slice: x: 4, y: 4, z: 16 (z_hi: 2, z_lo: 8; z = z_hi * 8 + z_lo), core: 2. Of those that a mesh axis runs over, the one named last changes fastest.
Arguments:
- samples: bfloat16 [32, 8192, 512], P('rep', 'tm'), may hold values from -5 to 5
- grad_out: bfloat16 [32, 8192, 512], P('rep', 'tm'), may hold values from -4 to 4
- w_conv: bfloat16 [1024, 1024], replicated, may hold values from -0.1875 to 0.1875
- w_res: bfloat16 [512, 512], replicated, may hold values from -0.25 to 0.25
- lengths: int32 [32], P('rep'), may hold values from 2048 to 8192
Outputs:
- grad_in: bfloat16 [32, 8192, 512], P('rep', 'tm')
- grad_conv: float32 [1024, 1024], P('tm', 'rep')
- grad_res: float32 [512, 512], P('tm', 'rep')
All inputs are finite; a program needn't handle non-finite values.
Results may differ from a plain program's by a relative error of at most 0.015.
Values may be sent and summed in bfloat16 or wider, within the bound.
A program may use at most 64 MiB of HBM per device.

v0:
```python
import jax
import jax.numpy as jnp
from jax import lax
from jax.sharding import PartitionSpec as P

DILATION_STEP = 256


def passed_along(array, axis, by):
    length = lax.axis_size(axis)
    pairs = [(i, i + by) for i in range(length) if 0 <= i + by < length]
    return lax.ppermute(array, axis, pairs)


def gate_backward(inputs, cotangent, in_length, w_conv, w_res):
    channel_count = w_res.shape[0]
    pre_act = jnp.dot(inputs, w_conv, preferred_element_type=jnp.float32)
    tanh_f = jnp.tanh(pre_act[:, :channel_count])
    sig_g = jax.nn.sigmoid(pre_act[:, channel_count:])
    gated = (in_length * tanh_f * sig_g).astype(jnp.bfloat16)
    gated_grad = in_length * jnp.dot(cotangent, w_res.T, preferred_element_type=jnp.float32)
    pre_grad = jnp.concatenate(
        [gated_grad * sig_g * (1.0 - tanh_f * tanh_f), gated_grad * tanh_f * sig_g * (1.0 - sig_g)],
        1,
    ).astype(jnp.bfloat16)
    return (gated, pre_grad)


def body(samples, grad_out, w_conv, w_res, lengths):
    sequence_rows = samples[0]
    cotangent = grad_out[0]
    seq_len = lengths[0]
    count_of_rows = sequence_rows.shape[0]
    channel_count = sequence_rows.shape[1]
    start_row = lax.axis_index("tm") * count_of_rows
    trailing_rows = sequence_rows[count_of_rows - DILATION_STEP :]
    arrived_gradient = passed_along(trailing_rows, "tm", 1)
    prior_samples = jnp.concatenate(
        [arrived_gradient, sequence_rows[: count_of_rows - DILATION_STEP]], 0
    )
    inputs = jnp.concatenate([prior_samples, sequence_rows], 1)
    in_length = (start_row + jnp.arange(count_of_rows) < seq_len).astype(jnp.float32)[:, None]
    gated, pre_grad = gate_backward(inputs, cotangent, in_length, w_conv, w_res)
    input_gradient = jnp.dot(pre_grad, w_conv.T, preferred_element_type=jnp.float32)
    incoming_gradient = passed_along(input_gradient[:DILATION_STEP, :channel_count], "tm", -1)
    delayed_gradient = jnp.concatenate(
        [input_gradient[DILATION_STEP:, :channel_count], incoming_gradient], 0
    )
    grad_rows = (
        cotangent.astype(jnp.float32) + input_gradient[:, channel_count:] + delayed_gradient
    ).astype(jnp.bfloat16)
    term_conv = jnp.einsum("tk,tn->kn", inputs, pre_grad, preferred_element_type=jnp.float32)
    term_res = jnp.einsum("tk,tn->kn", gated, cotangent, preferred_element_type=jnp.float32)
    part_conv, part_res = (
        lax.psum_scatter(
            term_conv.astype(jnp.bfloat16), "tm", scatter_dimension=0, tiled=True
        ).astype(jnp.float32),
        lax.psum_scatter(
            term_res.astype(jnp.bfloat16), "tm", scatter_dimension=0, tiled=True
        ).astype(jnp.float32),
    )
    sum_conv, sum_res = (
        lax.psum_scatter(part_conv, "rep", scatter_dimension=1, tiled=True),
        lax.psum_scatter(part_res, "rep", scatter_dimension=1, tiled=True),
    )
    all_tokens = count_of_rows * lax.axis_size("tm") * lax.axis_size("rep")
    grad_scale = float(all_tokens) ** (-0.5)
    return (grad_rows[None], sum_conv * grad_scale, sum_res * grad_scale)


def solution(mesh):
    return jax.shard_map(
        body,
        mesh=mesh,
        in_specs=(P("rep", "tm", None), P("rep", "tm", None), P(), P(), P("rep")),
        out_specs=(P("rep", "tm", None), P("tm", "rep"), P("tm", "rep")),
        check_vma=False,
    )
```

profile of v0, /device:TPU:2, one launch (start us, length us, event | category | flops | bytes accessed | tf_op | source)
XLA Modules:
  0.0 738.0 jit_solution(11197141020937432639)
XLA Ops:
  7.2 0.0 reduce-scatter.11.cloned.1.call-start
  7.2 1.2 slice_bitcast_fusion.1
  8.4 1.9 collective-permute-start
  11.0 16.9 %collective-permute-done = bf16[256,512]{1,0:T(8,128)(2,1)S(1)} collective-permute-done((bf16[256,512]{1,0:T(8,128)(2,1)S(1)}, bf16[256,512]{1,0:T(8,128)(2,1)S(1)}, u32[]{:S(2)}, u32[]{:S(2)}) %collective-permute-start) | collective-permute-done | bytes 262176 | tf_op jit(solution)/shard_map/ppermute | solution.py:12
  27.9 2.4 fusion.10
  30.4 1.3 copy-done.9
  31.7 1.4 convolution_convert_fusion.1
  33.1 0.0 reduce-scatter.11.cloned.1.call-update
  33.2 0.0 reduce-scatter.9.cloned.1.call-start
  33.2 2.6 multiply_convert_fusion.2
  35.8 0.8 copy-done.6
  36.6 0.2 copy-done.8
  36.8 2.6 convolution_convert_fusion
  39.4 0.0 reduce-scatter.9.cloned.1.call-update
  39.4 0.0 reduce-scatter.15.cloned.1.call-start
  39.5 1.0 copy-done.7
  40.5 2.3 fusion.5
  42.8 1.3 copy-done.1
  44.1 0.9 fusion.16
  45.0 1.9 collective-permute-start.1
  46.9 95.7 %reduce-scatter.11.cloned.1.call-done = bf16[32,512]{1,0:T(8,128)(2,1)} async-done(((bf16[512,512]{1,0:T(8,128)(2,1)}), bf16[32,512]{1,0:T(8,128)(2,1)}) %reduce-scatter.11.cloned.1.call-update) | async-done | bytes 32784 | tf_op jit(solution)/shard_map/reduce_scatter | solution.py:58
  142.6 1.6 copy.19
  144.2 0.0 reduce-scatter.13.cloned.1.call-start
  144.2 117.1 %reduce-scatter.9.cloned.1.call-done = bf16[64,1024]{1,0:T(8,128)(2,1)} async-done(((bf16[1024,1024]{1,0:T(8,128)(2,1)}), bf16[64,1024]{1,0:T(8,128)(2,1)}) %reduce-scatter.9.cloned.1.call-update) | async-done | bytes 131088 | tf_op jit(solution)/shard_map/reduce_scatter | solution.py:55
  261.4 1.8 copy.17
  263.2 2.5 fusion.6
  265.7 229.4 %reduce-scatter.15.cloned.1.call-done = f32[16,32]{1,0:T(8,128)} async-done(((f32[512,32]{1,0:T(8,128)}), f32[16,32]{1,0:T(8,128)}) %reduce-scatter.15.cloned.1.call-update) | async-done | bytes 2064
  495.1 0.8 copy.20
  495.9 0.7 copy.15
  496.5 233.4 %reduce-scatter.13.cloned.1.call-done = f32[32,64]{1,0:T(8,128)} async-done(((f32[1024,64]{1,0:T(8,128)}), f32[32,64]{1,0:T(8,128)}) %reduce-scatter.13.cloned.1.call-update) | async-done | bytes 8208
  730.0 0.8 copy.18
  730.8 0.7 copy.14
  (21 shorter events, 0.1 us)
Async XLA Ops:
  7.2 20.8 %copy-start = (bf16[1024,1024]{1,0:T(8,128)(2,1)S(1)}, bf16[1024,1024]{1,0:T(8,128)(2,1)}, u32[]{:S(2)}) copy-start(bf16[1024,1024]{1,0:T(8,128)(2,1)} %param.7) | copy-start | bytes 6291460
  7.2 135.4 %reduce-scatter.11.cloned.1.call-start = ((), (), s32[]{:S(2)}) async-start(), calls=%async_computation.5 | async-start | bytes 557056 | tf_op jit(solution)/shard_map/reduce_scatter | solution.py:58
  8.4 19.5 %collective-permute-start = (bf16[256,512]{1,0:T(8,128)(2,1)S(1)}, bf16[256,512]{1,0:T(8,128)(2,1)S(1)}, u32[]{:S(2)}, u32[]{:S(2)}) collective-permute-start(bf16[256,512]{1,0:T(8,128)(2,1)S(1)} %get-tuple-element.13), channel_id=1, source_target_pairs={{0,32},{32,64},{64,96},{96,128},{128,160},{160,192},{192,224},{224... | collective-permute-start | bytes 786440 | tf_op jit(solution)/shard_map/ppermute | solution.py:12
  27.9 2.5 copy-start.4
  27.9 3.8 copy-start.3
  30.4 1.3 copy-start.9
  33.1 3.7 copy-start.2
  33.2 228.2 %reduce-scatter.9.cloned.1.call-start = ((), (), s32[]{:S(2)}) async-start(), calls=%async_computation.4 | async-start | bytes 2228224 | tf_op jit(solution)/shard_map/reduce_scatter | solution.py:55
  33.2 3.6 copy-start.5
  35.8 0.8 copy-start.6
  35.8 1.0 copy-start.8
  39.4 1.0 copy-start.7
  39.4 455.6 %reduce-scatter.15.cloned.1.call-start = ((), (), s32[]{:S(2)}) async-start(), calls=%async_computation.7 | async-start | bytes 270336
  42.8 1.3 copy-start.1
  45.0 218.2 %collective-permute-start.1 = (f32[256,512]{1,0:T(8,128)}, f32[256,512]{1,0:T(8,128)}, u32[]{:S(2)}, u32[]{:S(2)}) collective-permute-start(f32[256,512]{1,0:T(8,128)} %get-tuple-element.12), channel_id=1, source_target_pairs={{32,0},{64,32},{96,64},{128,96},{160,128},{192,160},{224,192},{256... | collective-permute-start | bytes 1572872 | tf_op jit(solution)/shard_map/ppermute | solution.py:12
  144.2 585.8 %reduce-scatter.13.cloned.1.call-start = ((), (), s32[]{:S(2)}) async-start(), calls=%async_computation.6 | async-start | bytes 540672
Sparse Core Ops, SparseCore 0:
  33.3 109.2 reduce-scatter.10
  148.1 113.1 reduce-scatter.8
  264.4 230.6 reduce-scatter.14
  497.7 232.1 reduce-scatter.12
where the time goes:
time: 739 us; the launch traced here: 738 us
  waiting for transfers between devices  693 us (94%)
  between operations  14.5 us (2%)
  local copies, waits for them, and re-layouts  13 us (2%)
  matrix products  11.4 us (2%)
    unnamed x6, waiting for transfers between devices  463 us
    reduce_scatter x1, waiting for transfers between devices, body(): lax.psum_scatter(term_conv.astype(jnp.bfloat16), 'tm', scatter_dimension=...  117 us
    reduce_scatter x1, waiting for transfers between devices, body(): lax.psum_scatter(term_res.astype(jnp.bfloat16), 'tm', scatter_dimension=0...  95.7 us
    ppermute x2, waiting for transfers between devices, passed_along(): return lax.ppermute(array, axis, pairs)  16.9 us
  transfers between devices with their start and end apart: 6, of which 5 were waited for; matrix products, arithmetic and copies ran while one was open for 2% of the time, Pallas kernels for 0%

commit v1 on v0

v1 whole, which is shorter than its diff:
```python
import jax
import jax.numpy as jnp
from jax import lax
from jax.sharding import Mesh, PartitionSpec as P

DILATION_STEP = 256
TM = ("x", "zh", "c")
REP = ("y", "zl")


def passed_along(array, axis, by, length):
    pairs = [(i, i + by) for i in range(length) if 0 <= i + by < length]
    return lax.ppermute(array, axis, pairs)


def gate_backward(inputs, cotangent, in_length, w_conv, w_res):
    channel_count = w_res.shape[0]
    pre_act = jnp.dot(inputs, w_conv, preferred_element_type=jnp.float32)
    tanh_f = jnp.tanh(pre_act[:, :channel_count])
    sig_g = jax.nn.sigmoid(pre_act[:, channel_count:])
    gated = (in_length * tanh_f * sig_g).astype(jnp.bfloat16)
    gated_grad = in_length * jnp.dot(cotangent, w_res.T, preferred_element_type=jnp.float32)
    pre_grad = jnp.concatenate(
        [gated_grad * sig_g * (1.0 - tanh_f * tanh_f), gated_grad * tanh_f * sig_g * (1.0 - sig_g)],
        1,
    ).astype(jnp.bfloat16)
    return (gated, pre_grad)


def reduce_over(packed, axis, position, out_type):
    moved = lax.all_to_all(packed, axis, position, position, tiled=True)
    return jnp.sum(moved.astype(jnp.float32), axis=position).astype(out_type)


def make_body(sizes):
    nx, nzh, nc, ny, nzl = sizes
    n_tm = nx * nzh * nc
    n_rep = ny * nzl

    def body(samples, grad_out, w_conv, w_res, lengths):
        sequence_rows = samples[0]
        cotangent = grad_out[0]
        seq_len = lengths[0]
        count_of_rows = sequence_rows.shape[0]
        channel_count = sequence_rows.shape[1]
        start_row = lax.axis_index(TM) * count_of_rows
        trailing_rows = sequence_rows[count_of_rows - DILATION_STEP :]
        arrived = passed_along(trailing_rows, TM, 1, n_tm)
        prior_samples = jnp.concatenate(
            [arrived, sequence_rows[: count_of_rows - DILATION_STEP]], 0
        )
        inputs = jnp.concatenate([prior_samples, sequence_rows], 1)
        in_length = (start_row + jnp.arange(count_of_rows) < seq_len).astype(jnp.float32)[:, None]
        gated, pre_grad = gate_backward(inputs, cotangent, in_length, w_conv, w_res)
        input_gradient = jnp.dot(pre_grad, w_conv.T, preferred_element_type=jnp.float32)
        incoming_gradient = passed_along(input_gradient[:DILATION_STEP, :channel_count], TM, -1, n_tm)
        delayed_gradient = jnp.concatenate(
            [input_gradient[DILATION_STEP:, :channel_count], incoming_gradient], 0
        )
        grad_rows = (
            cotangent.astype(jnp.float32) + input_gradient[:, channel_count:] + delayed_gradient
        ).astype(jnp.bfloat16)
        term_conv = jnp.einsum("tk,tn->kn", inputs, pre_grad, preferred_element_type=jnp.float32)
        term_res = jnp.einsum("tk,tn->kn", gated, cotangent, preferred_element_type=jnp.float32)
        kc, nconv = term_conv.shape
        kr, nres = term_res.shape
        rc, cc = kc // n_tm, nconv // n_rep
        rr, cr = kr // n_tm, nres // n_rep
        conv_blocks = (
            term_conv.astype(jnp.bfloat16)
            .reshape(nx, nzh, nc, rc, ny, nzl, cc)
            .transpose(0, 1, 2, 4, 5, 3, 6)
            .reshape(nx, nzh, nc, ny, nzl, rc * cc)
        )
        res_blocks = (
            term_res.astype(jnp.bfloat16)
            .reshape(nx, nzh, nc, rr, ny, nzl, cr)
            .transpose(0, 1, 2, 4, 5, 3, 6)
            .reshape(nx, nzh, nc, ny, nzl, rr * cr)
        )
        packed = jnp.concatenate([conv_blocks, res_blocks], -1)
        packed = reduce_over(packed, "c", 2, jnp.bfloat16)
        packed = reduce_over(packed, "x", 0, jnp.bfloat16)
        packed = reduce_over(packed, "y", 1, jnp.float32)
        packed = packed.reshape(nzh * nzl, -1)
        total = reduce_over(packed, ("zh", "zl"), 0, jnp.float32)
        all_tokens = count_of_rows * n_tm * n_rep
        grad_scale = float(all_tokens) ** (-0.5)
        sum_conv = total[: rc * cc].reshape(rc, cc) * grad_scale
        sum_res = total[rc * cc :].reshape(rr, cr) * grad_scale
        return (grad_rows[None], sum_conv, sum_res)

    return body


def solution(mesh):
    n_tm, n_rep = mesh.devices.shape
    nc = 2
    nzh = 2
    nx = n_tm // (nc * nzh)
    nzl = 8
    ny = n_rep // nzl
    sizes = (nx, nzh, nc, ny, nzl)
    fine = Mesh(mesh.devices.reshape(sizes), ("x", "zh", "c", "y", "zl"))
    return jax.shard_map(
        make_body(sizes),
        mesh=fine,
        in_specs=(P(REP, TM, None), P(REP, TM, None), P(), P(), P(REP)),
        out_specs=(P(REP, TM, None), P(TM, REP), P(TM, REP)),
        check_vma=False,
    )
```

time: 739 us -> 186 us (0.25)
  the two profiles are of different devices: /device:TPU:2 before, /device:TPU:79 now
where the time goes in v1:
time: 186 us; the launch traced here: 184 us
  local copies, waits for them, and re-layouts  63.6 us (34%)
  starting transfers between devices  45.3 us (24%)
  waiting for transfers between devices  43.5 us (23%)
  matrix products  13.4 us (7%)
  other arithmetic  9.16 us (5%)
  blocking collectives  7.56 us (4%)
    ppermute x2, waiting for transfers between devices, passed_along(): return lax.ppermute(array, axis, pairs)  31.7 us
    all_to_all x3, starting transfers between devices, reduce_over(): moved = lax.all_to_all(packed, axis, position, position, tiled=True)  27.1 us
    reshape x2, local copies, waits for them, and re-layouts, body(): conv_blocks = term_conv.astype(jnp.bfloat16).reshape(nx, nzh, nc, rc, ny,...  20.9 us
    ppermute x2, starting transfers between devices, passed_along(): return lax.ppermute(array, axis, pairs)  18.1 us
    transpose x1, local copies, waits for them, and re-layouts, body(): conv_blocks = term_conv.astype(jnp.bfloat16).reshape(nx, nzh, nc, rc, ny,...  12.4 us
    all_to_all x3, waiting for transfers between devices, reduce_over(): moved = lax.all_to_all(packed, axis, position, position, tiled=True)  11.8 us
    reshape x2, local copies, waits for them, and re-layouts, body(): res_blocks = term_res.astype(jnp.bfloat16).reshape(nx, nzh, nc, rr, ny, n...  9.99 us
    all_to_all x1, blocking collectives, reduce_over(): moved = lax.all_to_all(packed, axis, position, position, tiled=True)  7.56 us
  transfers between devices with their start and end apart: 5, of which 3 were waited for; matrix products, arithmetic and copies ran while one was open for 5% of the time, Pallas kernels for 0%

profile of v1, /device:TPU:79, one launch (start us, length us, event | category | flops | bytes accessed | tf_op | source)
XLA Modules:
  0.0 184.0 jit_solution(4644706212794731085)
XLA Ops:
  0.6 1.2 slice_bitcast_fusion.1
  1.9 14.2 %collective-permute-start = (bf16[256,512]{1,0:T(8,128)(2,1)S(1)}, bf16[256,512]{1,0:T(8,128)(2,1)S(1)}, u32[]{:S(2)}, u32[]{:S(2)}) collective-permute-start(bf16[256,512]{1,0:T(8,128)(2,1)S(1)} %get-tuple-element.16), channel_id=1, source_target_pairs={{0,32},{32,64},{64,96},{96,128},{128,160},{160,192},{192,224},{224... | collective-permute-start | bytes 786440 | tf_op jit(solution)/shard_map/ppermute | solution.py:13
  16.7 5.4 %collective-permute-done = bf16[256,512]{1,0:T(8,128)(2,1)S(1)} collective-permute-done((bf16[256,512]{1,0:T(8,128)(2,1)S(1)}, bf16[256,512]{1,0:T(8,128)(2,1)S(1)}, u32[]{:S(2)}, u32[]{:S(2)}) %collective-permute-start) | collective-permute-done | bytes 262176 | tf_op jit(solution)/shard_map/ppermute | solution.py:13
  22.2 0.7 copy-done.4
  22.9 2.4 %fusion.10 = f32[512,1024]{0,1:T(8,128)S(1)} fusion(bf16[1024,1024]{1,0:T(8,128)(2,1)S(1)} %copy-done, bf16[512,512]{1,0:T(8,128)(2,1)} %bitcast.32, bf16[256,512]{1,0:T(8,128)(2,1)S(1)} %get-tuple-element.17, bf16[256,512]{1,0:T(8,128)(2,1)S(1)} %collective-permute-done), kind=kOutput, calls=%fused_computation.23 | convolution fusion | flops 1076887552 | bytes 5242880 | tf_op jit(solution)/shard_map/dot_general | solution.py:18
  25.3 1.5 convolution_convert_fusion.1
  26.8 1.8 %multiply_convert_fusion.2 = (bf16[512,512]{0,1:T(8,128)(2,1)}, bf16[512,512]{0,1:T(8,128)(2,1)}) fusion(f32[512,1024]{0,1:T(8,128)S(1)} %fusion.10, bf16[512,512]{1,0:T(8,128)(2,1)S(1)} %copy-done.3, bf16[1,512,512]{2,1,0:T(8,128)(2,1)S(1)} %copy-done.2, f32[512]{0:T(512)S(1)} %fusion.11), kind=kOutput, calls=%fused_computation.16 | convolution fusion | flops 272105472 | bytes 4196352 | tf_op jit(solution)/shard_map/dot_general | solution.py:22
  28.6 1.3 copy.31
  29.9 2.2 %reshape.54 = bf16[4,2,2,32,4,8,16]{3,2,1,0,6,5,4:T(2,128)(2,1)} reshape(bf16[512,512]{0,1:T(8,128)(2,1)S(1)} %copy.31) | data formatting | bytes 1048576 | tf_op jit(solution)/shard_map/reshape | solution.py:77
  32.2 3.9 %convolution_convert_fusion = bf16[1024,1024]{1,0:T(8,128)(2,1)} fusion(bf16[512,512]{0,1:T(8,128)(2,1)} %get-tuple-element.13, bf16[512,512]{0,1:T(8,128)(2,1)} %get-tuple-element.12, bf16[512,512]{1,0:T(8,128)(2,1)S(1)} %bitcast.33, bf16[256,512]{1,0:T(8,128)(2,1)S(1)} %get-tuple-element.17, bf16[256,512]{1,0:T(8,128)(2,1)} %copy-done.4), kind=kOutput, calls=%fused_computation.1 | convolution fusion | flops 1080033280 | bytes 4194304 | tf_op jit(solution)/shard_map/tk,tn->kn/dot_general | solution.py:63
  36.1 3.9 %copy.29 = bf16[1024,1024]{0,1:T(8,128)(2,1)} copy(bf16[1024,1024]{1,0:T(8,128)(2,1)} %convolution_convert_fusion) | data formatting | bytes 4194304 | tf_op jit(solution)/shard_map/convert_element_type | solution.py:70
  40.0 8.8 %reshape.52 = bf16[4,2,2,64,4,8,32]{3,2,1,0,6,5,4:T(2,128)(2,1)} reshape(bf16[1024,1024]{0,1:T(8,128)(2,1)} %copy.29) | data formatting | bytes 4194304 | tf_op jit(solution)/shard_map/reshape | solution.py:71
  48.8 6.8 %copy.32 = bf16[4,2,2,4,8,32,16]{6,5,4,3,2,1,0:T(8,128)(2,1)} copy(bf16[4,2,2,4,8,32,16]{5,2,1,0,6,4,3:T(2,128)(2,1)} %bitcast.31) | data formatting | bytes 1048576 | tf_op jit(solution)/shard_map/transpose | solution.py:78
  55.6 7.8 %reshape.55 = bf16[4,2,2,4,8,512]{5,4,3,2,1,0:T(8,128)(2,1)S(1)} reshape(bf16[4,2,2,4,8,32,16]{6,5,4,3,2,1,0:T(8,128)(2,1)} %copy.32) | data formatting | bytes 1048576 | tf_op jit(solution)/shard_map/reshape | solution.py:79
  63.4 12.4 %copy.30 = bf16[4,2,2,4,8,64,32]{6,5,4,3,2,1,0:T(8,128)(2,1)} copy(bf16[4,2,2,4,8,64,32]{5,2,1,0,6,4,3:T(2,128)(2,1)} %bitcast.30) | data formatting | bytes 4194304 | tf_op jit(solution)/shard_map/transpose | solution.py:72
  75.8 12.1 %reshape.53 = bf16[4,2,2,4,8,2048]{5,4,3,2,1,0:T(8,128)(2,1)} reshape(bf16[4,2,2,4,8,64,32]{6,5,4,3,2,1,0:T(8,128)(2,1)} %copy.30) | data formatting | bytes 4194304 | tf_op jit(solution)/shard_map/reshape | solution.py:73
  87.9 1.8 pad_maximum_fusion
  89.9 7.6 %all_to_all.24 = bf16[4,2,2,4,8,2560]{5,4,3,1,0,2:T(8,128)(2,1)} all-to-all(bf16[4,2,2,4,8,2560]{5,4,3,1,0,2:T(8,128)(2,1)S(1)} %copy.33), channel_id=1, replica_groups=mesh['x'=4,'zh'=2,'c'=2,'y'=4,'zl'=8] {'c'}, dimensions={2} | all-to-all | bytes 5242880 | tf_op jit(solution)/shard_map/all_to_all | solution.py:31
  97.5 3.6 %reduce_sum.42 = bf16[4,2,4,8,2560]{4,3,2,1,0:T(8,128)(2,1)} reduce(bf16[4,2,2,4,8,2560]{5,4,3,1,0,2:T(8,128)(2,1)} %all_to_all.24, bf16[]{:T(256)} %constant.29.clone.1), dimensions={2}, to_apply=%region_0.0 | reduce | flops 655360 | bytes 3932162 | tf_op jit(solution)/shard_map/reduce_sum | solution.py:32
  101.1 4.0 %all-to-all-start.1 = ((bf16[4,2,4,8,2560]{4,3,2,1,0:T(8,128)(2,1)}), bf16[4,2,4,8,2560]{4,3,2,1,0:T(8,128)(2,1)S(1)}, u32[]{:S(2)}, u32[]{:S(2)}) async-start(bf16[4,2,4,8,2560]{4,3,2,1,0:T(8,128)(2,1)} %reduce_sum.42), calls=%async_computation.1 | async-start | bytes 2621440 | tf_op jit(solution)/shard_map/all_to_all | solution.py:31
  105.1 3.8 %fusion.5 = f32[512,1024]{1,0:T(8,128)} fusion(bf16[1024,1024]{1,0:T(8,128)(2,1)S(1)} %copy-done, bf16[512,512]{0,1:T(8,128)(2,1)} %get-tuple-element.13, bf16[512,512]{0,1:T(8,128)(2,1)} %get-tuple-element.12), kind=kOutput, calls=%fused_computation.17 | convolution fusion | flops 1075838976 | bytes 5242880 | tf_op jit(solution)/shard_map/dot_general | solution.py:55
  108.9 11.8 %all-to-all-done.1 = bf16[4,2,4,8,2560]{4,3,2,1,0:T(8,128)(2,1)S(1)} async-done(((bf16[4,2,4,8,2560]{4,3,2,1,0:T(8,128)(2,1)}), bf16[4,2,4,8,2560]{4,3,2,1,0:T(8,128)(2,1)S(1)}, u32[]{:S(2)}, u32[]{:S(2)}) %all-to-all-start.1) | async-done | bytes 1310752 | tf_op jit(solution)/shard_map/all_to_all | solution.py:31
  120.7 1.0 reduce_sum.43
  121.7 1.7 copy.34
  123.4 4.3 %all-to-all-start.2 = ((bf16[2,4,8,2560]{3,2,0,1:T(8,128)(2,1)}), bf16[2,4,8,2560]{3,2,0,1:T(8,128)(2,1)S(1)}, u32[]{:S(2)}, u32[]{:S(2)}) async-start(bf16[2,4,8,2560]{3,2,0,1:T(8,128)(2,1)} %copy.34), calls=%async_computation.2 | async-start | bytes 655360 | tf_op jit(solution)/shard_map/all_to_all | solution.py:31
  127.7 2.1 %fusion.16 = (f32[256,512]{1,0:T(8,128)S(1)}, f32[256,512]{1,0:T(8,128)}) fusion(f32[512,1024]{1,0:T(8,128)} %fusion.5), kind=kLoop, calls=%fused_computation.33 | loop fusion | bytes 2097152 | tf_op jit(solution)/shard_map/slice | solution.py:58
  129.8 3.9 %collective-permute-start.1 = (f32[256,512]{1,0:T(8,128)}, f32[256,512]{1,0:T(8,128)}, u32[]{:S(2)}, u32[]{:S(2)}) collective-permute-start(f32[256,512]{1,0:T(8,128)} %get-tuple-element.15), channel_id=1, source_target_pairs={{32,0},{64,32},{96,64},{128,96},{160,128},{192,160},{224,192},{256... | collective-permute-start | bytes 1572872 | tf_op jit(solution)/shard_map/ppermute | solution.py:13
  133.8 0.9 all_to_all.18
  134.6 18.8 %all-to-all-start.3 = ((f32[16,1,2560]{2,1,0:T(1,128)}), f32[16,1,2560]{2,1,0:T(1,128)S(1)}, u32[]{:S(2)}, u32[]{:S(2)}) async-start(f32[16,1,2560]{2,1,0:T(1,128)} %all_to_all.18), calls=%async_computation.3 | async-start | bytes 327680 | tf_op jit(solution)/shard_map/all_to_all | solution.py:31
  153.5 26.3 %collective-permute-done.1 = f32[256,512]{1,0:T(8,128)} collective-permute-done((f32[256,512]{1,0:T(8,128)}, f32[256,512]{1,0:T(8,128)}, u32[]{:S(2)}, u32[]{:S(2)}) %collective-permute-start.1) | collective-permute-done | bytes 524320 | tf_op jit(solution)/shard_map/ppermute | solution.py:13
  179.8 2.6 %fusion.6 = bf16[1,512,512]{2,1,0:T(8,128)(2,1)} fusion(f32[256,512]{1,0:T(8,128)} %collective-permute-done.1, f32[256,512]{1,0:T(8,128)S(1)} %get-tuple-element.14, f32[512,1024]{1,0:T(8,128)} %fusion.5, bf16[1,512,512]{2,1,0:T(8,128)(2,1)} %param.6), kind=kLoop, calls=%fused_computation.19 | loop fusion | flops 1310720 | bytes 3145728 | tf_op jit(solution)/shard_map/broadcast_in_dim | solution.py:91
  183.3 0.7 copy.35
  (20 shorter events, 1.2 us)
Async XLA Ops:
  0.6 22.3 %copy-start = (bf16[1024,1024]{1,0:T(8,128)(2,1)S(1)}, bf16[1024,1024]{1,0:T(8,128)(2,1)}, u32[]{:S(2)}) copy-start(bf16[1024,1024]{1,0:T(8,128)(2,1)} %param.7) | copy-start | bytes 6291460
  1.9 20.3 %collective-permute-start = (bf16[256,512]{1,0:T(8,128)(2,1)S(1)}, bf16[256,512]{1,0:T(8,128)(2,1)S(1)}, u32[]{:S(2)}, u32[]{:S(2)}) collective-permute-start(bf16[256,512]{1,0:T(8,128)(2,1)S(1)} %get-tuple-element.16), channel_id=1, source_target_pairs={{0,32},{32,64},{64,96},{96,128},{128,160},{160,192},{192,224},{224... | collective-permute-start | bytes 786440 | tf_op jit(solution)/shard_map/ppermute | solution.py:13
  22.2 0.7 copy-start.4
  22.9 2.4 %copy-start.2 = (bf16[1,512,512]{2,1,0:T(8,128)(2,1)S(1)}, bf16[1,512,512]{2,1,0:T(8,128)(2,1)}, u32[]{:S(2)}) copy-start(bf16[1,512,512]{2,1,0:T(8,128)(2,1)} %param.6) | copy-start | bytes 1572868
  25.3 1.5 copy-start.3
  28.6 3.5 %copy-start.1 = (bf16[1,512,512]{2,1,0:T(8,128)(2,1)S(1)}, bf16[1,512,512]{2,1,0:T(8,128)(2,1)}, u32[]{:S(2)}) copy-start(bf16[1,512,512]{2,1,0:T(8,128)(2,1)} %param.5) | copy-start | bytes 1572868
  101.1 19.6 %all-to-all-start.1 = ((bf16[4,2,4,8,2560]{4,3,2,1,0:T(8,128)(2,1)}), bf16[4,2,4,8,2560]{4,3,2,1,0:T(8,128)(2,1)S(1)}, u32[]{:S(2)}, u32[]{:S(2)}) async-start(bf16[4,2,4,8,2560]{4,3,2,1,0:T(8,128)(2,1)} %reduce_sum.42), calls=%async_computation.1 | async-start | bytes 2621440 | tf_op jit(solution)/shard_map/all_to_all | solution.py:31
  123.4 10.3 %all-to-all-start.2 = ((bf16[2,4,8,2560]{3,2,0,1:T(8,128)(2,1)}), bf16[2,4,8,2560]{3,2,0,1:T(8,128)(2,1)S(1)}, u32[]{:S(2)}, u32[]{:S(2)}) async-start(bf16[2,4,8,2560]{3,2,0,1:T(8,128)(2,1)} %copy.34), calls=%async_computation.2 | async-start | bytes 655360 | tf_op jit(solution)/shard_map/all_to_all | solution.py:31
  129.8 50.0 %collective-permute-start.1 = (f32[256,512]{1,0:T(8,128)}, f32[256,512]{1,0:T(8,128)}, u32[]{:S(2)}, u32[]{:S(2)}) collective-permute-start(f32[256,512]{1,0:T(8,128)} %get-tuple-element.15), channel_id=1, source_target_pairs={{32,0},{64,32},{96,64},{128,96},{160,128},{192,160},{224,192},{256... | collective-permute-start | bytes 1572872 | tf_op jit(solution)/shard_map/ppermute | solution.py:13
  134.6 47.7 %all-to-all-start.3 = ((f32[16,1,2560]{2,1,0:T(1,128)}), f32[16,1,2560]{2,1,0:T(1,128)S(1)}, u32[]{:S(2)}, u32[]{:S(2)}) async-start(f32[16,1,2560]{2,1,0:T(1,128)} %all_to_all.18), calls=%async_computation.3 | async-start | bytes 327680 | tf_op jit(solution)/shard_map/all_to_all | solution.py:31

commit v2 on v1

--- a/solution.py
+++ b/solution.py
@@ -1,6 +1,8 @@
 import jax
 import jax.numpy as jnp
 from jax import lax
+from jax.experimental import pallas as pl
+from jax.experimental.pallas import tpu as pltpu
 from jax.sharding import Mesh, PartitionSpec as P
 
 DILATION_STEP = 256
@@ -27,9 +29,155 @@
     return (gated, pre_grad)
 
 
-def reduce_over(packed, axis, position, out_type):
-    moved = lax.all_to_all(packed, axis, position, position, tiled=True)
-    return jnp.sum(moved.astype(jnp.float32), axis=position).astype(out_type)
+def make_reducer(sizes, rc, n_conv, rr, n_res, scale):
+    nx, nzh, nc, ny, nzl = sizes
+    nz = nzh * nzl
+    cyc, cyr = n_conv // ny, n_res // ny
+    cc, cr = cyc // nzl, cyr // nzl
+    base_x, base_y, base_z = 1, 1 + nx, 1 + nx + ny
+    n_slots = base_z + nz
+    n_peers = (nc - 1) + (nx - 1) + (ny - 1) + (nz - 1)
+    mesh_id = pl.DeviceIdType.MESH
+
+    def kernel(conv_ref, res_ref, conv_out, res_out,
+               rc_conv, rc_res, sx_conv, sx_res, rx_conv, rx_res,
+               sy_conv, sy_res, ry_conv, ry_res, sz_conv, sz_res, rz_conv, rz_res,
+               send_sems, recv_sems):
+        me_x = lax.axis_index("x")
+        me_zh = lax.axis_index("zh")
+        me_c = lax.axis_index("c")
+        me_y = lax.axis_index("y")
+        me_zl = lax.axis_index("zl")
+        me_z = me_zh * nzl + me_zl
+        other_c = 1 - me_c
+
+        def dev(x=None, zh=None, c=None, y=None, zl=None):
+            return (me_x if x is None else x, me_zh if zh is None else zh,
+                    me_c if c is None else c, me_y if y is None else y,
+                    me_zl if zl is None else zl)
+
+        peers = [dev(c=other_c)]
+        peers += [dev(x=lax.rem(me_x + d, nx)) for d in range(1, nx)]
+        peers += [dev(y=lax.rem(me_y + d, ny)) for d in range(1, ny)]
+        for d in range(1, nz):
+            q = lax.rem(me_z + d, nz)
+            peers.append(dev(zh=q // nzl, zl=lax.rem(q, nzl)))
+        barrier = pltpu.get_barrier_semaphore()
+        for peer in peers:
+            pl.semaphore_signal(barrier, inc=1, device_id=peer, device_id_type=mesh_id)
+        pl.semaphore_wait(barrier, n_peers)
+
+        sends = []
+
+        def send(kind, src, dst, slot, peer):
+            copy = pltpu.make_async_remote_copy(
+                src_ref=src, dst_ref=dst, send_sem=send_sems.at[kind, slot],
+                recv_sem=recv_sems.at[kind, slot], device_id=peer, device_id_type=mesh_id)
+            copy.start()
+            sends.append(copy)
+
+        def arrive(kind, src, dst, slot):
+            pltpu.make_async_remote_copy(
+                src_ref=src, dst_ref=dst, send_sem=send_sems.at[kind, slot],
+                recv_sem=recv_sems.at[kind, slot], device_id=dev(),
+                device_id_type=mesh_id).wait_recv()
+
+        send(0, conv_ref.at[:, :, pl.ds(other_c, 1)], rc_conv, 0, peers[0])
+        send(1, res_ref.at[:, :, pl.ds(other_c, 1)], rc_res, 0, peers[0])
+        arrive(0, conv_ref.at[:, :, pl.ds(other_c, 1)], rc_conv, 0)
+        arrive(1, res_ref.at[:, :, pl.ds(other_c, 1)], rc_res, 0)
+        for x in range(nx):
+            for zh in range(nzh):
+                own_c = conv_ref[x, zh, pl.ds(me_c, 1)][0].astype(jnp.float32)
+                sx_conv[x, zh] = (own_c + rc_conv[x, zh, 0].astype(jnp.float32)).astype(jnp.bfloat16)
+                own_r = res_ref[x, zh, pl.ds(me_c, 1)][0].astype(jnp.float32)
+                sx_res[x, zh] = (own_r + rc_res[x, zh, 0].astype(jnp.float32)).astype(jnp.bfloat16)
+
+        for d in range(1, nx):
+            tx = lax.rem(me_x + d, nx)
+            send(0, sx_conv.at[tx], rx_conv.at[me_x], base_x + me_x, peers[d])
+            send(1, sx_res.at[tx], rx_res.at[me_x], base_x + me_x, peers[d])
+        for d in range(1, nx):
+            sx = lax.rem(me_x + nx - d, nx)
+            arrive(0, sx_conv.at[sx], rx_conv.at[sx], base_x + sx)
+            arrive(1, sx_res.at[sx], rx_res.at[sx], base_x + sx)
+        acc_c = sx_conv[me_x].astype(jnp.float32)
+        acc_r = sx_res[me_x].astype(jnp.float32)
+        for d in range(1, nx):
+            sx = lax.rem(me_x + nx - d, nx)
+            acc_c = acc_c + rx_conv[sx].astype(jnp.float32)
+            acc_r = acc_r + rx_res[sx].astype(jnp.float32)
+        for y in range(ny):
+            sy_conv[y] = acc_c[:, :, y * cyc:(y + 1) * cyc].astype(jnp.bfloat16)
+            sy_res[y] = acc_r[:, :, y * cyr:(y + 1) * cyr].astype(jnp.bfloat16)
+
+        for d in range(1, ny):
+            ty = lax.rem(me_y + d, ny)
+            peer = peers[nx - 1 + d]
+            send(0, sy_conv.at[ty], ry_conv.at[me_y], base_y + me_y, peer)
+            send(1, sy_res.at[ty], ry_res.at[me_y], base_y + me_y, peer)
+        for d in range(1, ny):
+            sy = lax.rem(me_y + ny - d, ny)
+            arrive(0, sy_conv.at[sy], ry_conv.at[sy], base_y + sy)
+            arrive(1, sy_res.at[sy], ry_res.at[sy], base_y + sy)
+        acc_c = sy_conv[me_y].astype(jnp.float32)
+        acc_r = sy_res[me_y].astype(jnp.float32)
+        for d in range(1, ny):
+            sy = lax.rem(me_y + ny - d, ny)
+            acc_c = acc_c + ry_conv[sy].astype(jnp.float32)
+            acc_r = acc_r + ry_res[sy].astype(jnp.float32)
+        for zh in range(nzh):
+            for zl in range(nzl):
+                sz_conv[zh * nzl + zl] = acc_c[zh, :, zl * cc:(zl + 1) * cc]
+                sz_res[zh * nzl + zl] = acc_r[zh, :, zl * cr:(zl + 1) * cr]
+
+        for d in range(1, nz):
+            tz = lax.rem(me_z + d, nz)
+            peer = peers[nx + ny - 2 + d]
+            send(0, sz_conv.at[tz], rz_conv.at[me_z], base_z + me_z, peer)
+            send(1, sz_res.at[tz], rz_res.at[me_z], base_z + me_z, peer)
+        for d in range(1, nz):
+            sz = lax.rem(me_z + nz - d, nz)
+            arrive(0, sz_conv.at[sz], rz_conv.at[sz], base_z + sz)
+            arrive(1, sz_res.at[sz], rz_res.at[sz], base_z + sz)
+        acc_c = sz_conv[me_z]
+        acc_r = sz_res[me_z]
+        for d in range(1, nz):
+            sz = lax.rem(me_z + nz - d, nz)
+            acc_c = acc_c + rz_conv[sz]
+            acc_r = acc_r + rz_res[sz]
+        conv_out[...] = acc_c * scale
+        res_out[...] = acc_r * scale
+        for copy in sends:
+            copy.wait_send()
+
+    vmem = pl.BlockSpec(memory_space=pltpu.VMEM)
+    bf16, f32 = jnp.bfloat16, jnp.float32
+    return pl.pallas_call(
+        kernel,
+        out_shape=(jax.ShapeDtypeStruct((rc, cc), f32), jax.ShapeDtypeStruct((rr, cr), f32)),
+        in_specs=[vmem, vmem],
+        out_specs=(vmem, vmem),
+        scratch_shapes=[
+            pltpu.VMEM((nx, nzh, 1, rc, n_conv), bf16),
+            pltpu.VMEM((nx, nzh, 1, rr, n_res), bf16),
+            pltpu.VMEM((nx, nzh, rc, n_conv), bf16),
+            pltpu.VMEM((nx, nzh, rr, n_res), bf16),
+            pltpu.VMEM((nx, nzh, rc, n_conv), bf16),
+            pltpu.VMEM((nx, nzh, rr, n_res), bf16),
+            pltpu.VMEM((ny, nzh, rc, cyc), bf16),
+            pltpu.VMEM((ny, nzh, rr, cyr), bf16),
+            pltpu.VMEM((ny, nzh, rc, cyc), bf16),
+            pltpu.VMEM((ny, nzh, rr, cyr), bf16),
+            pltpu.VMEM((nz, rc, cc), f32),
+            pltpu.VMEM((nz, rr, cr), f32),
+            pltpu.VMEM((nz, rc, cc), f32),
+            pltpu.VMEM((nz, rr, cr), f32),
+            pltpu.SemaphoreType.DMA((2, n_slots)),
+            pltpu.SemaphoreType.DMA((2, n_slots)),
+        ],
+        compiler_params=pltpu.CompilerParams(collective_id=0, has_side_effects=True),
+    )
 
 
 def make_body(sizes):
@@ -62,32 +210,15 @@
         ).astype(jnp.bfloat16)
         term_conv = jnp.einsum("tk,tn->kn", inputs, pre_grad, preferred_element_type=jnp.float32)
         term_res = jnp.einsum("tk,tn->kn", gated, cotangent, preferred_element_type=jnp.float32)
-        kc, nconv = term_conv.shape
-        kr, nres = term_res.shape
-        rc, cc = kc // n_tm, nconv // n_rep
-        rr, cr = kr // n_tm, nres // n_rep
-        conv_blocks = (
-            term_conv.astype(jnp.bfloat16)
-            .reshape(nx, nzh, nc, rc, ny, nzl, cc)
-            .transpose(0, 1, 2, 4, 5, 3, 6)
-            .reshape(nx, nzh, nc, ny, nzl, rc * cc)
+        kc, n_conv = term_conv.shape
+        kr, n_res = term_res.shape
+        rc, rr = kc // n_tm, kr // n_tm
+        all_tokens = count_of_rows * n_tm * n_rep
+        reducer = make_reducer(sizes, rc, n_conv, rr, n_res, float(all_tokens) ** (-0.5))
+        sum_conv, sum_res = reducer(
+            term_conv.astype(jnp.bfloat16).reshape(nx, nzh, nc, rc, n_conv),
+            term_res.astype(jnp.bfloat16).reshape(nx, nzh, nc, rr, n_res),
         )
-        res_blocks = (
-            term_res.astype(jnp.bfloat16)
-            .reshape(nx, nzh, nc, rr, ny, nzl, cr)
-            .transpose(0, 1, 2, 4, 5, 3, 6)
-            .reshape(nx, nzh, nc, ny, nzl, rr * cr)
-        )
-        packed = jnp.concatenate([conv_blocks, res_blocks], -1)
-        packed = reduce_over(packed, "c", 2, jnp.bfloat16)
-        packed = reduce_over(packed, "x", 0, jnp.bfloat16)
-        packed = reduce_over(packed, "y", 1, jnp.float32)
-        packed = packed.reshape(nzh * nzl, -1)
-        total = reduce_over(packed, ("zh", "zl"), 0, jnp.float32)
-        all_tokens = count_of_rows * n_tm * n_rep
-        grad_scale = float(all_tokens) ** (-0.5)
-        sum_conv = total[: rc * cc].reshape(rc, cc) * grad_scale
-        sum_res = total[rc * cc :].reshape(rr, cr) * grad_scale
         return (grad_rows[None], sum_conv, sum_res)
 
     return body

time: 186 us -> 127 us (0.68)
  the two profiles are of different devices: /device:TPU:79 before, /device:TPU:1 now
where the time goes in v2:
time: 127 us; the launch traced here: 126 us
  Pallas kernels  78.9 us (62%)
  starting transfers between devices  18.7 us (15%)
  waiting for transfers between devices  10 us (8%)
  matrix products  8.61 us (7%)
  local copies, waits for them, and re-layouts  6.25 us (5%)
  other arithmetic  2.48 us (2%)
  between operations  1.4 us (1%)
    pallas_call x1, Pallas kernels, body(): reducer(term_conv.astype(jnp.bfloat16).reshape(nx, nzh, nc, rc, n_conv),...  78.9 us
    ppermute x2, starting transfers between devices, passed_along(): return lax.ppermute(array, axis, pairs)  18.7 us
    ppermute x2, waiting for transfers between devices, passed_along(): return lax.ppermute(array, axis, pairs)  10 us
    unnamed x16, local copies, waits for them, and re-layouts  4.17 us
    dot_general x1, matrix products, body(): jnp.einsum('tk,tn->kn', inputs, pre_grad, preferred_element_type=jnp.floa...  2.62 us
  transfers between devices with their start and end apart: 2, of which 1 were waited for; matrix products, arithmetic and copies ran while one was open for 5% of the time, Pallas kernels for 62%

profile of v2, /device:TPU:1, one launch (start us, length us, event | category | flops | bytes accessed | tf_op | source)
XLA Modules:
  0.0 126.4 jit_solution(10854272619374408746)
XLA Ops:
  0.6 0.0 copy-start
  0.6 1.2 slice_bitcast_fusion.1
  1.9 16.8 %collective-permute-start = (bf16[256,512]{1,0:T(8,128)(2,1)S(1)}, bf16[256,512]{1,0:T(8,128)(2,1)S(1)}, u32[]{:S(2)}, u32[]{:S(2)}) collective-permute-start(bf16[256,512]{1,0:T(8,128)(2,1)S(1)} %get-tuple-element.14), channel_id=1, source_target_pairs={{0,32},{32,64},{64,96},{96,128},{128,160},{160,192},{192,224},{224... | collective-permute-start | bytes 786440 | tf_op jit(solution)/shard_map/ppermute | solution.py:15
  19.4 10.0 %collective-permute-done = bf16[256,512]{1,0:T(8,128)(2,1)S(1)} collective-permute-done((bf16[256,512]{1,0:T(8,128)(2,1)S(1)}, bf16[256,512]{1,0:T(8,128)(2,1)S(1)}, u32[]{:S(2)}, u32[]{:S(2)}) %collective-permute-start) | collective-permute-done | bytes 262176 | tf_op jit(solution)/shard_map/ppermute | solution.py:15
  29.4 0.0 copy-start.5
  29.4 0.0 copy-done
  29.4 0.0 copy-start.3
  29.4 0.0 copy-start.4
  29.4 2.5 %fusion.10 = f32[512,1024]{0,1:T(8,128)S(1)} fusion(bf16[1024,1024]{1,0:T(8,128)(2,1)S(1)} %copy-done, bf16[512,512]{1,0:T(8,128)(2,1)} %bitcast.24, bf16[256,512]{1,0:T(8,128)(2,1)S(1)} %get-tuple-element.15, bf16[256,512]{1,0:T(8,128)(2,1)S(1)} %collective-permute-done), kind=kOutput, calls=%fused_computation.21 | convolution fusion | flops 1076887552 | bytes 5242880 | tf_op jit(solution)/shard_map/dot_general | solution.py:20
  31.9 0.0 copy-done.5
  31.9 0.0 copy-done.3
  31.9 0.0 copy-done.4
  31.9 0.9 multiply_convert_fusion.2
  32.7 1.3 %fusion.5 = f32[512,1024]{1,0:T(8,128)S(1)} fusion(bf16[1024,1024]{1,0:T(8,128)(2,1)S(1)} %copy-done, bf16[512,512]{0,1:T(8,128)(2,1)S(1)} %get-tuple-element.11, bf16[512,512]{0,1:T(8,128)(2,1)S(1)} %get-tuple-element.10), kind=kOutput, calls=%fused_computation.16 | convolution fusion | flops 1075838976 | bytes 5242880 | tf_op jit(solution)/shard_map/dot_general | solution.py:203
  34.0 0.0 copy-start.1
  34.1 1.3 %copy-done.1 = f32[512,1024]{1,0:T(8,128)} copy-done((f32[512,1024]{1,0:T(8,128)}, f32[512,1024]{1,0:T(8,128)S(1)}, u32[]{:S(2)}) %copy-start.1) | copy-done | bytes 2097176
  35.4 0.0 copy-start.2
  35.4 0.0 copy-start.6
  35.4 0.9 fusion.16
  36.2 1.9 %collective-permute-start.1 = (f32[256,512]{1,0:T(8,128)}, f32[256,512]{1,0:T(8,128)}, u32[]{:S(2)}, u32[]{:S(2)}) collective-permute-start(f32[256,512]{1,0:T(8,128)} %get-tuple-element.13), channel_id=1, source_target_pairs={{32,0},{64,32},{96,64},{128,96},{160,128},{192,160},{224,192},{256... | collective-permute-start | bytes 1572872 | tf_op jit(solution)/shard_map/ppermute | solution.py:15
  38.2 0.0 copy-done.2
  38.2 0.0 copy-done.6
  38.2 2.6 %convolution_convert_fusion = bf16[1024,1024]{1,0:T(8,128)(2,1)} fusion(bf16[512,512]{0,1:T(8,128)(2,1)S(1)} %get-tuple-element.11, bf16[512,512]{0,1:T(8,128)(2,1)S(1)} %get-tuple-element.10, bf16[512,512]{1,0:T(8,128)(2,1)S(1)} %bitcast.25, bf16[256,512]{1,0:T(8,128)(2,1)S(1)} %get-tuple-element.15, bf16[256,512]{1,0:T(8,128)(2,1)S(1)} %copy-done.6), kind=kOutput, calls=%fused_computation | convolution fusion | flops 1080033280 | bytes 4194304 | tf_op jit(solution)/shard_map/tk,tn->kn/dot_general | solution.py:211
  40.8 1.4 %convolution_convert_fusion.1 = bf16[512,512]{1,0:T(8,128)(2,1)} fusion(f32[512,1024]{0,1:T(8,128)S(1)} %fusion.10, bf16[1,512,512]{2,1,0:T(8,128)(2,1)S(1)} %copy-done.3, f32[512]{0:T(512)S(1)} %fusion.11), kind=kOutput, calls=%fused_computation.2 | convolution fusion | flops 270270464 | bytes 3147776 | tf_op jit(solution)/shard_map/tk,tn->kn/dot_general | solution.py:212
  42.2 78.9 %shard_map.76 = (f32[64,32]{1,0:T(8,128)}, f32[32,16]{1,0:T(8,128)}) custom-call(bf16[4,2,2,64,1024]{4,3,2,1,0:T(8,128)(2,1)} %bitcast.22, bf16[4,2,2,32,512]{4,3,2,1,0:T(8,128)(2,1)} %bitcast.23), custom_call_target="tpu_custom_call" | custom-call | tf_op jit(solution)/shard_map/pallas_call | solution.py:218
  121.1 1.4 %copy.10 = f32[64,32]{0,1:T(8,128)} copy(f32[64,32]{1,0:T(8,128)} %get-tuple-element.8) | data formatting | bytes 16384
  122.6 1.4 %copy.11 = f32[32,16]{0,1:T(8,128)} copy(f32[32,16]{1,0:T(8,128)} %get-tuple-element.9) | data formatting | bytes 4096
  123.9 0.0 collective-permute-done.1
  123.9 2.5 %fusion.6 = bf16[1,512,512]{2,1,0:T(8,128)(2,1)} fusion(f32[256,512]{1,0:T(8,128)} %collective-permute-done.1, f32[256,512]{1,0:T(8,128)S(1)} %get-tuple-element.12, f32[512,1024]{1,0:T(8,128)} %copy-done.1, bf16[1,512,512]{2,1,0:T(8,128)(2,1)S(1)} %copy-done.3), kind=kLoop, calls=%fused_computation.17 | loop fusion | flops 1310720 | bytes 3145728 | tf_op jit(solution)/shard_map/broadcast_in_dim | solution.py:222
  (1 shorter events, 0.0 us)
Async XLA Ops:
  0.6 28.8 %copy-start = (bf16[1024,1024]{1,0:T(8,128)(2,1)S(1)}, bf16[1024,1024]{1,0:T(8,128)(2,1)}, u32[]{:S(2)}) copy-start(bf16[1024,1024]{1,0:T(8,128)(2,1)} %param.7) | copy-start | bytes 6291460
  1.9 27.5 %collective-permute-start = (bf16[256,512]{1,0:T(8,128)(2,1)S(1)}, bf16[256,512]{1,0:T(8,128)(2,1)S(1)}, u32[]{:S(2)}, u32[]{:S(2)}) collective-permute-start(bf16[256,512]{1,0:T(8,128)(2,1)S(1)} %get-tuple-element.14), channel_id=1, source_target_pairs={{0,32},{32,64},{64,96},{96,128},{128,160},{160,192},{192,224},{224... | collective-permute-start | bytes 786440 | tf_op jit(solution)/shard_map/ppermute | solution.py:15
  29.4 2.5 %copy-start.5 = (bf16[256,512]{1,0:T(8,128)(2,1)}, bf16[256,512]{1,0:T(8,128)(2,1)S(1)}, u32[]{:S(2)}) copy-start(bf16[256,512]{1,0:T(8,128)(2,1)S(1)} %collective-permute-done) | copy-start | bytes 786436
  29.4 2.5 %copy-start.3 = (bf16[1,512,512]{2,1,0:T(8,128)(2,1)S(1)}, bf16[1,512,512]{2,1,0:T(8,128)(2,1)}, u32[]{:S(2)}) copy-start(bf16[1,512,512]{2,1,0:T(8,128)(2,1)} %param.6) | copy-start | bytes 1572868
  29.4 2.5 %copy-start.4 = (bf16[512,512]{1,0:T(8,128)(2,1)S(1)}, bf16[512,512]{1,0:T(8,128)(2,1)}, u32[]{:S(2)}) copy-start(bf16[512,512]{1,0:T(8,128)(2,1)} %param.8) | copy-start | bytes 1572868
  34.0 1.3 %copy-start.1 = (f32[512,1024]{1,0:T(8,128)}, f32[512,1024]{1,0:T(8,128)S(1)}, u32[]{:S(2)}) copy-start(f32[512,1024]{1,0:T(8,128)S(1)} %fusion.5) | copy-start | bytes 6291460
  35.4 2.8 %copy-start.2 = (bf16[1,512,512]{2,1,0:T(8,128)(2,1)S(1)}, bf16[1,512,512]{2,1,0:T(8,128)(2,1)}, u32[]{:S(2)}) copy-start(bf16[1,512,512]{2,1,0:T(8,128)(2,1)} %param.5) | copy-start | bytes 1572868
  35.4 2.8 %copy-start.6 = (bf16[256,512]{1,0:T(8,128)(2,1)S(1)}, bf16[256,512]{1,0:T(8,128)(2,1)}, u32[]{:S(2)}) copy-start(bf16[256,512]{1,0:T(8,128)(2,1)} %copy-done.5) | copy-start | bytes 786436
  36.2 87.7 %collective-permute-start.1 = (f32[256,512]{1,0:T(8,128)}, f32[256,512]{1,0:T(8,128)}, u32[]{:S(2)}, u32[]{:S(2)}) collective-permute-start(f32[256,512]{1,0:T(8,128)} %get-tuple-element.13), channel_id=1, source_target_pairs={{32,0},{64,32},{96,64},{128,96},{160,128},{192,160},{224,192},{256... | collective-permute-start | bytes 1572872 | tf_op jit(solution)/shard_map/ppermute | solution.py:15

commit v3 on v2

--- a/solution.py
+++ b/solution.py
@@ -127,9 +127,11 @@
             acc_c = acc_c + ry_conv[sy].astype(jnp.float32)
             acc_r = acc_r + ry_res[sy].astype(jnp.float32)
         for zh in range(nzh):
+            flip_c = acc_c[zh].T
+            flip_r = acc_r[zh].T
             for zl in range(nzl):
-                sz_conv[zh * nzl + zl] = acc_c[zh, :, zl * cc:(zl + 1) * cc]
-                sz_res[zh * nzl + zl] = acc_r[zh, :, zl * cr:(zl + 1) * cr]
+                sz_conv[zh * nzl + zl] = flip_c[zl * cc:(zl + 1) * cc, :].astype(jnp.bfloat16)
+                sz_res[zh * nzl + zl] = flip_r[zl * cr:(zl + 1) * cr, :].astype(jnp.bfloat16)
 
         for d in range(1, nz):
             tz = lax.rem(me_z + d, nz)
@@ -140,14 +142,14 @@
             sz = lax.rem(me_z + nz - d, nz)
             arrive(0, sz_conv.at[sz], rz_conv.at[sz], base_z + sz)
             arrive(1, sz_res.at[sz], rz_res.at[sz], base_z + sz)
-        acc_c = sz_conv[me_z]
-        acc_r = sz_res[me_z]
+        acc_c = sz_conv[me_z].astype(jnp.float32)
+        acc_r = sz_res[me_z].astype(jnp.float32)
         for d in range(1, nz):
             sz = lax.rem(me_z + nz - d, nz)
-            acc_c = acc_c + rz_conv[sz]
-            acc_r = acc_r + rz_res[sz]
-        conv_out[...] = acc_c * scale
-        res_out[...] = acc_r * scale
+            acc_c = acc_c + rz_conv[sz].astype(jnp.float32)
+            acc_r = acc_r + rz_res[sz].astype(jnp.float32)
+        conv_out[...] = acc_c.T * scale
+        res_out[...] = acc_r.T * scale
         for copy in sends:
             copy.wait_send()
 
@@ -169,10 +171,10 @@
             pltpu.VMEM((ny, nzh, rr, cyr), bf16),
             pltpu.VMEM((ny, nzh, rc, cyc), bf16),
             pltpu.VMEM((ny, nzh, rr, cyr), bf16),
-            pltpu.VMEM((nz, rc, cc), f32),
-            pltpu.VMEM((nz, rr, cr), f32),
-            pltpu.VMEM((nz, rc, cc), f32),
-            pltpu.VMEM((nz, rr, cr), f32),
+            pltpu.VMEM((nz, cc, rc), bf16),
+            pltpu.VMEM((nz, cr, rr), bf16),
+            pltpu.VMEM((nz, cc, rc), bf16),
+            pltpu.VMEM((nz, cr, rr), bf16),
             pltpu.SemaphoreType.DMA((2, n_slots)),
             pltpu.SemaphoreType.DMA((2, n_slots)),
         ],

time: 127 us -> 102 us (0.80)
  Pallas kernels: 78.9 us -> 54.3 us
    pallas_call x1, Pallas kernels: 78.9 us -> 54.3 us  [body(): reducer(term_conv.astype(jnp.bfloat16).reshape(nx, nzh, nc, rc, n_conv),...]
  transfers between devices with their start and end apart: 2 -> 2, of which waited for: 1 -> 1; matrix products, arithmetic and copies ran while one was open for 5% -> 7% of each run, Pallas kernels for 62% -> 53%
where the time goes in v3:
time: 102 us
  Pallas kernels  54.3 us (53%)
  starting transfers between devices  18.7 us (18%)
  waiting for transfers between devices  10 us (10%)
  matrix products  8.61 us (8%)
  local copies, waits for them, and re-layouts  6.25 us (6%)
  other arithmetic  2.48 us (2%)
  between operations  1.4 us (1%)
    pallas_call x1, Pallas kernels, body(): reducer(term_conv.astype(jnp.bfloat16).reshape(nx, nzh, nc, rc, n_conv),...  54.3 us
    ppermute x2, starting transfers between devices, passed_along(): return lax.ppermute(array, axis, pairs)  18.7 us
    ppermute x2, waiting for transfers between devices, passed_along(): return lax.ppermute(array, axis, pairs)  10 us
    unnamed x16, local copies, waits for them, and re-layouts  4.17 us
    dot_general x1, matrix products, body(): jnp.einsum('tk,tn->kn', inputs, pre_grad, preferred_element_type=jnp.floa...  2.62 us
    broadcast_in_dim x1, other arithmetic, body(): return (grad_rows[None], sum_conv, sum_res)  2.47 us
    dot_general x1, matrix products, gate_backward(): pre_act = jnp.dot(inputs, w_conv, preferred_element_type=jnp.float32)  2.46 us
  transfers between devices with their start and end apart: 2, of which 1 were waited for; matrix products, arithmetic and copies ran while one was open for 7% of the time, Pallas kernels for 53%

profile of v3, /device:TPU:1, one launch (start us, length us, event | category | flops | bytes accessed | tf_op | source)
XLA Modules:
  0.0 101.8 jit_solution(5259672666088654641)
XLA Ops:
  0.6 0.0 copy-start
  0.6 1.2 %slice_bitcast_fusion.1 = (bf16[256,512]{1,0:T(8,128)(2,1)S(1)}, bf16[256,512]{1,0:T(8,128)(2,1)S(1)}) fusion(bf16[1,512,512]{2,1,0:T(8,128)(2,1)} %param.5), kind=kLoop, calls=%fused_computation.23 | loop fusion | bytes 1048576 | tf_op jit(solution)/shard_map/slice | solution.py:197
  1.9 16.8 %collective-permute-start = (bf16[256,512]{1,0:T(8,128)(2,1)S(1)}, bf16[256,512]{1,0:T(8,128)(2,1)S(1)}, u32[]{:S(2)}, u32[]{:S(2)}) collective-permute-start(bf16[256,512]{1,0:T(8,128)(2,1)S(1)} %get-tuple-element.14), channel_id=1, source_target_pairs={{0,32},{32,64},{64,96},{96,128},{128,160},{160,192},{192,224},{224... | collective-permute-start | bytes 786440 | tf_op jit(solution)/shard_map/ppermute | solution.py:15
  19.4 10.0 %collective-permute-done = bf16[256,512]{1,0:T(8,128)(2,1)S(1)} collective-permute-done((bf16[256,512]{1,0:T(8,128)(2,1)S(1)}, bf16[256,512]{1,0:T(8,128)(2,1)S(1)}, u32[]{:S(2)}, u32[]{:S(2)}) %collective-permute-start) | collective-permute-done | bytes 262176 | tf_op jit(solution)/shard_map/ppermute | solution.py:15
  29.4 0.0 copy-start.5
  29.4 0.0 copy-done
  29.4 0.0 copy-start.3
  29.4 0.0 copy-start.4
  29.4 2.5 %fusion.10 = f32[512,1024]{0,1:T(8,128)S(1)} fusion(bf16[1024,1024]{1,0:T(8,128)(2,1)S(1)} %copy-done, bf16[512,512]{1,0:T(8,128)(2,1)} %bitcast.24, bf16[256,512]{1,0:T(8,128)(2,1)S(1)} %get-tuple-element.15, bf16[256,512]{1,0:T(8,128)(2,1)S(1)} %collective-permute-done), kind=kOutput, calls=%fused_computation.21 | convolution fusion | flops 1076887552 | bytes 5242880 | tf_op jit(solution)/shard_map/dot_general | solution.py:20
  31.9 0.0 copy-done.5
  31.9 0.0 copy-done.3
  31.9 0.0 copy-done.4
  31.9 0.9 multiply_convert_fusion.2
  32.7 1.3 %fusion.5 = f32[512,1024]{1,0:T(8,128)S(1)} fusion(bf16[1024,1024]{1,0:T(8,128)(2,1)S(1)} %copy-done, bf16[512,512]{0,1:T(8,128)(2,1)S(1)} %get-tuple-element.11, bf16[512,512]{0,1:T(8,128)(2,1)S(1)} %get-tuple-element.10), kind=kOutput, calls=%fused_computation.16 | convolution fusion | flops 1075838976 | bytes 5242880 | tf_op jit(solution)/shard_map/dot_general | solution.py:205
  34.0 0.0 copy-start.1
  34.1 1.3 %copy-done.1 = f32[512,1024]{1,0:T(8,128)} copy-done((f32[512,1024]{1,0:T(8,128)}, f32[512,1024]{1,0:T(8,128)S(1)}, u32[]{:S(2)}) %copy-start.1) | copy-done | bytes 2097176
  35.4 0.0 copy-start.2
  35.4 0.0 copy-start.6
  35.4 0.9 fusion.16
  36.2 1.9 %collective-permute-start.1 = (f32[256,512]{1,0:T(8,128)}, f32[256,512]{1,0:T(8,128)}, u32[]{:S(2)}, u32[]{:S(2)}) collective-permute-start(f32[256,512]{1,0:T(8,128)} %get-tuple-element.13), channel_id=1, source_target_pairs={{32,0},{64,32},{96,64},{128,96},{160,128},{192,160},{224,192},{256... | collective-permute-start | bytes 1572872 | tf_op jit(solution)/shard_map/ppermute | solution.py:15
  38.2 0.0 copy-done.2
  38.2 0.0 copy-done.6
  38.2 2.6 %convolution_convert_fusion = bf16[1024,1024]{1,0:T(8,128)(2,1)} fusion(bf16[512,512]{0,1:T(8,128)(2,1)S(1)} %get-tuple-element.11, bf16[512,512]{0,1:T(8,128)(2,1)S(1)} %get-tuple-element.10, bf16[512,512]{1,0:T(8,128)(2,1)S(1)} %bitcast.25, bf16[256,512]{1,0:T(8,128)(2,1)S(1)} %get-tuple-element.15, bf16[256,512]{1,0:T(8,128)(2,1)S(1)} %copy-done.6), kind=kOutput, calls=%fused_computation | convolution fusion | flops 1080033280 | bytes 4194304 | tf_op jit(solution)/shard_map/tk,tn->kn/dot_general | solution.py:213
  40.8 1.4 %convolution_convert_fusion.1 = bf16[512,512]{1,0:T(8,128)(2,1)} fusion(f32[512,1024]{0,1:T(8,128)S(1)} %fusion.10, bf16[1,512,512]{2,1,0:T(8,128)(2,1)S(1)} %copy-done.3, f32[512]{0:T(512)S(1)} %fusion.11), kind=kOutput, calls=%fused_computation.2 | convolution fusion | flops 270270464 | bytes 3147776 | tf_op jit(solution)/shard_map/tk,tn->kn/dot_general | solution.py:214
  42.2 54.3 %shard_map.76 = (f32[64,32]{1,0:T(8,128)}, f32[32,16]{1,0:T(8,128)}) custom-call(bf16[4,2,2,64,1024]{4,3,2,1,0:T(8,128)(2,1)} %bitcast.22, bf16[4,2,2,32,512]{4,3,2,1,0:T(8,128)(2,1)} %bitcast.23), custom_call_target="tpu_custom_call" | custom-call | tf_op jit(solution)/shard_map/pallas_call | solution.py:220
  96.5 1.4 %copy.10 = f32[64,32]{0,1:T(8,128)} copy(f32[64,32]{1,0:T(8,128)} %get-tuple-element.8) | data formatting | bytes 16384
  97.9 1.4 %copy.11 = f32[32,16]{0,1:T(8,128)} copy(f32[32,16]{1,0:T(8,128)} %get-tuple-element.9) | data formatting | bytes 4096
  99.3 0.0 collective-permute-done.1
  99.3 2.5 %fusion.6 = bf16[1,512,512]{2,1,0:T(8,128)(2,1)} fusion(f32[256,512]{1,0:T(8,128)} %collective-permute-done.1, f32[256,512]{1,0:T(8,128)S(1)} %get-tuple-element.12, f32[512,1024]{1,0:T(8,128)} %copy-done.1, bf16[1,512,512]{2,1,0:T(8,128)(2,1)S(1)} %copy-done.3), kind=kLoop, calls=%fused_computation.17 | loop fusion | flops 1310720 | bytes 3145728 | tf_op jit(solution)/shard_map/broadcast_in_dim | solution.py:224
  (1 shorter events, 0.0 us)
Async XLA Ops:
  0.6 28.8 %copy-start = (bf16[1024,1024]{1,0:T(8,128)(2,1)S(1)}, bf16[1024,1024]{1,0:T(8,128)(2,1)}, u32[]{:S(2)}) copy-start(bf16[1024,1024]{1,0:T(8,128)(2,1)} %param.7) | copy-start | bytes 6291460
  1.9 27.5 %collective-permute-start = (bf16[256,512]{1,0:T(8,128)(2,1)S(1)}, bf16[256,512]{1,0:T(8,128)(2,1)S(1)}, u32[]{:S(2)}, u32[]{:S(2)}) collective-permute-start(bf16[256,512]{1,0:T(8,128)(2,1)S(1)} %get-tuple-element.14), channel_id=1, source_target_pairs={{0,32},{32,64},{64,96},{96,128},{128,160},{160,192},{192,224},{224... | collective-permute-start | bytes 786440 | tf_op jit(solution)/shard_map/ppermute | solution.py:15
  29.4 2.5 %copy-start.5 = (bf16[256,512]{1,0:T(8,128)(2,1)}, bf16[256,512]{1,0:T(8,128)(2,1)S(1)}, u32[]{:S(2)}) copy-start(bf16[256,512]{1,0:T(8,128)(2,1)S(1)} %collective-permute-done) | copy-start | bytes 786436
  29.4 2.5 %copy-start.3 = (bf16[1,512,512]{2,1,0:T(8,128)(2,1)S(1)}, bf16[1,512,512]{2,1,0:T(8,128)(2,1)}, u32[]{:S(2)}) copy-start(bf16[1,512,512]{2,1,0:T(8,128)(2,1)} %param.6) | copy-start | bytes 1572868
  29.4 2.5 %copy-start.4 = (bf16[512,512]{1,0:T(8,128)(2,1)S(1)}, bf16[512,512]{1,0:T(8,128)(2,1)}, u32[]{:S(2)}) copy-start(bf16[512,512]{1,0:T(8,128)(2,1)} %param.8) | copy-start | bytes 1572868
  34.0 1.3 %copy-start.1 = (f32[512,1024]{1,0:T(8,128)}, f32[512,1024]{1,0:T(8,128)S(1)}, u32[]{:S(2)}) copy-start(f32[512,1024]{1,0:T(8,128)S(1)} %fusion.5) | copy-start | bytes 6291460
  35.4 2.8 %copy-start.2 = (bf16[1,512,512]{2,1,0:T(8,128)(2,1)S(1)}, bf16[1,512,512]{2,1,0:T(8,128)(2,1)}, u32[]{:S(2)}) copy-start(bf16[1,512,512]{2,1,0:T(8,128)(2,1)} %param.5) | copy-start | bytes 1572868
  35.4 2.8 %copy-start.6 = (bf16[256,512]{1,0:T(8,128)(2,1)S(1)}, bf16[256,512]{1,0:T(8,128)(2,1)}, u32[]{:S(2)}) copy-start(bf16[256,512]{1,0:T(8,128)(2,1)} %copy-done.5) | copy-start | bytes 786436
  36.2 63.0 %collective-permute-start.1 = (f32[256,512]{1,0:T(8,128)}, f32[256,512]{1,0:T(8,128)}, u32[]{:S(2)}, u32[]{:S(2)}) collective-permute-start(f32[256,512]{1,0:T(8,128)} %get-tuple-element.13), channel_id=1, source_target_pairs={{32,0},{64,32},{96,64},{128,96},{160,128},{192,160},{224,192},{256... | collective-permute-start | bytes 1572872 | tf_op jit(solution)/shard_map/ppermute | solution.py:15

commit v4 on v3

--- a/solution.py
+++ b/solution.py
@@ -34,15 +34,21 @@
     nz = nzh * nzl
     cyc, cyr = n_conv // ny, n_res // ny
     cc, cr = cyc // nzl, cyr // nzl
-    base_x, base_y, base_z = 1, 1 + nx, 1 + nx + ny
+    hc, hr = rc // 2, rr // 2
+    base_xa, base_yb = 1, 1 + nx
+    base_ya, base_xb = 1 + nx + ny, 1 + nx + 2 * ny
+    base_z = 1 + 2 * nx + 2 * ny
     n_slots = base_z + nz
     n_peers = (nc - 1) + (nx - 1) + (ny - 1) + (nz - 1)
     mesh_id = pl.DeviceIdType.MESH
 
     def kernel(conv_ref, res_ref, conv_out, res_out,
-               rc_conv, rc_res, sx_conv, sx_res, rx_conv, rx_res,
-               sy_conv, sy_res, ry_conv, ry_res, sz_conv, sz_res, rz_conv, rz_res,
-               send_sems, recv_sems):
+               rc_conv, rc_res, sx_conv, sx_res,
+               rxa_conv, rxa_res, ryb_conv, ryb_res,
+               sa_conv, sa_res, rya_conv, rya_res,
+               sb_conv, sb_res, rxb_conv, rxb_res,
+               sz_conv, sz_res, rz_conv, rz_res,
+               send_sems, recv_sems, local_sems):
         me_x = lax.axis_index("x")
         me_zh = lax.axis_index("zh")
         me_c = lax.axis_index("c")
@@ -57,13 +63,14 @@
                     me_zl if zl is None else zl)
 
         peers = [dev(c=other_c)]
-        peers += [dev(x=lax.rem(me_x + d, nx)) for d in range(1, nx)]
-        peers += [dev(y=lax.rem(me_y + d, ny)) for d in range(1, ny)]
+        x_peers = [dev(x=lax.rem(me_x + d, nx)) for d in range(1, nx)]
+        y_peers = [dev(y=lax.rem(me_y + d, ny)) for d in range(1, ny)]
+        z_peers = []
         for d in range(1, nz):
             q = lax.rem(me_z + d, nz)
-            peers.append(dev(zh=q // nzl, zl=lax.rem(q, nzl)))
+            z_peers.append(dev(zh=q // nzl, zl=lax.rem(q, nzl)))
         barrier = pltpu.get_barrier_semaphore()
-        for peer in peers:
+        for peer in peers + x_peers + y_peers + z_peers:
             pl.semaphore_signal(barrier, inc=1, device_id=peer, device_id_type=mesh_id)
         pl.semaphore_wait(barrier, n_peers)
 
@@ -81,6 +88,11 @@
                 src_ref=src, dst_ref=dst, send_sem=send_sems.at[kind, slot],
                 recv_sem=recv_sems.at[kind, slot], device_id=dev(),
                 device_id_type=mesh_id).wait_recv()
+
+        def keep(kind, which, src, dst):
+            copy = pltpu.make_async_copy(src, dst, local_sems.at[kind, which])
+            copy.start()
+            return copy
 
         send(0, conv_ref.at[:, :, pl.ds(other_c, 1)], rc_conv, 0, peers[0])
         send(1, res_ref.at[:, :, pl.ds(other_c, 1)], rc_res, 0, peers[0])
@@ -95,37 +107,77 @@
 
         for d in range(1, nx):
             tx = lax.rem(me_x + d, nx)
-            send(0, sx_conv.at[tx], rx_conv.at[me_x], base_x + me_x, peers[d])
-            send(1, sx_res.at[tx], rx_res.at[me_x], base_x + me_x, peers[d])
-        for d in range(1, nx):
-            sx = lax.rem(me_x + nx - d, nx)
-            arrive(0, sx_conv.at[sx], rx_conv.at[sx], base_x + sx)
-            arrive(1, sx_res.at[sx], rx_res.at[sx], base_x + sx)
-        acc_c = sx_conv[me_x].astype(jnp.float32)
-        acc_r = sx_res[me_x].astype(jnp.float32)
-        for d in range(1, nx):
-            sx = lax.rem(me_x + nx - d, nx)
-            acc_c = acc_c + rx_conv[sx].astype(jnp.float32)
-            acc_r = acc_r + rx_res[sx].astype(jnp.float32)
-        for y in range(ny):
-            sy_conv[y] = acc_c[:, :, y * cyc:(y + 1) * cyc].astype(jnp.bfloat16)
-            sy_res[y] = acc_r[:, :, y * cyr:(y + 1) * cyr].astype(jnp.bfloat16)
-
+            send(0, sx_conv.at[tx, :, pl.ds(0, hc)], rxa_conv.at[me_x], base_xa + me_x, x_peers[d - 1])
+            send(1, sx_res.at[tx, :, pl.ds(0, hr)], rxa_res.at[me_x], base_xa + me_x, x_peers[d - 1])
         for d in range(1, ny):
             ty = lax.rem(me_y + d, ny)
-            peer = peers[nx - 1 + d]
-            send(0, sy_conv.at[ty], ry_conv.at[me_y], base_y + me_y, peer)
-            send(1, sy_res.at[ty], ry_res.at[me_y], base_y + me_y, peer)
+            send(0, sx_conv.at[:, :, pl.ds(hc, hc), pl.ds(ty * cyc, cyc)], ryb_conv.at[me_y],
+                 base_yb + me_y, y_peers[d - 1])
+            send(1, sx_res.at[:, :, pl.ds(hr, hr), pl.ds(ty * cyr, cyr)], ryb_res.at[me_y],
+                 base_yb + me_y, y_peers[d - 1])
+        own_b = [keep(0, 0, sx_conv.at[:, :, pl.ds(hc, hc), pl.ds(me_y * cyc, cyc)], ryb_conv.at[me_y]),
+                 keep(1, 0, sx_res.at[:, :, pl.ds(hr, hr), pl.ds(me_y * cyr, cyr)], ryb_res.at[me_y])]
+
+        for d in range(1, nx):
+            sx = lax.rem(me_x + nx - d, nx)
+            arrive(0, sx_conv.at[sx, :, pl.ds(0, hc)], rxa_conv.at[sx], base_xa + sx)
+            arrive(1, sx_res.at[sx, :, pl.ds(0, hr)], rxa_res.at[sx], base_xa + sx)
+        acc_c = sx_conv[me_x, :, :hc].astype(jnp.float32)
+        acc_r = sx_res[me_x, :, :hr].astype(jnp.float32)
+        for d in range(1, nx):
+            sx = lax.rem(me_x + nx - d, nx)
+            acc_c = acc_c + rxa_conv[sx].astype(jnp.float32)
+            acc_r = acc_r + rxa_res[sx].astype(jnp.float32)
+        sa_conv[...] = acc_c.astype(jnp.bfloat16)
+        sa_res[...] = acc_r.astype(jnp.bfloat16)
+        for d in range(1, ny):
+            ty = lax.rem(me_y + d, ny)
+            send(0, sa_conv.at[:, :, pl.ds(ty * cyc, cyc)], rya_conv.at[me_y], base_ya + me_y, y_peers[d - 1])
+            send(1, sa_res.at[:, :, pl.ds(ty * cyr, cyr)], rya_res.at[me_y], base_ya + me_y, y_peers[d - 1])
+        own_a = [keep(0, 1, sa_conv.at[:, :, pl.ds(me_y * cyc, cyc)], rya_conv.at[me_y]),
+                 keep(1, 1, sa_res.at[:, :, pl.ds(me_y * cyr, cyr)], rya_res.at[me_y])]
+
         for d in range(1, ny):
             sy = lax.rem(me_y + ny - d, ny)
-            arrive(0, sy_conv.at[sy], ry_conv.at[sy], base_y + sy)
-            arrive(1, sy_res.at[sy], ry_res.at[sy], base_y + sy)
-        acc_c = sy_conv[me_y].astype(jnp.float32)
-        acc_r = sy_res[me_y].astype(jnp.float32)
+            arrive(0, sx_conv.at[:, :, pl.ds(hc, hc), pl.ds(0, cyc)], ryb_conv.at[sy], base_yb + sy)
+            arrive(1, sx_res.at[:, :, pl.ds(hr, hr), pl.ds(0, cyr)], ryb_res.at[sy], base_yb + sy)
+        for copy in own_b:
+            copy.wait()
+        acc_c = ryb_conv[0].astype(jnp.float32)
+        acc_r = ryb_res[0].astype(jnp.float32)
+        for s in range(1, ny):
+            acc_c = acc_c + ryb_conv[s].astype(jnp.float32)
+            acc_r = acc_r + ryb_res[s].astype(jnp.float32)
+        sb_conv[...] = acc_c.astype(jnp.bfloat16)
+        sb_res[...] = acc_r.astype(jnp.bfloat16)
+        for d in range(1, nx):
+            tx = lax.rem(me_x + d, nx)
+            send(0, sb_conv.at[tx], rxb_conv.at[me_x], base_xb + me_x, x_peers[d - 1])
+            send(1, sb_res.at[tx], rxb_res.at[me_x], base_xb + me_x, x_peers[d - 1])
+
         for d in range(1, ny):
             sy = lax.rem(me_y + ny - d, ny)
-            acc_c = acc_c + ry_conv[sy].astype(jnp.float32)
-            acc_r = acc_r + ry_res[sy].astype(jnp.float32)
+            arrive(0, sa_conv.at[:, :, pl.ds(0, cyc)], rya_conv.at[sy], base_ya + sy)
+            arrive(1, sa_res.at[:, :, pl.ds(0, cyr)], rya_res.at[sy], base_ya + sy)
+        for copy in own_a:
+            copy.wait()
+        for d in range(1, nx):
+            sx = lax.rem(me_x + nx - d, nx)
+            arrive(0, sb_conv.at[sx], rxb_conv.at[sx], base_xb + sx)
+            arrive(1, sb_res.at[sx], rxb_res.at[sx], base_xb + sx)
+        top_c = rya_conv[0].astype(jnp.float32)
+        top_r = rya_res[0].astype(jnp.float32)
+        for s in range(1, ny):
+            top_c = top_c + rya_conv[s].astype(jnp.float32)
+            top_r = top_r + rya_res[s].astype(jnp.float32)
+        low_c = sb_conv[me_x].astype(jnp.float32)
+        low_r = sb_res[me_x].astype(jnp.float32)
+        for d in range(1, nx):
+            sx = lax.rem(me_x + nx - d, nx)
+            low_c = low_c + rxb_conv[sx].astype(jnp.float32)
+            low_r = low_r + rxb_res[sx].astype(jnp.float32)
+        acc_c = jnp.concatenate([top_c, low_c], axis=1)
+        acc_r = jnp.concatenate([top_r, low_r], axis=1)
         for zh in range(nzh):
             flip_c = acc_c[zh].T
             flip_r = acc_r[zh].T
@@ -135,9 +187,8 @@
 
         for d in range(1, nz):
             tz = lax.rem(me_z + d, nz)
-            peer = peers[nx + ny - 2 + d]
-            send(0, sz_conv.at[tz], rz_conv.at[me_z], base_z + me_z, peer)
-            send(1, sz_res.at[tz], rz_res.at[me_z], base_z + me_z, peer)
+            send(0, sz_conv.at[tz], rz_conv.at[me_z], base_z + me_z, z_peers[d - 1])
+            send(1, sz_res.at[tz], rz_res.at[me_z], base_z + me_z, z_peers[d - 1])
         for d in range(1, nz):
             sz = lax.rem(me_z + nz - d, nz)
             arrive(0, sz_conv.at[sz], rz_conv.at[sz], base_z + sz)
@@ -165,18 +216,25 @@
             pltpu.VMEM((nx, nzh, 1, rr, n_res), bf16),
             pltpu.VMEM((nx, nzh, rc, n_conv), bf16),
             pltpu.VMEM((nx, nzh, rr, n_res), bf16),
-            pltpu.VMEM((nx, nzh, rc, n_conv), bf16),
-            pltpu.VMEM((nx, nzh, rr, n_res), bf16),
-            pltpu.VMEM((ny, nzh, rc, cyc), bf16),
-            pltpu.VMEM((ny, nzh, rr, cyr), bf16),
-            pltpu.VMEM((ny, nzh, rc, cyc), bf16),
-            pltpu.VMEM((ny, nzh, rr, cyr), bf16),
+            pltpu.VMEM((nx, nzh, hc, n_conv), bf16),
+            pltpu.VMEM((nx, nzh, hr, n_res), bf16),
+            pltpu.VMEM((ny, nx, nzh, hc, cyc), bf16),
+            pltpu.VMEM((ny, nx, nzh, hr, cyr), bf16),
+            pltpu.VMEM((nzh, hc, n_conv), bf16),
+            pltpu.VMEM((nzh, hr, n_res), bf16),
+            pltpu.VMEM((ny, nzh, hc, cyc), bf16),
+            pltpu.VMEM((ny, nzh, hr, cyr), bf16),
+            pltpu.VMEM((nx, nzh, hc, cyc), bf16),
+            pltpu.VMEM((nx, nzh, hr, cyr), bf16),
+            pltpu.VMEM((nx, nzh, hc, cyc), bf16),
+            pltpu.VMEM((nx, nzh, hr, cyr), bf16),
             pltpu.VMEM((nz, cc, rc), bf16),
             pltpu.VMEM((nz, cr, rr), bf16),
             pltpu.VMEM((nz, cc, rc), bf16),
             pltpu.VMEM((nz, cr, rr), bf16),
             pltpu.SemaphoreType.DMA((2, n_slots)),
             pltpu.SemaphoreType.DMA((2, n_slots)),
+            pltpu.SemaphoreType.DMA((2, 2)),
         ],
         compiler_params=pltpu.CompilerParams(collective_id=0, has_side_effects=True),
     )

time: 102 us -> 93.9 us (0.921)
  Pallas kernels: 54.3 us -> 46 us
    pallas_call x1, Pallas kernels: 54.3 us -> 46 us  [body(): reducer(term_conv.astype(jnp.bfloat16).reshape(nx, nzh, nc, rc, n_conv),...]
  transfers between devices with their start and end apart: 2 -> 2, of which waited for: 1 -> 1; matrix products, arithmetic and copies ran while one was open for 7% -> 7% of each run, Pallas kernels for 53% -> 49%
where the time goes in v4:
time: 93.9 us; the launch traced here: 93.5 us
  Pallas kernels  46 us (49%)
  starting transfers between devices  18.7 us (20%)
  waiting for transfers between devices  10 us (11%)
  matrix products  8.61 us (9%)
  local copies, waits for them, and re-layouts  6.25 us (7%)
  other arithmetic  2.48 us (3%)
  between operations  1.4 us (1%)
    pallas_call x1, Pallas kernels, body(): reducer(term_conv.astype(jnp.bfloat16).reshape(nx, nzh, nc, rc, n_conv),...  46 us
    ppermute x2, starting transfers between devices, passed_along(): return lax.ppermute(array, axis, pairs)  18.7 us
    ppermute x2, waiting for transfers between devices, passed_along(): return lax.ppermute(array, axis, pairs)  10 us
    unnamed x16, local copies, waits for them, and re-layouts  4.17 us
    dot_general x1, matrix products, body(): jnp.einsum('tk,tn->kn', inputs, pre_grad, preferred_element_type=jnp.floa...  2.62 us
    broadcast_in_dim x1, other arithmetic, body(): return (grad_rows[None], sum_conv, sum_res)  2.47 us
    dot_general x1, matrix products, gate_backward(): pre_act = jnp.dot(inputs, w_conv, preferred_element_type=jnp.float32)  2.46 us
  transfers between devices with their start and end apart: 2, of which 1 were waited for; matrix products, arithmetic and copies ran while one was open for 7% of the time, Pallas kernels for 49%

profile of v4, /device:TPU:1, one launch (start us, length us, event | category | flops | bytes accessed | tf_op | source)
XLA Modules:
  0.0 93.5 jit_solution(11892060038986818973)
XLA Ops:
  0.6 0.0 copy-start
  0.6 1.2 %slice_bitcast_fusion.1 = (bf16[256,512]{1,0:T(8,128)(2,1)S(1)}, bf16[256,512]{1,0:T(8,128)(2,1)S(1)}) fusion(bf16[1,512,512]{2,1,0:T(8,128)(2,1)} %param.5), kind=kLoop, calls=%fused_computation.23 | loop fusion | bytes 1048576 | tf_op jit(solution)/shard_map/slice | solution.py:255
  1.9 16.8 %collective-permute-start = (bf16[256,512]{1,0:T(8,128)(2,1)S(1)}, bf16[256,512]{1,0:T(8,128)(2,1)S(1)}, u32[]{:S(2)}, u32[]{:S(2)}) collective-permute-start(bf16[256,512]{1,0:T(8,128)(2,1)S(1)} %get-tuple-element.14), channel_id=1, source_target_pairs={{0,32},{32,64},{64,96},{96,128},{128,160},{160,192},{192,224},{224... | collective-permute-start | bytes 786440 | tf_op jit(solution)/shard_map/ppermute | solution.py:15
  19.4 10.0 %collective-permute-done = bf16[256,512]{1,0:T(8,128)(2,1)S(1)} collective-permute-done((bf16[256,512]{1,0:T(8,128)(2,1)S(1)}, bf16[256,512]{1,0:T(8,128)(2,1)S(1)}, u32[]{:S(2)}, u32[]{:S(2)}) %collective-permute-start) | collective-permute-done | bytes 262176 | tf_op jit(solution)/shard_map/ppermute | solution.py:15
  29.4 0.0 copy-start.5
  29.4 0.0 copy-done
  29.4 0.0 copy-start.3
  29.4 0.0 copy-start.4
  29.4 2.5 %fusion.10 = f32[512,1024]{0,1:T(8,128)S(1)} fusion(bf16[1024,1024]{1,0:T(8,128)(2,1)S(1)} %copy-done, bf16[512,512]{1,0:T(8,128)(2,1)} %bitcast.24, bf16[256,512]{1,0:T(8,128)(2,1)S(1)} %get-tuple-element.15, bf16[256,512]{1,0:T(8,128)(2,1)S(1)} %collective-permute-done), kind=kOutput, calls=%fused_computation.21 | convolution fusion | flops 1076887552 | bytes 5242880 | tf_op jit(solution)/shard_map/dot_general | solution.py:20
  31.9 0.0 copy-done.5
  31.9 0.0 copy-done.3
  31.9 0.0 copy-done.4
  31.9 0.9 multiply_convert_fusion.2
  32.7 1.3 %fusion.5 = f32[512,1024]{1,0:T(8,128)S(1)} fusion(bf16[1024,1024]{1,0:T(8,128)(2,1)S(1)} %copy-done, bf16[512,512]{0,1:T(8,128)(2,1)S(1)} %get-tuple-element.11, bf16[512,512]{0,1:T(8,128)(2,1)S(1)} %get-tuple-element.10), kind=kOutput, calls=%fused_computation.16 | convolution fusion | flops 1075838976 | bytes 5242880 | tf_op jit(solution)/shard_map/dot_general | solution.py:263
  34.0 0.0 copy-start.1
  34.1 1.3 %copy-done.1 = f32[512,1024]{1,0:T(8,128)} copy-done((f32[512,1024]{1,0:T(8,128)}, f32[512,1024]{1,0:T(8,128)S(1)}, u32[]{:S(2)}) %copy-start.1) | copy-done | bytes 2097176
  35.4 0.0 copy-start.2
  35.4 0.0 copy-start.6
  35.4 0.9 fusion.16
  36.2 1.9 %collective-permute-start.1 = (f32[256,512]{1,0:T(8,128)}, f32[256,512]{1,0:T(8,128)}, u32[]{:S(2)}, u32[]{:S(2)}) collective-permute-start(f32[256,512]{1,0:T(8,128)} %get-tuple-element.13), channel_id=1, source_target_pairs={{32,0},{64,32},{96,64},{128,96},{160,128},{192,160},{224,192},{256... | collective-permute-start | bytes 1572872 | tf_op jit(solution)/shard_map/ppermute | solution.py:15
  38.2 0.0 copy-done.2
  38.2 0.0 copy-done.6
  38.2 2.6 %convolution_convert_fusion = bf16[1024,1024]{1,0:T(8,128)(2,1)} fusion(bf16[512,512]{0,1:T(8,128)(2,1)S(1)} %get-tuple-element.11, bf16[512,512]{0,1:T(8,128)(2,1)S(1)} %get-tuple-element.10, bf16[512,512]{1,0:T(8,128)(2,1)S(1)} %bitcast.25, bf16[256,512]{1,0:T(8,128)(2,1)S(1)} %get-tuple-element.15, bf16[256,512]{1,0:T(8,128)(2,1)S(1)} %copy-done.6), kind=kOutput, calls=%fused_computation | convolution fusion | flops 1080033280 | bytes 4194304 | tf_op jit(solution)/shard_map/tk,tn->kn/dot_general | solution.py:271
  40.8 1.4 %convolution_convert_fusion.1 = bf16[512,512]{1,0:T(8,128)(2,1)} fusion(f32[512,1024]{0,1:T(8,128)S(1)} %fusion.10, bf16[1,512,512]{2,1,0:T(8,128)(2,1)S(1)} %copy-done.3, f32[512]{0:T(512)S(1)} %fusion.11), kind=kOutput, calls=%fused_computation.2 | convolution fusion | flops 270270464 | bytes 3147776 | tf_op jit(solution)/shard_map/tk,tn->kn/dot_general | solution.py:272
  42.2 46.0 %shard_map.76 = (f32[64,32]{1,0:T(8,128)}, f32[32,16]{1,0:T(8,128)}) custom-call(bf16[4,2,2,64,1024]{4,3,2,1,0:T(8,128)(2,1)} %bitcast.22, bf16[4,2,2,32,512]{4,3,2,1,0:T(8,128)(2,1)} %bitcast.23), custom_call_target="tpu_custom_call" | custom-call | tf_op jit(solution)/shard_map/pallas_call | solution.py:278
  88.2 1.4 %copy.10 = f32[64,32]{0,1:T(8,128)} copy(f32[64,32]{1,0:T(8,128)} %get-tuple-element.8) | data formatting | bytes 16384
  89.6 1.4 %copy.11 = f32[32,16]{0,1:T(8,128)} copy(f32[32,16]{1,0:T(8,128)} %get-tuple-element.9) | data formatting | bytes 4096
  91.0 0.0 collective-permute-done.1
  91.0 2.5 %fusion.6 = bf16[1,512,512]{2,1,0:T(8,128)(2,1)} fusion(f32[256,512]{1,0:T(8,128)} %collective-permute-done.1, f32[256,512]{1,0:T(8,128)S(1)} %get-tuple-element.12, f32[512,1024]{1,0:T(8,128)} %copy-done.1, bf16[1,512,512]{2,1,0:T(8,128)(2,1)S(1)} %copy-done.3), kind=kLoop, calls=%fused_computation.17 | loop fusion | flops 1310720 | bytes 3145728 | tf_op jit(solution)/shard_map/broadcast_in_dim | solution.py:282
  (1 shorter events, 0.0 us)
Async XLA Ops:
  0.6 28.8 %copy-start = (bf16[1024,1024]{1,0:T(8,128)(2,1)S(1)}, bf16[1024,1024]{1,0:T(8,128)(2,1)}, u32[]{:S(2)}) copy-start(bf16[1024,1024]{1,0:T(8,128)(2,1)} %param.7) | copy-start | bytes 6291460
  1.9 27.5 %collective-permute-start = (bf16[256,512]{1,0:T(8,128)(2,1)S(1)}, bf16[256,512]{1,0:T(8,128)(2,1)S(1)}, u32[]{:S(2)}, u32[]{:S(2)}) collective-permute-start(bf16[256,512]{1,0:T(8,128)(2,1)S(1)} %get-tuple-element.14), channel_id=1, source_target_pairs={{0,32},{32,64},{64,96},{96,128},{128,160},{160,192},{192,224},{224... | collective-permute-start | bytes 786440 | tf_op jit(solution)/shard_map/ppermute | solution.py:15
  29.4 2.5 %copy-start.5 = (bf16[256,512]{1,0:T(8,128)(2,1)}, bf16[256,512]{1,0:T(8,128)(2,1)S(1)}, u32[]{:S(2)}) copy-start(bf16[256,512]{1,0:T(8,128)(2,1)S(1)} %collective-permute-done) | copy-start | bytes 786436
  29.4 2.5 %copy-start.3 = (bf16[1,512,512]{2,1,0:T(8,128)(2,1)S(1)}, bf16[1,512,512]{2,1,0:T(8,128)(2,1)}, u32[]{:S(2)}) copy-start(bf16[1,512,512]{2,1,0:T(8,128)(2,1)} %param.6) | copy-start | bytes 1572868
  29.4 2.5 %copy-start.4 = (bf16[512,512]{1,0:T(8,128)(2,1)S(1)}, bf16[512,512]{1,0:T(8,128)(2,1)}, u32[]{:S(2)}) copy-start(bf16[512,512]{1,0:T(8,128)(2,1)} %param.8) | copy-start | bytes 1572868
  34.0 1.3 %copy-start.1 = (f32[512,1024]{1,0:T(8,128)}, f32[512,1024]{1,0:T(8,128)S(1)}, u32[]{:S(2)}) copy-start(f32[512,1024]{1,0:T(8,128)S(1)} %fusion.5) | copy-start | bytes 6291460
  35.4 2.8 %copy-start.2 = (bf16[1,512,512]{2,1,0:T(8,128)(2,1)S(1)}, bf16[1,512,512]{2,1,0:T(8,128)(2,1)}, u32[]{:S(2)}) copy-start(bf16[1,512,512]{2,1,0:T(8,128)(2,1)} %param.5) | copy-start | bytes 1572868
  35.4 2.8 %copy-start.6 = (bf16[256,512]{1,0:T(8,128)(2,1)S(1)}, bf16[256,512]{1,0:T(8,128)(2,1)}, u32[]{:S(2)}) copy-start(bf16[256,512]{1,0:T(8,128)(2,1)} %copy-done.5) | copy-start | bytes 786436
  36.2 54.8 %collective-permute-start.1 = (f32[256,512]{1,0:T(8,128)}, f32[256,512]{1,0:T(8,128)}, u32[]{:S(2)}, u32[]{:S(2)}) collective-permute-start(f32[256,512]{1,0:T(8,128)} %get-tuple-element.13), channel_id=1, source_target_pairs={{32,0},{64,32},{96,64},{128,96},{160,128},{192,160},{224,192},{256... | collective-permute-start | bytes 1572872 | tf_op jit(solution)/shard_map/ppermute | solution.py:15

commit v5 on v4

--- a/solution.py
+++ b/solution.py
@@ -251,25 +251,40 @@
         seq_len = lengths[0]
         count_of_rows = sequence_rows.shape[0]
         channel_count = sequence_rows.shape[1]
+        step = DILATION_STEP
         start_row = lax.axis_index(TM) * count_of_rows
-        trailing_rows = sequence_rows[count_of_rows - DILATION_STEP :]
-        arrived = passed_along(trailing_rows, TM, 1, n_tm)
-        prior_samples = jnp.concatenate(
-            [arrived, sequence_rows[: count_of_rows - DILATION_STEP]], 0
+        arrived = passed_along(sequence_rows[count_of_rows - step :], TM, 1, n_tm)
+        in_length = (start_row + jnp.arange(count_of_rows) < seq_len).astype(jnp.float32)[:, None]
+        w_earlier, w_current = w_conv[:channel_count], w_conv[channel_count:]
+        current_part = jnp.dot(sequence_rows, w_current, preferred_element_type=jnp.float32)
+        gated_grad = in_length * jnp.dot(cotangent, w_res.T, preferred_element_type=jnp.float32)
+
+        def rows_of(lo, hi, prior):
+            pre_act = current_part[lo:hi] + jnp.dot(prior, w_earlier, preferred_element_type=jnp.float32)
+            tanh_f = jnp.tanh(pre_act[:, :channel_count])
+            sig_g = jax.nn.sigmoid(pre_act[:, channel_count:])
+            gated = (in_length[lo:hi] * tanh_f * sig_g).astype(jnp.bfloat16)
+            grad = gated_grad[lo:hi]
+            pre_grad = jnp.concatenate(
+                [grad * sig_g * (1.0 - tanh_f * tanh_f), grad * tanh_f * sig_g * (1.0 - sig_g)], 1
+            ).astype(jnp.bfloat16)
+            inputs = jnp.concatenate([prior, sequence_rows[lo:hi]], 1)
+            input_gradient = jnp.dot(pre_grad, w_conv.T, preferred_element_type=jnp.float32)
+            term_conv = jnp.einsum("tk,tn->kn", inputs, pre_grad, preferred_element_type=jnp.float32)
+            term_res = jnp.einsum("tk,tn->kn", gated, cotangent[lo:hi], preferred_element_type=jnp.float32)
+            return input_gradient, term_conv, term_res
+
+        late_grad, late_conv, late_res = rows_of(step, count_of_rows, sequence_rows[: count_of_rows - step])
+        early_grad, early_conv, early_res = rows_of(0, step, arrived)
+        incoming_gradient = passed_along(early_grad[:, :channel_count].astype(jnp.bfloat16), TM, -1, n_tm)
+        delayed_gradient = jnp.concatenate(
+            [early_grad[step:, :channel_count], late_grad[:, :channel_count],
+             incoming_gradient.astype(jnp.float32)], 0
         )
-        inputs = jnp.concatenate([prior_samples, sequence_rows], 1)
-        in_length = (start_row + jnp.arange(count_of_rows) < seq_len).astype(jnp.float32)[:, None]
-        gated, pre_grad = gate_backward(inputs, cotangent, in_length, w_conv, w_res)
-        input_gradient = jnp.dot(pre_grad, w_conv.T, preferred_element_type=jnp.float32)
-        incoming_gradient = passed_along(input_gradient[:DILATION_STEP, :channel_count], TM, -1, n_tm)
-        delayed_gradient = jnp.concatenate(
-            [input_gradient[DILATION_STEP:, :channel_count], incoming_gradient], 0
-        )
-        grad_rows = (
-            cotangent.astype(jnp.float32) + input_gradient[:, channel_count:] + delayed_gradient
-        ).astype(jnp.bfloat16)
-        term_conv = jnp.einsum("tk,tn->kn", inputs, pre_grad, preferred_element_type=jnp.float32)
-        term_res = jnp.einsum("tk,tn->kn", gated, cotangent, preferred_element_type=jnp.float32)
+        current_gradient = jnp.concatenate([early_grad[:, channel_count:], late_grad[:, channel_count:]], 0)
+        grad_rows = (cotangent.astype(jnp.float32) + current_gradient + delayed_gradient).astype(jnp.bfloat16)
+        term_conv = early_conv + late_conv
+        term_res = early_res + late_res
         kc, n_conv = term_conv.shape
         kr, n_res = term_res.shape
         rc, rr = kc // n_tm, kr // n_tm

time: 93.9 us -> 96.2 us (1.024)
  matrix products: 8.61 us -> 13.6 us
  waiting for transfers between devices: 10 us -> 6.66 us
    dot_general x5 -> x10, matrix products: 8.61 us -> 13.6 us  [the longest x2 4.79 us: rows_of(): jnp.einsum('tk,tn->kn', inputs, pre_grad, preferred_element_type=jnp.floa...]
    ppermute x2, waiting for transfers between devices: 10 us -> 6.66 us  [passed_along(): return lax.ppermute(array, axis, pairs)]
    broadcast_in_dim x1 -> x0, other arithmetic: 2.47 us -> none  [body(): return (grad_rows[None], sum_conv, sum_res)]
    convert_element_type x0 -> x1, other arithmetic: none -> 1.12 us  [body(): (cotangent.astype(jnp.float32) + current_gradient + delayed_gradient).ast...]
    concatenate x0 -> x1, other arithmetic: none -> 1 us  [body(): jnp.concatenate([early_grad[step:, :channel_count], late_grad[:, :channel...]
    unnamed x16 -> x18, local copies, waits for them, and re-layouts: 4.17 us -> 3.38 us
    slice x2 -> x3, local copies, waits for them, and re-layouts: 2.08 us -> 2.62 us  [the longest x1 1.82 us: body(): sequence_rows[:count_of_rows - step]]
  transfers between devices with their start and end apart: 2 -> 2, of which waited for: 1 -> 1; matrix products, arithmetic and copies ran while one was open for 7% -> 15% of each run, Pallas kernels for 49% -> 48%
where the time goes in v5:
time: 96.2 us; the launch traced here: 95.7 us
  Pallas kernels  46.2 us (48%)
  starting transfers between devices  19 us (20%)
  matrix products  13.6 us (14%)
  waiting for transfers between devices  6.66 us (7%)
  local copies, waits for them, and re-layouts  6.13 us (6%)
  other arithmetic  2.69 us (3%)
  between operations  1.47 us (2%)
    pallas_call x1, Pallas kernels, body(): reducer(term_conv.astype(jnp.bfloat16).reshape(nx, nzh, nc, rc, n_conv),...  46.2 us
    ppermute x2, starting transfers between devices, passed_along(): return lax.ppermute(array, axis, pairs)  19 us
    ppermute x2, waiting for transfers between devices, passed_along(): return lax.ppermute(array, axis, pairs)  6.66 us
    dot_general x2, matrix products, rows_of(): jnp.einsum('tk,tn->kn', inputs, pre_grad, preferred_element_type=jnp.floa...  4.79 us
    unnamed x18, local copies, waits for them, and re-layouts  3.38 us
    dot_general x2, matrix products, rows_of(): jnp.dot(pre_grad, w_conv.T, preferred_element_type=jnp.float32)  2.54 us
    dot_general x1, matrix products, body(): jnp.dot(sequence_rows, w_current, preferred_element_type=jnp.float32)  2.15 us
    dot_general x2, matrix products, rows_of(): jnp.dot(prior, w_earlier, preferred_element_type=jnp.float32)  2.07 us
  transfers between devices with their start and end apart: 2, of which 1 were waited for; matrix products, arithmetic and copies ran while one was open for 15% of the time, Pallas kernels for 48%

profile of v5, /device:TPU:1, one launch (start us, length us, event | category | flops | bytes accessed | tf_op | source)
XLA Modules:
  0.0 95.7 jit_solution(13743445144114849806)
XLA Ops:
  0.6 0.0 copy-start
  0.6 1.8 %slice_bitcast_fusion.3 = (bf16[256,512]{1,0:T(8,128)(2,1)S(1)}, bf16[256,512]{1,0:T(8,128)(2,1)}) fusion(bf16[1,512,512]{2,1,0:T(8,128)(2,1)} %param.5), kind=kLoop, calls=%fused_computation.54 | loop fusion | bytes 1048576 | tf_op jit(solution)/shard_map/slice | solution.py:277
  2.5 17.1 %collective-permute-start = (bf16[256,512]{1,0:T(8,128)(2,1)}, bf16[256,512]{1,0:T(8,128)(2,1)}, u32[]{:S(2)}, u32[]{:S(2)}) collective-permute-start(bf16[256,512]{1,0:T(8,128)(2,1)} %get-tuple-element.19), channel_id=1, source_target_pairs={{0,32},{32,64},{64,96},{96,128},{128,160},{160,192},{192,224},{224... | collective-permute-start | bytes 786440 | tf_op jit(solution)/shard_map/ppermute | solution.py:15
  20.2 2.1 %fusion.3 = f32[512,1024]{0,1:T(8,128)S(1)} fusion(bf16[1024,1024]{1,0:T(8,128)(2,1)} %param.7, bf16[1,512,512]{2,1,0:T(8,128)(2,1)} %param.5), kind=kOutput, calls=%fused_computation.9 | convolution fusion | flops 536870912 | bytes 3670016 | tf_op jit(solution)/shard_map/dot_general | solution.py:259
  22.4 0.0 copy-done.1
  22.4 0.0 copy-done.3
  22.4 0.0 copy-start.6
  22.4 0.6 convolution_add_fusion.1
  23.0 0.0 copy-done
  23.0 0.5 copy-done.6
  23.5 0.5 convolution_multiply_fusion
  23.9 6.7 %collective-permute-done = bf16[256,512]{1,0:T(8,128)(2,1)} collective-permute-done((bf16[256,512]{1,0:T(8,128)(2,1)}, bf16[256,512]{1,0:T(8,128)(2,1)}, u32[]{:S(2)}, u32[]{:S(2)}) %collective-permute-start) | collective-permute-done | bytes 262176 | tf_op jit(solution)/shard_map/ppermute | solution.py:15
  30.6 1.5 %convolution_add_fusion.2 = f32[256,1024]{0,1:T(8,128)S(1)} fusion(bf16[256,512]{1,0:T(8,128)(2,1)} %collective-permute-done, f32[512,1024]{0,1:T(8,128)S(1)} %fusion.3, bf16[1024,1024]{1,0:T(8,128)(2,1)S(1)} %copy-done.1), kind=kOutput, calls=%fused_computation.4 | convolution fusion | flops 268697600 | bytes 3407872 | tf_op jit(solution)/shard_map/dot_general | solution.py:263
  32.1 0.4 fusion.24
  32.5 0.6 multiply_convert_fusion.5
  33.1 0.8 fusion.23
  33.8 0.0 copy-start.4
  33.9 0.8 slice.184
  34.7 1.9 %collective-permute-start.1 = (bf16[256,512]{1,0:T(8,128)(2,1)}, bf16[256,512]{1,0:T(8,128)(2,1)}, u32[]{:S(2)}, u32[]{:S(2)}) collective-permute-start(bf16[256,512]{1,0:T(8,128)(2,1)} %slice.184), channel_id=1, source_target_pairs={{32,0},{64,32},{96,64},{128,96},{160,128},{192,160},{224,192},{256... | collective-permute-start | bytes 786440 | tf_op jit(solution)/shard_map/ppermute | solution.py:15
  36.6 1.8 %fusion.22 = f32[256,1024]{1,0:T(8,128)} fusion(bf16[1024,1024]{1,0:T(8,128)(2,1)S(1)} %copy-done.1, bf16[256,512]{0,1:T(8,128)(2,1)S(1)} %get-tuple-element.16, bf16[256,512]{0,1:T(8,128)(2,1)S(1)} %get-tuple-element.17), kind=kOutput, calls=%fused_computation.44 | convolution fusion | flops 537919488 | bytes 3670016 | tf_op jit(solution)/shard_map/dot_general | solution.py:272
  38.3 0.0 copy-done.4
  38.3 1.7 %fusion.16 = f32[1024,1024]{1,0:T(8,128)S(1)} fusion(bf16[256,512]{1,0:T(8,128)(2,1)} %get-tuple-element.19, bf16[256,512]{1,0:T(8,128)(2,1)S(1)} %get-tuple-element.18, bf16[256,512]{0,1:T(8,128)(2,1)S(1)} %get-tuple-element.16, bf16[256,512]{0,1:T(8,128)(2,1)S(1)} %get-tuple-element.17), kind=kOutput, calls=%fused_computation.32 | convolution fusion | flops 538968064 | bytes 5242880 | tf_op jit(solution)/shard_map/tk,tn->kn/dot_general | solution.py:273
  40.0 1.2 %fusion = bf16[512,512]{1,0:T(8,128)(2,1)} fusion(f32[512,512]{1,0:T(8,128)S(1)} %fusion.24, f32[256,1024]{0,1:T(8,128)S(1)} %convolution_add_fusion.1, bf16[1,512,512]{2,1,0:T(8,128)(2,1)S(1)} %copy-done.6, f32[256]{0:T(256)S(1)} %get-tuple-element.20), kind=kOutput, calls=%fused_computation.5 | convolution fusion | flops 135528448 | bytes 2884608 | tf_op jit(solution)/shard_map/tk,tn->kn/dot_general | solution.py:274
  41.2 3.1 %add_convert_fusion = bf16[1024,1024]{1,0:T(8,128)(2,1)} fusion(f32[1024,1024]{1,0:T(8,128)S(1)} %fusion.16, bf16[256,512]{1,0:T(8,128)(2,1)S(1)} %get-tuple-element.18, bf16[256,512]{1,0:T(8,128)(2,1)} %collective-permute-done, bf16[256,512]{0,1:T(8,128)(2,1)S(1)} %get-tuple-element.11, bf16[256,512]{0,1:T(8,128)(2,1)S(1)} %get-tuple-element.10), kind=kOutput, calls=%fused_computation | convolution fusion | flops 541065216 | bytes 7340032 | tf_op jit(solution)/shard_map/tk,tn->kn/dot_general | solution.py:273
  44.3 46.2 %shard_map.76 = (f32[64,32]{1,0:T(8,128)}, f32[32,16]{1,0:T(8,128)}) custom-call(bf16[4,2,2,64,1024]{4,3,2,1,0:T(8,128)(2,1)} %bitcast.34, bf16[4,2,2,32,512]{4,3,2,1,0:T(8,128)(2,1)} %bitcast.35), custom_call_target="tpu_custom_call" | custom-call | tf_op jit(solution)/shard_map/pallas_call | solution.py:293
  90.5 0.0 copy-start.7
  90.5 1.5 %copy.12 = f32[64,32]{0,1:T(8,128)} copy(f32[64,32]{1,0:T(8,128)} %get-tuple-element.8) | data formatting | bytes 16384
  92.0 1.4 %copy.13 = f32[32,16]{0,1:T(8,128)} copy(f32[32,16]{1,0:T(8,128)} %get-tuple-element.9) | data formatting | bytes 4096
  93.4 0.1 slice_bitcast_fusion
  93.5 0.0 collective-permute-done.1
  93.5 1.0 %bitcast_convert_fusion = f32[1,256,512]{2,1,0:T(8,128)S(1)} fusion(bf16[256,512]{1,0:T(8,128)(2,1)} %collective-permute-done.1), kind=kLoop, calls=%fused_computation.47 | loop fusion | flops 131072 | bytes 786432 | tf_op jit(solution)/shard_map/concatenate | solution.py:280
  94.6 1.1 %fusion.2 = bf16[1,512,512]{2,1,0:T(8,128)(2,1)} fusion(f32[1,256,512]{2,1,0:T(8,128)S(1)} %get-tuple-element.15, f32[1,256,512]{2,1,0:T(8,128)S(1)} %get-tuple-element.22, f32[1,256,512]{2,1,0:T(8,128)S(1)} %bitcast_convert_fusion, f32[1,256,512]{2,1,0:T(8,128)S(1)} %get-tuple-element.14, bf16[1,512,512]{2,1,0:T(8,128)(2,1)S(1)} %copy-done.7), kind=kLoop, calls=%fused_computation.8 | loop fusion | flops 1572864 | bytes 3145728 | tf_op jit(solution)/shard_map/convert_element_type | solution.py:285
  (9 shorter events, 0.0 us)
Async XLA Ops:
  0.6 22.4 %copy-start = (bf16[512,512]{1,0:T(8,128)(2,1)S(1)}, bf16[512,512]{1,0:T(8,128)(2,1)}, u32[]{:S(2)}) copy-start(bf16[512,512]{1,0:T(8,128)(2,1)} %param.8) | copy-start | bytes 1572868
  2.5 19.9 %copy-start.1 = (bf16[1024,1024]{1,0:T(8,128)(2,1)S(1)}, bf16[1024,1024]{1,0:T(8,128)(2,1)}, u32[]{:S(2)}) copy-start(bf16[1024,1024]{1,0:T(8,128)(2,1)} %param.7) | copy-start | bytes 6291460
  2.5 19.9 %copy-start.3 = (bf16[1,512,512]{2,1,0:T(8,128)(2,1)S(1)}, bf16[1,512,512]{2,1,0:T(8,128)(2,1)}, u32[]{:S(2)}) copy-start(bf16[1,512,512]{2,1,0:T(8,128)(2,1)} %param.5) | copy-start | bytes 1572868
  2.5 28.1 %collective-permute-start = (bf16[256,512]{1,0:T(8,128)(2,1)}, bf16[256,512]{1,0:T(8,128)(2,1)}, u32[]{:S(2)}, u32[]{:S(2)}) collective-permute-start(bf16[256,512]{1,0:T(8,128)(2,1)} %get-tuple-element.19), channel_id=1, source_target_pairs={{0,32},{32,64},{64,96},{96,128},{128,160},{160,192},{192,224},{224... | collective-permute-start | bytes 786440 | tf_op jit(solution)/shard_map/ppermute | solution.py:15
  22.4 1.0 %copy-start.6 = (bf16[1,512,512]{2,1,0:T(8,128)(2,1)S(1)}, bf16[1,512,512]{2,1,0:T(8,128)(2,1)}, u32[]{:S(2)}) copy-start(bf16[1,512,512]{2,1,0:T(8,128)(2,1)} %param.6) | copy-start | bytes 1572868
  33.8 4.5 %copy-start.4 = (f32[256,1024]{1,0:T(8,128)}, f32[256,1024]{1,0:T(8,128)S(1)}, u32[]{:S(2)}) copy-start(f32[256,1024]{1,0:T(8,128)S(1)} %fusion.23) | copy-start | bytes 3145732
  34.7 58.9 %collective-permute-start.1 = (bf16[256,512]{1,0:T(8,128)(2,1)}, bf16[256,512]{1,0:T(8,128)(2,1)}, u32[]{:S(2)}, u32[]{:S(2)}) collective-permute-start(bf16[256,512]{1,0:T(8,128)(2,1)} %slice.184), channel_id=1, source_target_pairs={{32,0},{64,32},{96,64},{128,96},{160,128},{192,160},{224,192},{256... | collective-permute-start | bytes 786440 | tf_op jit(solution)/shard_map/ppermute | solution.py:15
  44.3 49.1 %copy-start.2 = (f32[256,1024]{1,0:T(8,128)S(1)}, f32[256,1024]{1,0:T(8,128)}, u32[]{:S(2)}) copy-start(f32[256,1024]{1,0:T(8,128)} %fusion.22) | copy-start | bytes 3145732
  44.3 49.1 %copy-start.5 = (f32[256,1024]{1,0:T(8,128)S(1)}, f32[256,1024]{1,0:T(8,128)}, u32[]{:S(2)}) copy-start(f32[256,1024]{1,0:T(8,128)} %copy-done.4) | copy-start | bytes 3145732
  90.5 4.1 %copy-start.7 = (bf16[1,512,512]{2,1,0:T(8,128)(2,1)S(1)}, bf16[1,512,512]{2,1,0:T(8,128)(2,1)}, u32[]{:S(2)}) copy-start(bf16[1,512,512]{2,1,0:T(8,128)(2,1)} %param.6) | copy-start | bytes 1572868

commit v6 on v4

--- a/solution.py
+++ b/solution.py
@@ -199,8 +199,8 @@
             sz = lax.rem(me_z + nz - d, nz)
             acc_c = acc_c + rz_conv[sz].astype(jnp.float32)
             acc_r = acc_r + rz_res[sz].astype(jnp.float32)
-        conv_out[...] = acc_c.T * scale
-        res_out[...] = acc_r.T * scale
+        conv_out[...] = acc_c * scale
+        res_out[...] = acc_r * scale
         for copy in sends:
             copy.wait_send()
 
@@ -208,7 +208,7 @@
     bf16, f32 = jnp.bfloat16, jnp.float32
     return pl.pallas_call(
         kernel,
-        out_shape=(jax.ShapeDtypeStruct((rc, cc), f32), jax.ShapeDtypeStruct((rr, cr), f32)),
+        out_shape=(jax.ShapeDtypeStruct((cc, rc), f32), jax.ShapeDtypeStruct((cr, rr), f32)),
         in_specs=[vmem, vmem],
         out_specs=(vmem, vmem),
         scratch_shapes=[
@@ -261,7 +261,9 @@
         in_length = (start_row + jnp.arange(count_of_rows) < seq_len).astype(jnp.float32)[:, None]
         gated, pre_grad = gate_backward(inputs, cotangent, in_length, w_conv, w_res)
         input_gradient = jnp.dot(pre_grad, w_conv.T, preferred_element_type=jnp.float32)
-        incoming_gradient = passed_along(input_gradient[:DILATION_STEP, :channel_count], TM, -1, n_tm)
+        incoming_gradient = passed_along(
+            input_gradient[:DILATION_STEP, :channel_count].astype(jnp.bfloat16), TM, -1, n_tm
+        ).astype(jnp.float32)
         delayed_gradient = jnp.concatenate(
             [input_gradient[DILATION_STEP:, :channel_count], incoming_gradient], 0
         )
@@ -275,11 +277,11 @@
         rc, rr = kc // n_tm, kr // n_tm
         all_tokens = count_of_rows * n_tm * n_rep
         reducer = make_reducer(sizes, rc, n_conv, rr, n_res, float(all_tokens) ** (-0.5))
-        sum_conv, sum_res = reducer(
+        flip_conv, flip_res = reducer(
             term_conv.astype(jnp.bfloat16).reshape(nx, nzh, nc, rc, n_conv),
             term_res.astype(jnp.bfloat16).reshape(nx, nzh, nc, rr, n_res),
         )
-        return (grad_rows[None], sum_conv, sum_res)
+        return (grad_rows[None], flip_conv.T, flip_res.T)
 
     return body
 

time: 93.9 us -> 91.1 us (0.970)
  local copies, waits for them, and re-layouts: 6.25 us -> 3.91 us
    unnamed x16 -> x24, local copies, waits for them, and re-layouts: 4.17 us -> 1.88 us
  transfers between devices with their start and end apart: 2 -> 2, of which waited for: 1 -> 1; matrix products, arithmetic and copies ran while one was open for 7% -> 4% of each run, Pallas kernels for 49% -> 50%
where the time goes in v6:
time: 91.1 us; the launch traced here: 90.8 us
  Pallas kernels  45.6 us (50%)
  starting transfers between devices  18.8 us (21%)
  waiting for transfers between devices  10 us (11%)
  matrix products  8.61 us (9%)
  local copies, waits for them, and re-layouts  3.91 us (4%)
  other arithmetic  2.38 us (3%)
  between operations  1.48 us (2%)
    pallas_call x1, Pallas kernels, body(): reducer(term_conv.astype(jnp.bfloat16).reshape(nx, nzh, nc, rc, n_conv),...  45.6 us
    ppermute x2, starting transfers between devices, passed_along(): return lax.ppermute(array, axis, pairs)  18.8 us
    ppermute x2, waiting for transfers between devices, passed_along(): return lax.ppermute(array, axis, pairs)  10 us
    dot_general x1, matrix products, body(): jnp.einsum('tk,tn->kn', inputs, pre_grad, preferred_element_type=jnp.floa...  2.63 us
    dot_general x1, matrix products, gate_backward(): pre_act = jnp.dot(inputs, w_conv, preferred_element_type=jnp.float32)  2.46 us
    broadcast_in_dim x1, other arithmetic, body(): return (grad_rows[None], flip_conv.T, flip_res.T)  2.32 us
    unnamed x24, local copies, waits for them, and re-layouts  1.88 us
  transfers between devices with their start and end apart: 2, of which 1 were waited for; matrix products, arithmetic and copies ran while one was open for 4% of the time, Pallas kernels for 50%

profile of v6, /device:TPU:1, one launch (start us, length us, event | category | flops | bytes accessed | tf_op | source)
XLA Modules:
  0.0 90.8 jit_solution(12694948705837505673)
XLA Ops:
  0.6 0.0 copy-start
  0.6 1.2 %slice_bitcast_fusion.1 = (bf16[256,512]{1,0:T(8,128)(2,1)S(1)}, bf16[256,512]{1,0:T(8,128)(2,1)S(1)}) fusion(bf16[1,512,512]{2,1,0:T(8,128)(2,1)} %param.5), kind=kLoop, calls=%fused_computation.24 | loop fusion | bytes 1048576 | tf_op jit(solution)/shard_map/slice | solution.py:255
  1.9 0.0 copy-start.4
  1.9 16.8 %collective-permute-start = (bf16[256,512]{1,0:T(8,128)(2,1)S(1)}, bf16[256,512]{1,0:T(8,128)(2,1)S(1)}, u32[]{:S(2)}, u32[]{:S(2)}) collective-permute-start(bf16[256,512]{1,0:T(8,128)(2,1)S(1)} %get-tuple-element.9), channel_id=1, source_target_pairs={{0,32},{32,64},{64,96},{96,128},{128,160},{160,192},{192,224},{224... | collective-permute-start | bytes 786440 | tf_op jit(solution)/shard_map/ppermute | solution.py:15
  19.4 10.0 %collective-permute-done = bf16[256,512]{1,0:T(8,128)(2,1)S(1)} collective-permute-done((bf16[256,512]{1,0:T(8,128)(2,1)S(1)}, bf16[256,512]{1,0:T(8,128)(2,1)S(1)}, u32[]{:S(2)}, u32[]{:S(2)}) %collective-permute-start) | collective-permute-done | bytes 262176 | tf_op jit(solution)/shard_map/ppermute | solution.py:15
  29.4 0.0 copy-done
  29.4 2.5 %fusion.10 = f32[512,1024]{0,1:T(8,128)S(1)} fusion(bf16[1024,1024]{1,0:T(8,128)(2,1)S(1)} %copy-done, bf16[512,512]{1,0:T(8,128)(2,1)} %bitcast.26, bf16[256,512]{1,0:T(8,128)(2,1)S(1)} %get-tuple-element.10, bf16[256,512]{1,0:T(8,128)(2,1)S(1)} %collective-permute-done), kind=kOutput, calls=%fused_computation.22 | convolution fusion | flops 1076887552 | bytes 5242880 | tf_op jit(solution)/shard_map/dot_general | solution.py:20
  31.9 0.0 copy-done.4
  31.9 0.0 copy-done.9
  31.9 0.0 copy-done.3
  31.9 0.0 copy-done.8
  31.9 0.9 multiply_convert_fusion.2
  32.8 0.0 copy-start.2
  32.8 0.0 copy-start.5
  32.8 0.0 copy-start.10
  32.8 1.3 %fusion.5 = f32[512,1024]{1,0:T(8,128)S(1)} fusion(bf16[1024,1024]{1,0:T(8,128)(2,1)S(1)} %copy-done, bf16[512,512]{0,1:T(8,128)(2,1)S(1)} %get-tuple-element.8, bf16[512,512]{0,1:T(8,128)(2,1)S(1)} %get-tuple-element.7), kind=kOutput, calls=%fused_computation.16 | convolution fusion | flops 1075838976 | bytes 5242880 | tf_op jit(solution)/shard_map/dot_general | solution.py:263
  34.1 0.0 copy-start.1
  34.1 0.8 slice.74
  34.9 0.6 copy-done.1
  35.6 1.9 %collective-permute-start.1 = (bf16[256,512]{1,0:T(8,128)(2,1)}, bf16[256,512]{1,0:T(8,128)(2,1)S(1)}, u32[]{:S(2)}, u32[]{:S(2)}) collective-permute-start(bf16[256,512]{1,0:T(8,128)(2,1)} %slice.74), channel_id=1, source_target_pairs={{32,0},{64,32},{96,64},{128,96},{160,128},{192,160},{224,192},{256... | collective-permute-start | bytes 786440 | tf_op jit(solution)/shard_map/ppermute | solution.py:15
  37.5 0.0 copy-done.2
  37.5 0.0 copy-done.5
  37.5 0.0 copy-done.10
  37.5 2.6 %convolution_convert_fusion = bf16[1024,1024]{1,0:T(8,128)(2,1)} fusion(bf16[512,512]{0,1:T(8,128)(2,1)S(1)} %get-tuple-element.8, bf16[512,512]{0,1:T(8,128)(2,1)S(1)} %get-tuple-element.7, bf16[512,512]{1,0:T(8,128)(2,1)S(1)} %bitcast.27, bf16[256,512]{1,0:T(8,128)(2,1)S(1)} %copy-done.5, bf16[256,512]{1,0:T(8,128)(2,1)S(1)} %copy-done.10), kind=kOutput, calls=%fused_computation | convolution fusion | flops 1080033280 | bytes 4194304 | tf_op jit(solution)/shard_map/tk,tn->kn/dot_general | solution.py:273
  40.1 1.4 %convolution_convert_fusion.1 = bf16[512,512]{1,0:T(8,128)(2,1)} fusion(f32[512,1024]{0,1:T(8,128)S(1)} %fusion.10, bf16[1,512,512]{2,1,0:T(8,128)(2,1)S(1)} %copy-done.3, f32[512]{0:T(512)S(1)} %fusion.11), kind=kOutput, calls=%fused_computation.2 | convolution fusion | flops 270270464 | bytes 3147776 | tf_op jit(solution)/shard_map/tk,tn->kn/dot_general | solution.py:274
  41.5 45.6 %shard_map.76 = (f32[32,64]{1,0:T(8,128)}, f32[16,32]{1,0:T(8,128)}) custom-call(bf16[4,2,2,64,1024]{4,3,2,1,0:T(8,128)(2,1)} %bitcast.24, bf16[4,2,2,32,512]{4,3,2,1,0:T(8,128)(2,1)} %bitcast.25), custom_call_target="tpu_custom_call" | custom-call | tf_op jit(solution)/shard_map/pallas_call | solution.py:280
  87.2 0.0 copy-start.6
  87.2 0.0 collective-permute-done.1
  87.2 0.1 convert_element_type.29
  87.3 2.3 %fusion.6 = bf16[1,512,512]{2,1,0:T(8,128)(2,1)} fusion(f32[256,512]{1,0:T(8,128)S(1)} %convert_element_type.29, f32[256,512]{1,0:T(8,128)S(1)} %slice.40, f32[512,1024]{1,0:T(8,128)} %copy-done.1, bf16[1,512,512]{2,1,0:T(8,128)(2,1)S(1)} %copy-done.3), kind=kLoop, calls=%fused_computation.17 | loop fusion | flops 1310720 | bytes 3145728 | tf_op jit(solution)/shard_map/broadcast_in_dim | solution.py:284
  89.6 0.6 copy.14
  90.2 0.6 copy.15
  (8 shorter events, 0.1 us)
Async XLA Ops:
  0.6 28.8 %copy-start = (bf16[1024,1024]{1,0:T(8,128)(2,1)S(1)}, bf16[1024,1024]{1,0:T(8,128)(2,1)}, u32[]{:S(2)}) copy-start(bf16[1024,1024]{1,0:T(8,128)(2,1)} %param.7) | copy-start | bytes 6291460
  1.9 30.0 %copy-start.4 = (bf16[256,512]{1,0:T(8,128)(2,1)}, bf16[256,512]{1,0:T(8,128)(2,1)S(1)}, u32[]{:S(2)}) copy-start(bf16[256,512]{1,0:T(8,128)(2,1)S(1)} %get-tuple-element.10) | copy-start | bytes 786436
  1.9 27.5 %collective-permute-start = (bf16[256,512]{1,0:T(8,128)(2,1)S(1)}, bf16[256,512]{1,0:T(8,128)(2,1)S(1)}, u32[]{:S(2)}, u32[]{:S(2)}) collective-permute-start(bf16[256,512]{1,0:T(8,128)(2,1)S(1)} %get-tuple-element.9), channel_id=1, source_target_pairs={{0,32},{32,64},{64,96},{96,128},{128,160},{160,192},{192,224},{224... | collective-permute-start | bytes 786440 | tf_op jit(solution)/shard_map/ppermute | solution.py:15
  29.4 2.5 %copy-start.9 = (bf16[256,512]{1,0:T(8,128)(2,1)}, bf16[256,512]{1,0:T(8,128)(2,1)S(1)}, u32[]{:S(2)}) copy-start(bf16[256,512]{1,0:T(8,128)(2,1)S(1)} %collective-permute-done) | copy-start | bytes 786436
  29.4 2.5 %copy-start.3 = (bf16[1,512,512]{2,1,0:T(8,128)(2,1)S(1)}, bf16[1,512,512]{2,1,0:T(8,128)(2,1)}, u32[]{:S(2)}) copy-start(bf16[1,512,512]{2,1,0:T(8,128)(2,1)} %param.6) | copy-start | bytes 1572868
  29.4 2.5 %copy-start.8 = (bf16[512,512]{1,0:T(8,128)(2,1)S(1)}, bf16[512,512]{1,0:T(8,128)(2,1)}, u32[]{:S(2)}) copy-start(bf16[512,512]{1,0:T(8,128)(2,1)} %param.8) | copy-start | bytes 1572868
  32.8 4.7 %copy-start.2 = (bf16[1,512,512]{2,1,0:T(8,128)(2,1)S(1)}, bf16[1,512,512]{2,1,0:T(8,128)(2,1)}, u32[]{:S(2)}) copy-start(bf16[1,512,512]{2,1,0:T(8,128)(2,1)} %param.5) | copy-start | bytes 1572868
  32.8 4.7 %copy-start.5 = (bf16[256,512]{1,0:T(8,128)(2,1)S(1)}, bf16[256,512]{1,0:T(8,128)(2,1)}, u32[]{:S(2)}) copy-start(bf16[256,512]{1,0:T(8,128)(2,1)} %copy-done.4) | copy-start | bytes 786436
  32.8 4.7 %copy-start.10 = (bf16[256,512]{1,0:T(8,128)(2,1)S(1)}, bf16[256,512]{1,0:T(8,128)(2,1)}, u32[]{:S(2)}) copy-start(bf16[256,512]{1,0:T(8,128)(2,1)} %copy-done.9) | copy-start | bytes 786436
  34.1 1.4 %copy-start.1 = (f32[512,1024]{1,0:T(8,128)}, f32[512,1024]{1,0:T(8,128)S(1)}, u32[]{:S(2)}) copy-start(f32[512,1024]{1,0:T(8,128)S(1)} %fusion.5) | copy-start | bytes 6291460
  35.6 51.6 %collective-permute-start.1 = (bf16[256,512]{1,0:T(8,128)(2,1)}, bf16[256,512]{1,0:T(8,128)(2,1)S(1)}, u32[]{:S(2)}, u32[]{:S(2)}) collective-permute-start(bf16[256,512]{1,0:T(8,128)(2,1)} %slice.74), channel_id=1, source_target_pairs={{32,0},{64,32},{96,64},{128,96},{160,128},{192,160},{224,192},{256... | collective-permute-start | bytes 786440 | tf_op jit(solution)/shard_map/ppermute | solution.py:15
  87.2 2.4 %copy-start.6 = (f32[32,64]{1,0:T(8,128)S(1)}, f32[32,64]{1,0:T(8,128)}, u32[]{:S(2)}) copy-start(f32[32,64]{1,0:T(8,128)} %get-tuple-element.5) | copy-start | bytes 24580
  87.2 3.0 %copy-start.7 = (f32[16,32]{1,0:T(8,128)S(1)}, f32[16,32]{1,0:T(8,128)}, u32[]{:S(2)}) copy-start(f32[16,32]{1,0:T(8,128)} %get-tuple-element.6) | copy-start | bytes 6148

commit v7 on v6

--- a/solution.py
+++ b/solution.py
@@ -240,6 +240,75 @@
     )
 
 
+def make_halo(sizes):
+    nx, nzh, nc, ny, nzl = sizes
+    n_tm = nx * nzh * nc
+    mesh_id = pl.DeviceIdType.MESH
+
+    def kernel(src_ref, out_ref, buf, send_sem, recv_sem):
+        me_y = lax.axis_index("y")
+        me_zl = lax.axis_index("zl")
+        t = (lax.axis_index("x") * nzh + lax.axis_index("zh")) * nc + lax.axis_index("c")
+
+        def dev(u):
+            return (u // (nzh * nc), lax.rem(u // nc, nzh), lax.rem(u, nc), me_y, me_zl)
+
+        nxt = jnp.minimum(t + 1, n_tm - 1)
+        prv = jnp.maximum(t - 1, 0)
+        has_next = t < n_tm - 1
+        has_prev = t > 0
+        barrier = pltpu.get_barrier_semaphore()
+
+        @pl.when(has_next)
+        def _():
+            pl.semaphore_signal(barrier, inc=1, device_id=dev(nxt), device_id_type=mesh_id)
+
+        @pl.when(has_prev)
+        def _():
+            pl.semaphore_signal(barrier, inc=1, device_id=dev(prv), device_id_type=mesh_id)
+
+        pl.semaphore_wait(barrier, (1 - (t + 1) // n_tm) + (t + n_tm - 1) // n_tm)
+
+        copy = pltpu.make_async_remote_copy(
+            src_ref=src_ref, dst_ref=buf, send_sem=send_sem, recv_sem=recv_sem,
+            device_id=dev(nxt), device_id_type=mesh_id)
+
+        @pl.when(has_next)
+        def _():
+            copy.start()
+
+        @pl.when(has_prev)
+        def _():
+            copy.wait_recv()
+            out_ref[...] = buf[...]
+
+        @pl.when(t == 0)
+        def _():
+            out_ref[...] = jnp.zeros_like(out_ref)
+
+        @pl.when(has_next)
+        def _():
+            copy.wait_send()
+
+    vmem = pl.BlockSpec(memory_space=pltpu.VMEM)
+
+    def call(rows):
+        return pl.pallas_call(
+            kernel,
+            out_shape=jax.ShapeDtypeStruct(rows.shape, rows.dtype),
+            in_specs=[vmem],
+            out_specs=vmem,
+            scratch_shapes=[
+                pltpu.VMEM(rows.shape, rows.dtype),
+                pltpu.SemaphoreType.DMA(()),
+                pltpu.SemaphoreType.DMA(()),
+            ],
+            compiler_params=pltpu.CompilerParams(collective_id=1, has_side_effects=True),
+        )(rows)
+
+    return call
+
+
 def make_body(sizes):
     nx, nzh, nc, ny, nzl = sizes
     n_tm = nx * nzh * nc
@@ -253,7 +322,7 @@
         channel_count = sequence_rows.shape[1]
         start_row = lax.axis_index(TM) * count_of_rows
         trailing_rows = sequence_rows[count_of_rows - DILATION_STEP :]
-        arrived = passed_along(trailing_rows, TM, 1, n_tm)
+        arrived = make_halo(sizes)(trailing_rows)
         prior_samples = jnp.concatenate(
             [arrived, sequence_rows[: count_of_rows - DILATION_STEP]], 0
         )

time: 91.1 us -> 92.3 us (1.013)
  Pallas kernels: 45.6 us -> 73.6 us
  starting transfers between devices: 18.8 us -> 1.91 us
  waiting for transfers between devices: 10 us -> 0.01 us
    pallas_call x0 -> x1, Pallas kernels: none -> 20.7 us  [call(): pl.pallas_call(kernel, out_shape=jax.ShapeDtypeStruct(rows.shape, rows.dt...]
    ppermute x2 -> x1, starting transfers between devices: 18.8 us -> 1.91 us  [passed_along(): return lax.ppermute(array, axis, pairs)]
    ppermute x2 -> x1, waiting for transfers between devices: 10 us -> 0.01 us  [passed_along(): return lax.ppermute(array, axis, pairs)]
    pallas_call x1, Pallas kernels: 45.6 us -> 52.9 us  [body(): reducer(term_conv.astype(jnp.bfloat16).reshape(nx, nzh, nc, rc, n_conv),...]
    unnamed x24 -> x18, local copies, waits for them, and re-layouts: 1.88 us -> 1.25 us
  transfers between devices with their start and end apart: 2 -> 1, of which waited for: 1 -> 0; matrix products, arithmetic and copies ran while one was open for 4% -> 4% of each run, Pallas kernels for 50% -> 58%
where the time goes in v7:
time: 92.3 us; the launch traced here: 92 us
  Pallas kernels  73.6 us (80%)
  matrix products  8.64 us (9%)
  local copies, waits for them, and re-layouts  3.84 us (4%)
  other arithmetic  2.38 us (3%)
  starting transfers between devices  1.91 us (2%)
  between operations  1.62 us (2%)
    pallas_call x1, Pallas kernels, body(): reducer(term_conv.astype(jnp.bfloat16).reshape(nx, nzh, nc, rc, n_conv),...  52.9 us
    pallas_call x1, Pallas kernels, call(): pl.pallas_call(kernel, out_shape=jax.ShapeDtypeStruct(rows.shape, rows.dt...  20.7 us
    dot_general x1, matrix products, body(): jnp.einsum('tk,tn->kn', inputs, pre_grad, preferred_element_type=jnp.floa...  2.63 us
    dot_general x1, matrix products, gate_backward(): pre_act = jnp.dot(inputs, w_conv, preferred_element_type=jnp.float32)  2.49 us
    broadcast_in_dim x1, other arithmetic, body(): return (grad_rows[None], flip_conv.T, flip_res.T)  2.32 us
    ppermute x1, starting transfers between devices, passed_along(): return lax.ppermute(array, axis, pairs)  1.91 us
  transfers between devices with their start and end apart: 1, of which 0 were waited for; matrix products, arithmetic and copies ran while one was open for 4% of the time, Pallas kernels for 58%

profile of v7, /device:TPU:1, one launch (start us, length us, event | category | flops | bytes accessed | tf_op | source)
XLA Modules:
  0.0 92.0 jit_solution(14539585742180873207)
XLA Ops:
  0.6 0.0 copy-start
  1.4 1.8 %slice_bitcast_fusion.1 = (bf16[256,512]{1,0:T(8,128)(2,1)}, bf16[256,512]{1,0:T(8,128)(2,1)S(1)}) fusion(bf16[1,512,512]{2,1,0:T(8,128)(2,1)} %param.5), kind=kLoop, calls=%fused_computation.24 | loop fusion | bytes 1048576 | tf_op jit(solution)/shard_map/slice | solution.py:324
  3.2 20.7 %shard_map.76 = bf16[256,512]{1,0:T(8,128)(2,1)} custom-call(bf16[256,512]{1,0:T(8,128)(2,1)} %get-tuple-element.9.src_ref), custom_call_target="tpu_custom_call" | custom-call | tf_op jit(solution)/shard_map/pallas_call | solution.py:296
  24.0 0.0 copy-done
  24.0 0.0 copy-start.3
  24.0 0.0 copy-start.7
  24.0 2.5 %fusion.10 = f32[512,1024]{0,1:T(8,128)S(1)} fusion(bf16[1024,1024]{1,0:T(8,128)(2,1)S(1)} %copy-done, bf16[512,512]{1,0:T(8,128)(2,1)} %bitcast.26, bf16[256,512]{1,0:T(8,128)(2,1)S(1)} %get-tuple-element.10, bf16[256,512]{1,0:T(8,128)(2,1)} %shard_map.76), kind=kOutput, calls=%fused_computation.22 | convolution fusion | flops 1076887552 | bytes 5242880 | tf_op jit(solution)/shard_map/dot_general | solution.py:20
  26.5 0.0 copy-done.3
  26.5 0.0 copy-done.7
  26.5 0.9 multiply_convert_fusion.2
  27.4 0.0 copy-start.2
  27.4 0.0 copy-start.4
  27.4 1.3 %fusion.5 = f32[512,1024]{1,0:T(8,128)S(1)} fusion(bf16[1024,1024]{1,0:T(8,128)(2,1)S(1)} %copy-done, bf16[512,512]{0,1:T(8,128)(2,1)S(1)} %get-tuple-element.8, bf16[512,512]{0,1:T(8,128)(2,1)S(1)} %get-tuple-element.7), kind=kOutput, calls=%fused_computation.16 | convolution fusion | flops 1075838976 | bytes 5242880 | tf_op jit(solution)/shard_map/dot_general | solution.py:332
  28.7 0.0 copy-start.1
  28.7 0.8 slice.74
  29.5 1.9 %collective-permute-start = (bf16[256,512]{1,0:T(8,128)(2,1)}, bf16[256,512]{1,0:T(8,128)(2,1)S(1)}, u32[]{:S(2)}, u32[]{:S(2)}) collective-permute-start(bf16[256,512]{1,0:T(8,128)(2,1)} %slice.74), channel_id=1, source_target_pairs={{32,0},{64,32},{96,64},{128,96},{160,128},{192,160},{224,192},{256... | collective-permute-start | bytes 786440 | tf_op jit(solution)/shard_map/ppermute | solution.py:15
  31.4 0.0 copy-done.2
  31.4 0.0 copy-done.4
  31.4 2.6 %convolution_convert_fusion = bf16[1024,1024]{1,0:T(8,128)(2,1)} fusion(bf16[512,512]{0,1:T(8,128)(2,1)S(1)} %get-tuple-element.8, bf16[512,512]{0,1:T(8,128)(2,1)S(1)} %get-tuple-element.7, bf16[512,512]{1,0:T(8,128)(2,1)S(1)} %bitcast.27, bf16[256,512]{1,0:T(8,128)(2,1)S(1)} %get-tuple-element.10, bf16[256,512]{1,0:T(8,128)(2,1)S(1)} %copy-done.4), kind=kOutput, calls=%fused_computation | convolution fusion | flops 1080033280 | bytes 4194304 | tf_op jit(solution)/shard_map/tk,tn->kn/dot_general | solution.py:342
  34.1 0.0 copy-done.1
  34.1 1.4 %convolution_convert_fusion.1 = bf16[512,512]{1,0:T(8,128)(2,1)} fusion(f32[512,1024]{0,1:T(8,128)S(1)} %fusion.10, bf16[1,512,512]{2,1,0:T(8,128)(2,1)S(1)} %copy-done.3, f32[512]{0:T(512)S(1)} %fusion.11), kind=kOutput, calls=%fused_computation.2 | convolution fusion | flops 270270464 | bytes 3147776 | tf_op jit(solution)/shard_map/tk,tn->kn/dot_general | solution.py:343
  35.5 52.9 %shard_map.77 = (f32[32,64]{1,0:T(8,128)}, f32[16,32]{1,0:T(8,128)}) custom-call(bf16[4,2,2,64,1024]{4,3,2,1,0:T(8,128)(2,1)} %bitcast.24, bf16[4,2,2,32,512]{4,3,2,1,0:T(8,128)(2,1)} %bitcast.25), custom_call_target="tpu_custom_call" | custom-call | tf_op jit(solution)/shard_map/pallas_call | solution.py:349
  88.4 0.0 copy-start.5
  88.4 0.0 copy-start.6
  88.4 0.0 collective-permute-done
  88.4 0.1 convert_element_type.29
  88.5 2.3 %fusion.6 = bf16[1,512,512]{2,1,0:T(8,128)(2,1)} fusion(f32[256,512]{1,0:T(8,128)S(1)} %convert_element_type.29, f32[256,512]{1,0:T(8,128)S(1)} %slice.40, f32[512,1024]{1,0:T(8,128)} %copy-done.1, bf16[1,512,512]{2,1,0:T(8,128)(2,1)S(1)} %copy-done.3), kind=kLoop, calls=%fused_computation.17 | loop fusion | flops 1310720 | bytes 3145728 | tf_op jit(solution)/shard_map/broadcast_in_dim | solution.py:353
  90.8 0.0 copy-done.5
  90.8 0.6 copy.14
  91.4 0.0 copy-done.6
  91.4 0.6 copy.15
  (2 shorter events, 0.0 us)
Async XLA Ops:
  0.6 23.4 %copy-start = (bf16[1024,1024]{1,0:T(8,128)(2,1)S(1)}, bf16[1024,1024]{1,0:T(8,128)(2,1)}, u32[]{:S(2)}) copy-start(bf16[1024,1024]{1,0:T(8,128)(2,1)} %param.7) | copy-start | bytes 6291460
  24.0 2.5 %copy-start.3 = (bf16[1,512,512]{2,1,0:T(8,128)(2,1)S(1)}, bf16[1,512,512]{2,1,0:T(8,128)(2,1)}, u32[]{:S(2)}) copy-start(bf16[1,512,512]{2,1,0:T(8,128)(2,1)} %param.6) | copy-start | bytes 1572868
  24.0 2.5 %copy-start.7 = (bf16[512,512]{1,0:T(8,128)(2,1)S(1)}, bf16[512,512]{1,0:T(8,128)(2,1)}, u32[]{:S(2)}) copy-start(bf16[512,512]{1,0:T(8,128)(2,1)} %param.8) | copy-start | bytes 1572868
  27.4 4.0 %copy-start.2 = (bf16[1,512,512]{2,1,0:T(8,128)(2,1)S(1)}, bf16[1,512,512]{2,1,0:T(8,128)(2,1)}, u32[]{:S(2)}) copy-start(bf16[1,512,512]{2,1,0:T(8,128)(2,1)} %param.5) | copy-start | bytes 1572868
  27.4 4.0 %copy-start.4 = (bf16[256,512]{1,0:T(8,128)(2,1)S(1)}, bf16[256,512]{1,0:T(8,128)(2,1)}, u32[]{:S(2)}) copy-start(bf16[256,512]{1,0:T(8,128)(2,1)} %shard_map.76) | copy-start | bytes 786436
  28.7 5.4 %copy-start.1 = (f32[512,1024]{1,0:T(8,128)}, f32[512,1024]{1,0:T(8,128)S(1)}, u32[]{:S(2)}) copy-start(f32[512,1024]{1,0:T(8,128)S(1)} %fusion.5) | copy-start | bytes 6291460
  29.5 58.9 %collective-permute-start = (bf16[256,512]{1,0:T(8,128)(2,1)}, bf16[256,512]{1,0:T(8,128)(2,1)S(1)}, u32[]{:S(2)}, u32[]{:S(2)}) collective-permute-start(bf16[256,512]{1,0:T(8,128)(2,1)} %slice.74), channel_id=1, source_target_pairs={{32,0},{64,32},{96,64},{128,96},{160,128},{192,160},{224,192},{256... | collective-permute-start | bytes 786440 | tf_op jit(solution)/shard_map/ppermute | solution.py:15
  88.4 2.4 %copy-start.5 = (f32[32,64]{1,0:T(8,128)S(1)}, f32[32,64]{1,0:T(8,128)}, u32[]{:S(2)}) copy-start(f32[32,64]{1,0:T(8,128)} %get-tuple-element.5) | copy-start | bytes 24580
  88.4 3.0 %copy-start.6 = (f32[16,32]{1,0:T(8,128)S(1)}, f32[16,32]{1,0:T(8,128)}, u32[]{:S(2)}) copy-start(f32[16,32]{1,0:T(8,128)} %get-tuple-element.6) | copy-start | bytes 6148

commit v8 on v6

--- a/solution.py
+++ b/solution.py
@@ -240,6 +240,116 @@
     )
 
 
+def make_halo(sizes):
+    nx, nzh, nc, ny, nzl = sizes
+    n_tm = nx * nzh * nc
+    nz = nzh * nzl
+    quarter = nz // 4
+    mesh_id = pl.DeviceIdType.MESH
+
+    def kernel(src_ref, out_ref, buf_f, rel_a, rel_b, buf_a, buf_b, send_sems, recv_sems):
+        me_x = lax.axis_index("x")
+        me_c = lax.axis_index("c")
+        me_y = lax.axis_index("y")
+        me_zl = lax.axis_index("zl")
+        me_z = lax.axis_index("zh") * nzl + me_zl
+        t = (me_x * nzh + lax.axis_index("zh")) * nc + me_c
+        half = src_ref.shape[0] // 2
+
+        def dev(x, z, c):
+            return (x, z // nzl, c, me_y, lax.rem(z, nzl))
+
+        def dest_of(x, z):
+            t_d = lax.rem((x * nzh + z // nzl) * nc + nc, n_tm)
+            return dev(t_d // (nzh * nc), lax.rem(t_d // nc, nzh) * nzl + lax.rem(z, nzl), 0)
+
+        def copy(src, dst, k, peer):
+            return pltpu.make_async_remote_copy(
+                src_ref=src, dst_ref=dst, send_sem=send_sems.at[k], recv_sem=recv_sems.at[k],
+                device_id=peer, device_id_type=mesh_id)
+
+        barrier = pltpu.get_barrier_semaphore()
+
+        @pl.when(me_c == 0)
+        def _():
+            t_s = lax.rem(t + n_tm - 1, n_tm)
+            x_s = t_s // (nzh * nc)
+            z_s = lax.rem(t_s // nc, nzh) * nzl + me_zl
+            partner = dev(me_x, me_z, 1)
+            up = dev(x_s, lax.rem(z_s + quarter, nz), 1)
+            down = dev(x_s, lax.rem(z_s + nz - quarter, nz), 1)
+            for peer in (partner, up, down):
+                pl.semaphore_signal(barrier, inc=1, device_id=peer, device_id_type=mesh_id)
+            pl.semaphore_wait(barrier, 3)
+            whole = copy(src_ref, buf_f, 0, partner)
+            whole.start()
+            copy(src_ref.at[pl.ds(0, half)], buf_a, 3, up).wait_recv()
+            copy(src_ref.at[pl.ds(0, half)], buf_b, 4, down).wait_recv()
+
+            @pl.when(t > 0)
+            def _():
+                out_ref[pl.ds(0, half)] = buf_a[...]
+                out_ref[pl.ds(half, half)] = buf_b[...]
+
+            @pl.when(t == 0)
+            def _():
+                out_ref[...] = jnp.zeros_like(out_ref)
+
+            whole.wait_send()
+
+        @pl.when(me_c == 1)
+        def _():
+            z_up = lax.rem(me_z + quarter, nz)
+            z_down = lax.rem(me_z + nz - quarter, nz)
+            partner = dev(me_x, me_z, 0)
+            up = dev(me_x, z_up, 1)
+            down = dev(me_x, z_down, 1)
+            after_up = dest_of(me_x, z_up)
+            after_down = dest_of(me_x, z_down)
+            for peer in (partner, up, down, after_up, after_down):
+                pl.semaphore_signal(barrier, inc=1, device_id=peer, device_id_type=mesh_id)
+            pl.semaphore_wait(barrier, 5)
+            first = copy(src_ref.at[pl.ds(0, half)], rel_a, 1, up)
+            second = copy(src_ref.at[pl.ds(half, half)], rel_b, 2, down)
+            first.start()
+            second.start()
+            first.wait_recv()
+            on_a = copy(rel_a, buf_a, 3, after_down)
+            on_a.start()
+            second.wait_recv()
+            on_b = copy(rel_b, buf_b, 4, after_up)
+            on_b.start()
+            copy(src_ref, buf_f, 0, partner).wait_recv()
+            out_ref[...] = buf_f[...]
+            first.wait_send()
+            second.wait_send()
+            on_a.wait_send()
+            on_b.wait_send()
+
+    vmem = pl.BlockSpec(memory_space=pltpu.VMEM)
+
+    def call(rows):
+        half_shape = (rows.shape[0] // 2, rows.shape[1])
+        return pl.pallas_call(
+            kernel,
+            out_shape=jax.ShapeDtypeStruct(rows.shape, rows.dtype),
+            in_specs=[vmem],
+            out_specs=vmem,
+            scratch_shapes=[
+                pltpu.VMEM(rows.shape, rows.dtype),
+                pltpu.VMEM(half_shape, rows.dtype),
+                pltpu.VMEM(half_shape, rows.dtype),
+                pltpu.VMEM(half_shape, rows.dtype),
+                pltpu.VMEM(half_shape, rows.dtype),
+                pltpu.SemaphoreType.DMA((5,)),
+                pltpu.SemaphoreType.DMA((5,)),
+            ],
+            compiler_params=pltpu.CompilerParams(collective_id=1, has_side_effects=True),
+        )(rows)
+
+    return call
+
+
 def make_body(sizes):
     nx, nzh, nc, ny, nzl = sizes
     n_tm = nx * nzh * nc
@@ -253,7 +363,7 @@
         channel_count = sequence_rows.shape[1]
         start_row = lax.axis_index(TM) * count_of_rows
         trailing_rows = sequence_rows[count_of_rows - DILATION_STEP :]
-        arrived = passed_along(trailing_rows, TM, 1, n_tm)
+        arrived = make_halo(sizes)(trailing_rows)
         prior_samples = jnp.concatenate(
             [arrived, sequence_rows[: count_of_rows - DILATION_STEP]], 0
         )

time: 91.1 us -> 93 us (1.021)
  Pallas kernels: 45.6 us -> 68.6 us
  starting transfers between devices: 18.8 us -> 7.59 us
  waiting for transfers between devices: 10 us -> 0.01 us
    pallas_call x0 -> x1, Pallas kernels: none -> 30.1 us  [call(): pl.pallas_call(kernel, out_shape=jax.ShapeDtypeStruct(rows.shape, rows.dt...]
    ppermute x2 -> x1, starting transfers between devices: 18.8 us -> 7.59 us  [passed_along(): return lax.ppermute(array, axis, pairs)]
    ppermute x2 -> x1, waiting for transfers between devices: 10 us -> 0.01 us  [passed_along(): return lax.ppermute(array, axis, pairs)]
    pallas_call x1, Pallas kernels: 45.6 us -> 38.6 us  [body(): reducer(term_conv.astype(jnp.bfloat16).reshape(nx, nzh, nc, rc, n_conv),...]
    unnamed x24 -> x18, local copies, waits for them, and re-layouts: 1.88 us -> 1.25 us
  transfers between devices with their start and end apart: 2 -> 1, of which waited for: 1 -> 0; matrix products, arithmetic and copies ran while one was open for 4% -> 4% of each run, Pallas kernels for 50% -> 42%
where the time goes in v8:
time: 93 us; the launch traced here: 92.7 us
  Pallas kernels  68.6 us (74%)
  matrix products  8.64 us (9%)
  starting transfers between devices  7.59 us (8%)
  local copies, waits for them, and re-layouts  3.84 us (4%)
  other arithmetic  2.38 us (3%)
  between operations  1.62 us (2%)
    pallas_call x1, Pallas kernels, body(): reducer(term_conv.astype(jnp.bfloat16).reshape(nx, nzh, nc, rc, n_conv),...  38.6 us
    pallas_call x1, Pallas kernels, call(): pl.pallas_call(kernel, out_shape=jax.ShapeDtypeStruct(rows.shape, rows.dt...  30.1 us
    ppermute x1, starting transfers between devices, passed_along(): return lax.ppermute(array, axis, pairs)  7.59 us
    dot_general x1, matrix products, body(): jnp.einsum('tk,tn->kn', inputs, pre_grad, preferred_element_type=jnp.floa...  2.63 us
    dot_general x1, matrix products, gate_backward(): pre_act = jnp.dot(inputs, w_conv, preferred_element_type=jnp.float32)  2.49 us
    broadcast_in_dim x1, other arithmetic, body(): return (grad_rows[None], flip_conv.T, flip_res.T)  2.32 us
  transfers between devices with their start and end apart: 1, of which 0 were waited for; matrix products, arithmetic and copies ran while one was open for 4% of the time, Pallas kernels for 42%

profile of v8, /device:TPU:1, one launch (start us, length us, event | category | flops | bytes accessed | tf_op | source)
XLA Modules:
  0.0 92.7 jit_solution(3857885046354605080)
XLA Ops:
  0.6 0.0 copy-start
  1.4 1.8 %slice_bitcast_fusion.1 = (bf16[256,512]{1,0:T(8,128)(2,1)}, bf16[256,512]{1,0:T(8,128)(2,1)S(1)}) fusion(bf16[1,512,512]{2,1,0:T(8,128)(2,1)} %param.5), kind=kLoop, calls=%fused_computation.24 | loop fusion | bytes 1048576 | tf_op jit(solution)/shard_map/slice | solution.py:365
  3.2 30.1 %shard_map.76 = bf16[256,512]{1,0:T(8,128)(2,1)} custom-call(bf16[256,512]{1,0:T(8,128)(2,1)} %get-tuple-element.9.src_ref), custom_call_target="tpu_custom_call" | custom-call | tf_op jit(solution)/shard_map/pallas_call | solution.py:333
  33.3 0.0 copy-done
  33.3 0.0 copy-start.3
  33.3 0.0 copy-start.7
  33.3 2.5 %fusion.10 = f32[512,1024]{0,1:T(8,128)S(1)} fusion(bf16[1024,1024]{1,0:T(8,128)(2,1)S(1)} %copy-done, bf16[512,512]{1,0:T(8,128)(2,1)} %bitcast.26, bf16[256,512]{1,0:T(8,128)(2,1)S(1)} %get-tuple-element.10, bf16[256,512]{1,0:T(8,128)(2,1)} %shard_map.76), kind=kOutput, calls=%fused_computation.22 | convolution fusion | flops 1076887552 | bytes 5242880 | tf_op jit(solution)/shard_map/dot_general | solution.py:20
  35.8 0.0 copy-done.3
  35.8 0.0 copy-done.7
  35.9 0.9 multiply_convert_fusion.2
  36.7 0.0 copy-start.2
  36.7 0.0 copy-start.4
  36.7 1.3 %fusion.5 = f32[512,1024]{1,0:T(8,128)S(1)} fusion(bf16[1024,1024]{1,0:T(8,128)(2,1)S(1)} %copy-done, bf16[512,512]{0,1:T(8,128)(2,1)S(1)} %get-tuple-element.8, bf16[512,512]{0,1:T(8,128)(2,1)S(1)} %get-tuple-element.7), kind=kOutput, calls=%fused_computation.16 | convolution fusion | flops 1075838976 | bytes 5242880 | tf_op jit(solution)/shard_map/dot_general | solution.py:373
  38.0 0.0 copy-start.1
  38.0 0.8 slice.74
  38.8 7.6 %collective-permute-start = (bf16[256,512]{1,0:T(8,128)(2,1)}, bf16[256,512]{1,0:T(8,128)(2,1)S(1)}, u32[]{:S(2)}, u32[]{:S(2)}) collective-permute-start(bf16[256,512]{1,0:T(8,128)(2,1)} %slice.74), channel_id=1, source_target_pairs={{32,0},{64,32},{96,64},{128,96},{160,128},{192,160},{224,192},{256... | collective-permute-start | bytes 786440 | tf_op jit(solution)/shard_map/ppermute | solution.py:15
  46.4 0.0 copy-done.2
  46.4 0.0 copy-done.4
  46.5 2.6 %convolution_convert_fusion = bf16[1024,1024]{1,0:T(8,128)(2,1)} fusion(bf16[512,512]{0,1:T(8,128)(2,1)S(1)} %get-tuple-element.8, bf16[512,512]{0,1:T(8,128)(2,1)S(1)} %get-tuple-element.7, bf16[512,512]{1,0:T(8,128)(2,1)S(1)} %bitcast.27, bf16[256,512]{1,0:T(8,128)(2,1)S(1)} %get-tuple-element.10, bf16[256,512]{1,0:T(8,128)(2,1)S(1)} %copy-done.4), kind=kOutput, calls=%fused_computation | convolution fusion | flops 1080033280 | bytes 4194304 | tf_op jit(solution)/shard_map/tk,tn->kn/dot_general | solution.py:383
  49.1 0.0 copy-done.1
  49.1 1.4 %convolution_convert_fusion.1 = bf16[512,512]{1,0:T(8,128)(2,1)} fusion(f32[512,1024]{0,1:T(8,128)S(1)} %fusion.10, bf16[1,512,512]{2,1,0:T(8,128)(2,1)S(1)} %copy-done.3, f32[512]{0:T(512)S(1)} %fusion.11), kind=kOutput, calls=%fused_computation.2 | convolution fusion | flops 270270464 | bytes 3147776 | tf_op jit(solution)/shard_map/tk,tn->kn/dot_general | solution.py:384
  50.5 38.6 %shard_map.77 = (f32[32,64]{1,0:T(8,128)}, f32[16,32]{1,0:T(8,128)}) custom-call(bf16[4,2,2,64,1024]{4,3,2,1,0:T(8,128)(2,1)} %bitcast.24, bf16[4,2,2,32,512]{4,3,2,1,0:T(8,128)(2,1)} %bitcast.25), custom_call_target="tpu_custom_call" | custom-call | tf_op jit(solution)/shard_map/pallas_call | solution.py:390
  89.1 0.0 copy-start.5
  89.1 0.0 copy-start.6
  89.1 0.0 collective-permute-done
  89.1 0.1 convert_element_type.29
  89.2 2.3 %fusion.6 = bf16[1,512,512]{2,1,0:T(8,128)(2,1)} fusion(f32[256,512]{1,0:T(8,128)S(1)} %convert_element_type.29, f32[256,512]{1,0:T(8,128)S(1)} %slice.40, f32[512,1024]{1,0:T(8,128)} %copy-done.1, bf16[1,512,512]{2,1,0:T(8,128)(2,1)S(1)} %copy-done.3), kind=kLoop, calls=%fused_computation.17 | loop fusion | flops 1310720 | bytes 3145728 | tf_op jit(solution)/shard_map/broadcast_in_dim | solution.py:394
  91.5 0.0 copy-done.5
  91.5 0.6 copy.14
  92.1 0.0 copy-done.6
  92.1 0.6 copy.15
  (2 shorter events, 0.0 us)
Async XLA Ops:
  0.6 32.7 %copy-start = (bf16[1024,1024]{1,0:T(8,128)(2,1)S(1)}, bf16[1024,1024]{1,0:T(8,128)(2,1)}, u32[]{:S(2)}) copy-start(bf16[1024,1024]{1,0:T(8,128)(2,1)} %param.7) | copy-start | bytes 6291460
  33.3 2.5 %copy-start.3 = (bf16[1,512,512]{2,1,0:T(8,128)(2,1)S(1)}, bf16[1,512,512]{2,1,0:T(8,128)(2,1)}, u32[]{:S(2)}) copy-start(bf16[1,512,512]{2,1,0:T(8,128)(2,1)} %param.6) | copy-start | bytes 1572868
  33.3 2.5 %copy-start.7 = (bf16[512,512]{1,0:T(8,128)(2,1)S(1)}, bf16[512,512]{1,0:T(8,128)(2,1)}, u32[]{:S(2)}) copy-start(bf16[512,512]{1,0:T(8,128)(2,1)} %param.8) | copy-start | bytes 1572868
  36.7 9.7 %copy-start.2 = (bf16[1,512,512]{2,1,0:T(8,128)(2,1)S(1)}, bf16[1,512,512]{2,1,0:T(8,128)(2,1)}, u32[]{:S(2)}) copy-start(bf16[1,512,512]{2,1,0:T(8,128)(2,1)} %param.5) | copy-start | bytes 1572868
  36.7 9.7 %copy-start.4 = (bf16[256,512]{1,0:T(8,128)(2,1)S(1)}, bf16[256,512]{1,0:T(8,128)(2,1)}, u32[]{:S(2)}) copy-start(bf16[256,512]{1,0:T(8,128)(2,1)} %shard_map.76) | copy-start | bytes 786436
  38.0 11.0 %copy-start.1 = (f32[512,1024]{1,0:T(8,128)}, f32[512,1024]{1,0:T(8,128)S(1)}, u32[]{:S(2)}) copy-start(f32[512,1024]{1,0:T(8,128)S(1)} %fusion.5) | copy-start | bytes 6291460
  38.8 50.3 %collective-permute-start = (bf16[256,512]{1,0:T(8,128)(2,1)}, bf16[256,512]{1,0:T(8,128)(2,1)S(1)}, u32[]{:S(2)}, u32[]{:S(2)}) collective-permute-start(bf16[256,512]{1,0:T(8,128)(2,1)} %slice.74), channel_id=1, source_target_pairs={{32,0},{64,32},{96,64},{128,96},{160,128},{192,160},{224,192},{256... | collective-permute-start | bytes 786440 | tf_op jit(solution)/shard_map/ppermute | solution.py:15
  89.1 2.4 %copy-start.5 = (f32[32,64]{1,0:T(8,128)S(1)}, f32[32,64]{1,0:T(8,128)}, u32[]{:S(2)}) copy-start(f32[32,64]{1,0:T(8,128)} %get-tuple-element.5) | copy-start | bytes 24580
  89.1 3.0 %copy-start.6 = (f32[16,32]{1,0:T(8,128)S(1)}, f32[16,32]{1,0:T(8,128)}, u32[]{:S(2)}) copy-start(f32[16,32]{1,0:T(8,128)} %get-tuple-element.6) | copy-start | bytes 6148

commit v9 on v6

--- a/solution.py
+++ b/solution.py
@@ -29,7 +29,7 @@
     return (gated, pre_grad)
 
 
-def make_reducer(sizes, rc, n_conv, rr, n_res, scale):
+def make_reducer(sizes, rc, n_conv, rr, n_res, scale, edge_shape):
     nx, nzh, nc, ny, nzl = sizes
     nz = nzh * nzl
     cyc, cyr = n_conv // ny, n_res // ny
@@ -39,16 +39,17 @@
     base_ya, base_xb = 1 + nx + ny, 1 + nx + 2 * ny
     base_z = 1 + 2 * nx + 2 * ny
     n_slots = base_z + nz
-    n_peers = (nc - 1) + (nx - 1) + (ny - 1) + (nz - 1)
+    n_peers = (nc - 1) + (nx - 1) + (ny - 1) + (nz - 1) + 2
+    n_tm = nx * nzh * nc
     mesh_id = pl.DeviceIdType.MESH
 
-    def kernel(conv_ref, res_ref, conv_out, res_out,
+    def kernel(conv_ref, res_ref, edge_ref, conv_out, res_out, edge_out,
                rc_conv, rc_res, sx_conv, sx_res,
                rxa_conv, rxa_res, ryb_conv, ryb_res,
                sa_conv, sa_res, rya_conv, rya_res,
                sb_conv, sb_res, rxb_conv, rxb_res,
                sz_conv, sz_res, rz_conv, rz_res,
-               send_sems, recv_sems, local_sems):
+               edge_buf, send_sems, recv_sems, local_sems):
         me_x = lax.axis_index("x")
         me_zh = lax.axis_index("zh")
         me_c = lax.axis_index("c")
@@ -70,7 +71,14 @@
             q = lax.rem(me_z + d, nz)
             z_peers.append(dev(zh=q // nzl, zl=lax.rem(q, nzl)))
         barrier = pltpu.get_barrier_semaphore()
-        for peer in peers + x_peers + y_peers + z_peers:
+        t = (me_x * nzh + me_zh) * nc + me_c
+
+        def tm_dev(u):
+            return dev(x=u // (nzh * nc), zh=lax.rem(u // nc, nzh), c=lax.rem(u, nc))
+
+        before = tm_dev(lax.rem(t + n_tm - 1, n_tm))
+        after = tm_dev(lax.rem(t + 1, n_tm))
+        for peer in peers + x_peers + y_peers + z_peers + [before, after]:
             pl.semaphore_signal(barrier, inc=1, device_id=peer, device_id_type=mesh_id)
         pl.semaphore_wait(barrier, n_peers)
 
@@ -93,6 +101,11 @@
             copy = pltpu.make_async_copy(src, dst, local_sems.at[kind, which])
             copy.start()
             return copy
+
+        edge = pltpu.make_async_remote_copy(
+            src_ref=edge_ref, dst_ref=edge_buf, send_sem=local_sems.at[0, 2],
+            recv_sem=local_sems.at[1, 2], device_id=before, device_id_type=mesh_id)
+        edge.start()
 
         send(0, conv_ref.at[:, :, pl.ds(other_c, 1)], rc_conv, 0, peers[0])
         send(1, res_ref.at[:, :, pl.ds(other_c, 1)], rc_res, 0, peers[0])
@@ -201,16 +214,28 @@
             acc_r = acc_r + rz_res[sz].astype(jnp.float32)
         conv_out[...] = acc_c * scale
         res_out[...] = acc_r * scale
+        edge.wait_recv()
+
+        @pl.when(t < n_tm - 1)
+        def _():
+            edge_out[...] = edge_buf[...]
+
+        @pl.when(t == n_tm - 1)
+        def _():
+            edge_out[...] = jnp.zeros_like(edge_out)
+
         for copy in sends:
             copy.wait_send()
+        edge.wait_send()
 
     vmem = pl.BlockSpec(memory_space=pltpu.VMEM)
     bf16, f32 = jnp.bfloat16, jnp.float32
     return pl.pallas_call(
         kernel,
-        out_shape=(jax.ShapeDtypeStruct((cc, rc), f32), jax.ShapeDtypeStruct((cr, rr), f32)),
-        in_specs=[vmem, vmem],
-        out_specs=(vmem, vmem),
+        out_shape=(jax.ShapeDtypeStruct((cc, rc), f32), jax.ShapeDtypeStruct((cr, rr), f32),
+                   jax.ShapeDtypeStruct(edge_shape, bf16)),
+        in_specs=[vmem, vmem, vmem],
+        out_specs=(vmem, vmem, vmem),
         scratch_shapes=[
             pltpu.VMEM((nx, nzh, 1, rc, n_conv), bf16),
             pltpu.VMEM((nx, nzh, 1, rr, n_res), bf16),
@@ -232,9 +257,10 @@
             pltpu.VMEM((nz, cr, rr), bf16),
             pltpu.VMEM((nz, cc, rc), bf16),
             pltpu.VMEM((nz, cr, rr), bf16),
+            pltpu.VMEM(edge_shape, bf16),
             pltpu.SemaphoreType.DMA((2, n_slots)),
             pltpu.SemaphoreType.DMA((2, n_slots)),
-            pltpu.SemaphoreType.DMA((2, 2)),
+            pltpu.SemaphoreType.DMA((2, 3)),
         ],
         compiler_params=pltpu.CompilerParams(collective_id=0, has_side_effects=True),
     )
@@ -261,26 +287,25 @@
         in_length = (start_row + jnp.arange(count_of_rows) < seq_len).astype(jnp.float32)[:, None]
         gated, pre_grad = gate_backward(inputs, cotangent, in_length, w_conv, w_res)
         input_gradient = jnp.dot(pre_grad, w_conv.T, preferred_element_type=jnp.float32)
-        incoming_gradient = passed_along(
-            input_gradient[:DILATION_STEP, :channel_count].astype(jnp.bfloat16), TM, -1, n_tm
-        ).astype(jnp.float32)
-        delayed_gradient = jnp.concatenate(
-            [input_gradient[DILATION_STEP:, :channel_count], incoming_gradient], 0
-        )
-        grad_rows = (
-            cotangent.astype(jnp.float32) + input_gradient[:, channel_count:] + delayed_gradient
-        ).astype(jnp.bfloat16)
         term_conv = jnp.einsum("tk,tn->kn", inputs, pre_grad, preferred_element_type=jnp.float32)
         term_res = jnp.einsum("tk,tn->kn", gated, cotangent, preferred_element_type=jnp.float32)
         kc, n_conv = term_conv.shape
         kr, n_res = term_res.shape
         rc, rr = kc // n_tm, kr // n_tm
         all_tokens = count_of_rows * n_tm * n_rep
-        reducer = make_reducer(sizes, rc, n_conv, rr, n_res, float(all_tokens) ** (-0.5))
-        flip_conv, flip_res = reducer(
+        edge_rows = input_gradient[:DILATION_STEP, :channel_count].astype(jnp.bfloat16)
+        reducer = make_reducer(sizes, rc, n_conv, rr, n_res, float(all_tokens) ** (-0.5), edge_rows.shape)
+        flip_conv, flip_res, incoming_gradient = reducer(
             term_conv.astype(jnp.bfloat16).reshape(nx, nzh, nc, rc, n_conv),
             term_res.astype(jnp.bfloat16).reshape(nx, nzh, nc, rr, n_res),
+            edge_rows,
         )
+        delayed_gradient = jnp.concatenate(
+            [input_gradient[DILATION_STEP:, :channel_count], incoming_gradient.astype(jnp.float32)], 0
+        )
+        grad_rows = (
+            cotangent.astype(jnp.float32) + input_gradient[:, channel_count:] + delayed_gradient
+        ).astype(jnp.bfloat16)
         return (grad_rows[None], flip_conv.T, flip_res.T)
 
     return body

time: 91.1 us -> 90.9 us (level)
  starting transfers between devices: 18.8 us -> 16.8 us
  other arithmetic: 2.38 us -> 3.34 us
    ppermute x2 -> x1, starting transfers between devices: 18.8 us -> 16.8 us  [passed_along(): return lax.ppermute(array, axis, pairs)]
    convert_element_type x1, other arithmetic: 0.05 us -> 1.01 us  [body(): incoming_gradient.astype(jnp.float32)]
    unnamed x24 -> x20, local copies, waits for them, and re-layouts: 1.88 us -> 1.87 us
    ppermute x2 -> x1, waiting for transfers between devices: 10 us -> 10 us  [passed_along(): return lax.ppermute(array, axis, pairs)]
  transfers between devices with their start and end apart: 2 -> 1, of which waited for: 1 -> 1; matrix products, arithmetic and copies ran while one was open for 4% -> 0% of each run, Pallas kernels for 50% -> 0%
where the time goes in v9:
time: 90.9 us; the launch traced here: 90.6 us
  Pallas kernels  46.4 us (51%)
  starting transfers between devices  16.8 us (18%)
  waiting for transfers between devices  10 us (11%)
  matrix products  8.62 us (9%)
  local copies, waits for them, and re-layouts  3.9 us (4%)
  other arithmetic  3.34 us (4%)
  between operations  1.43 us (2%)
    pallas_call x1, Pallas kernels, body(): reducer(term_conv.astype(jnp.bfloat16).reshape(nx, nzh, nc, rc, n_conv),...  46.4 us
    ppermute x1, starting transfers between devices, passed_along(): return lax.ppermute(array, axis, pairs)  16.8 us
    ppermute x1, waiting for transfers between devices, passed_along(): return lax.ppermute(array, axis, pairs)  10 us
    dot_general x1, matrix products, body(): jnp.einsum('tk,tn->kn', inputs, pre_grad, preferred_element_type=jnp.floa...  2.62 us
    dot_general x1, matrix products, gate_backward(): pre_act = jnp.dot(inputs, w_conv, preferred_element_type=jnp.float32)  2.45 us
    broadcast_in_dim x1, other arithmetic, body(): return (grad_rows[None], flip_conv.T, flip_res.T)  2.32 us
    unnamed x20, local copies, waits for them, and re-layouts  1.87 us
  transfers between devices with their start and end apart: 1, of which 1 were waited for; matrix products, arithmetic and copies ran while one was open for 0% of the time, Pallas kernels for 0%

profile of v9, /device:TPU:1, one launch (start us, length us, event | category | flops | bytes accessed | tf_op | source)
XLA Modules:
  0.0 90.6 jit_solution(11633085354252016659)
XLA Ops:
  0.6 0.0 copy-start
  0.6 1.2 %slice_bitcast_fusion.1 = (bf16[256,512]{1,0:T(8,128)(2,1)S(1)}, bf16[256,512]{1,0:T(8,128)(2,1)S(1)}) fusion(bf16[1,512,512]{2,1,0:T(8,128)(2,1)} %param.5), kind=kLoop, calls=%fused_computation.24 | loop fusion | bytes 1048576 | tf_op jit(solution)/shard_map/slice | solution.py:281
  1.9 16.8 %collective-permute-start = (bf16[256,512]{1,0:T(8,128)(2,1)S(1)}, bf16[256,512]{1,0:T(8,128)(2,1)S(1)}, u32[]{:S(2)}, u32[]{:S(2)}) collective-permute-start(bf16[256,512]{1,0:T(8,128)(2,1)S(1)} %get-tuple-element.11), channel_id=1, source_target_pairs={{0,32},{32,64},{64,96},{96,128},{128,160},{160,192},{192,224},{224... | collective-permute-start | bytes 786440 | tf_op jit(solution)/shard_map/ppermute | solution.py:15
  19.4 10.0 %collective-permute-done = bf16[256,512]{1,0:T(8,128)(2,1)S(1)} collective-permute-done((bf16[256,512]{1,0:T(8,128)(2,1)S(1)}, bf16[256,512]{1,0:T(8,128)(2,1)S(1)}, u32[]{:S(2)}, u32[]{:S(2)}) %collective-permute-start) | collective-permute-done | bytes 262176 | tf_op jit(solution)/shard_map/ppermute | solution.py:15
  29.4 0.0 copy-start.7
  29.4 0.0 copy-done
  29.4 0.0 copy-start.3
  29.4 2.5 %fusion.10 = f32[512,1024]{0,1:T(8,128)S(1)} fusion(bf16[1024,1024]{1,0:T(8,128)(2,1)S(1)} %copy-done, bf16[512,512]{1,0:T(8,128)(2,1)} %bitcast.25, bf16[256,512]{1,0:T(8,128)(2,1)S(1)} %get-tuple-element.12, bf16[256,512]{1,0:T(8,128)(2,1)S(1)} %collective-permute-done), kind=kOutput, calls=%fused_computation.22 | convolution fusion | flops 1076887552 | bytes 5242880 | tf_op jit(solution)/shard_map/dot_general | solution.py:20
  31.8 0.0 copy-done.3
  31.9 0.0 copy-start.6
  31.9 1.4 %convolution_convert_fusion.1 = bf16[512,512]{1,0:T(8,128)(2,1)} fusion(f32[512,1024]{0,1:T(8,128)S(1)} %fusion.10, bf16[1,512,512]{2,1,0:T(8,128)(2,1)S(1)} %copy-done.3, f32[512]{0:T(512)S(1)} %fusion.11), kind=kOutput, calls=%fused_computation.2 | convolution fusion | flops 270270464 | bytes 3147776 | tf_op jit(solution)/shard_map/tk,tn->kn/dot_general | solution.py:291
  33.2 0.0 copy-done.7
  33.2 0.0 copy-done.6
  33.2 0.9 multiply_convert_fusion.2
  34.1 0.0 copy-start.2
  34.1 0.0 copy-start.8
  34.1 1.3 %fusion.5 = f32[512,1024]{1,0:T(8,128)S(1)} fusion(bf16[1024,1024]{1,0:T(8,128)(2,1)S(1)} %copy-done, bf16[512,512]{0,1:T(8,128)(2,1)S(1)} %get-tuple-element.10, bf16[512,512]{0,1:T(8,128)(2,1)S(1)} %get-tuple-element.9), kind=kOutput, calls=%fused_computation.16 | convolution fusion | flops 1075838976 | bytes 5242880 | tf_op jit(solution)/shard_map/dot_general | solution.py:289
  35.5 0.0 copy-start.1
  35.5 0.8 slice.74.edge_ref
  36.2 0.6 copy-done.1
  36.9 0.0 copy-done.2
  36.9 0.0 copy-done.8
  36.9 2.6 %convolution_convert_fusion = bf16[1024,1024]{1,0:T(8,128)(2,1)} fusion(bf16[512,512]{0,1:T(8,128)(2,1)S(1)} %get-tuple-element.10, bf16[512,512]{0,1:T(8,128)(2,1)S(1)} %get-tuple-element.9, bf16[512,512]{1,0:T(8,128)(2,1)S(1)} %bitcast.26, bf16[256,512]{1,0:T(8,128)(2,1)S(1)} %get-tuple-element.12, bf16[256,512]{1,0:T(8,128)(2,1)S(1)} %copy-done.8), kind=kOutput, calls=%fused_computation | convolution fusion | flops 1080033280 | bytes 4194304 | tf_op jit(solution)/shard_map/tk,tn->kn/dot_general | solution.py:290
  39.5 46.4 %shard_map.76 = (f32[32,64]{1,0:T(8,128)}, f32[16,32]{1,0:T(8,128)}, bf16[256,512]{1,0:T(8,128)(2,1)}) custom-call(bf16[4,2,2,64,1024]{4,3,2,1,0:T(8,128)(2,1)} %bitcast.24, bf16[4,2,2,32,512]{4,3,2,1,0:T(8,128)(2,1)} %bitcast.27, bf16[256,512]{1,0:T(8,128)(2,1)} %slice.74.edge_ref), custom_call_target="tpu_custom_call" | custom-call | tf_op jit(solution)/shard_map/pallas_call | solution.py:298
  86.0 0.0 copy-start.4
  86.0 0.0 copy-start.5
  86.0 1.0 %convert_element_type.32 = f32[256,512]{1,0:T(8,128)S(1)} convert(bf16[256,512]{1,0:T(8,128)(2,1)} %get-tuple-element.6) | non-fusion elementwise | flops 131072 | bytes 786432 | tf_op jit(solution)/shard_map/convert_element_type | solution.py:304
  87.0 2.3 %fusion.6 = bf16[1,512,512]{2,1,0:T(8,128)(2,1)} fusion(f32[256,512]{1,0:T(8,128)S(1)} %convert_element_type.32, f32[256,512]{1,0:T(8,128)S(1)} %slice.40, f32[512,1024]{1,0:T(8,128)} %copy-done.1, bf16[1,512,512]{2,1,0:T(8,128)(2,1)S(1)} %copy-done.3), kind=kLoop, calls=%fused_computation.17 | loop fusion | flops 1310720 | bytes 3145728 | tf_op jit(solution)/shard_map/broadcast_in_dim | solution.py:309
  89.4 0.0 copy-done.4
  89.4 0.6 copy.14
  90.0 0.0 copy-done.5
  90.0 0.6 copy.15
  (2 shorter events, 0.0 us)
Async XLA Ops:
  0.6 28.8 %copy-start = (bf16[1024,1024]{1,0:T(8,128)(2,1)S(1)}, bf16[1024,1024]{1,0:T(8,128)(2,1)}, u32[]{:S(2)}) copy-start(bf16[1024,1024]{1,0:T(8,128)(2,1)} %param.7) | copy-start | bytes 6291460
  1.9 27.5 %collective-permute-start = (bf16[256,512]{1,0:T(8,128)(2,1)S(1)}, bf16[256,512]{1,0:T(8,128)(2,1)S(1)}, u32[]{:S(2)}, u32[]{:S(2)}) collective-permute-start(bf16[256,512]{1,0:T(8,128)(2,1)S(1)} %get-tuple-element.11), channel_id=1, source_target_pairs={{0,32},{32,64},{64,96},{96,128},{128,160},{160,192},{192,224},{224... | collective-permute-start | bytes 786440 | tf_op jit(solution)/shard_map/ppermute | solution.py:15
  29.4 3.9 %copy-start.7 = (bf16[256,512]{1,0:T(8,128)(2,1)}, bf16[256,512]{1,0:T(8,128)(2,1)S(1)}, u32[]{:S(2)}) copy-start(bf16[256,512]{1,0:T(8,128)(2,1)S(1)} %collective-permute-done) | copy-start | bytes 786436
  29.4 2.5 %copy-start.3 = (bf16[1,512,512]{2,1,0:T(8,128)(2,1)S(1)}, bf16[1,512,512]{2,1,0:T(8,128)(2,1)}, u32[]{:S(2)}) copy-start(bf16[1,512,512]{2,1,0:T(8,128)(2,1)} %param.6) | copy-start | bytes 1572868
  31.9 1.4 %copy-start.6 = (bf16[512,512]{1,0:T(8,128)(2,1)S(1)}, bf16[512,512]{1,0:T(8,128)(2,1)}, u32[]{:S(2)}) copy-start(bf16[512,512]{1,0:T(8,128)(2,1)} %param.8) | copy-start | bytes 1572868
  34.1 2.8 %copy-start.2 = (bf16[1,512,512]{2,1,0:T(8,128)(2,1)S(1)}, bf16[1,512,512]{2,1,0:T(8,128)(2,1)}, u32[]{:S(2)}) copy-start(bf16[1,512,512]{2,1,0:T(8,128)(2,1)} %param.5) | copy-start | bytes 1572868
  34.1 2.8 %copy-start.8 = (bf16[256,512]{1,0:T(8,128)(2,1)S(1)}, bf16[256,512]{1,0:T(8,128)(2,1)}, u32[]{:S(2)}) copy-start(bf16[256,512]{1,0:T(8,128)(2,1)} %copy-done.7) | copy-start | bytes 786436
  35.5 1.4 %copy-start.1 = (f32[512,1024]{1,0:T(8,128)}, f32[512,1024]{1,0:T(8,128)S(1)}, u32[]{:S(2)}) copy-start(f32[512,1024]{1,0:T(8,128)S(1)} %fusion.5) | copy-start | bytes 6291460
  86.0 3.4 %copy-start.4 = (f32[32,64]{1,0:T(8,128)S(1)}, f32[32,64]{1,0:T(8,128)}, u32[]{:S(2)}) copy-start(f32[32,64]{1,0:T(8,128)} %get-tuple-element.7) | copy-start | bytes 24580
  86.0 4.0 %copy-start.5 = (f32[16,32]{1,0:T(8,128)S(1)}, f32[16,32]{1,0:T(8,128)}, u32[]{:S(2)}) copy-start(f32[16,32]{1,0:T(8,128)} %get-tuple-element.8) | copy-start | bytes 6148

commit v10 on v9

--- a/solution.py
+++ b/solution.py
@@ -295,17 +295,20 @@
         all_tokens = count_of_rows * n_tm * n_rep
         edge_rows = input_gradient[:DILATION_STEP, :channel_count].astype(jnp.bfloat16)
         reducer = make_reducer(sizes, rc, n_conv, rr, n_res, float(all_tokens) ** (-0.5), edge_rows.shape)
-        flip_conv, flip_res, incoming_gradient = reducer(
-            term_conv.astype(jnp.bfloat16).reshape(nx, nzh, nc, rc, n_conv),
-            term_res.astype(jnp.bfloat16).reshape(nx, nzh, nc, rr, n_res),
-            edge_rows,
-        )
-        delayed_gradient = jnp.concatenate(
-            [input_gradient[DILATION_STEP:, :channel_count], incoming_gradient.astype(jnp.float32)], 0
-        )
-        grad_rows = (
-            cotangent.astype(jnp.float32) + input_gradient[:, channel_count:] + delayed_gradient
+        split = count_of_rows - DILATION_STEP
+        head_rows = (
+            cotangent[:split].astype(jnp.float32) + input_gradient[:split, channel_count:]
+            + input_gradient[DILATION_STEP:, :channel_count]
         ).astype(jnp.bfloat16)
+        conv_in = term_conv.astype(jnp.bfloat16).reshape(nx, nzh, nc, rc, n_conv)
+        res_in = term_res.astype(jnp.bfloat16).reshape(nx, nzh, nc, rr, n_res)
+        head_rows, conv_in, res_in, edge_rows = lax.optimization_barrier((head_rows, conv_in, res_in, edge_rows))
+        flip_conv, flip_res, incoming_gradient = reducer(conv_in, res_in, edge_rows)
+        tail_rows = (
+            cotangent[split:].astype(jnp.float32) + input_gradient[split:, channel_count:]
+            + incoming_gradient.astype(jnp.float32)
+        ).astype(jnp.bfloat16)
+        grad_rows = jnp.concatenate([head_rows, tail_rows], 0)
         return (grad_rows[None], flip_conv.T, flip_res.T)
 
     return body

time: 90.9 us -> 89.5 us (0.985)
  other arithmetic: 3.34 us -> 2.2 us
    broadcast_in_dim x1, other arithmetic: 2.32 us -> 0.83 us  [body(): return (grad_rows[None], flip_conv.T, flip_res.T)]
    unnamed x20 -> x16, local copies, waits for them, and re-layouts: 1.87 us -> 1.89 us
where the time goes in v10:
time: 89.5 us; the launch traced here: 89.3 us
  Pallas kernels  46.4 us (52%)
  starting transfers between devices  16.8 us (19%)
  waiting for transfers between devices  10 us (11%)
  matrix products  8.57 us (10%)
  local copies, waits for them, and re-layouts  3.85 us (4%)
  other arithmetic  2.2 us (2%)
  between operations  1.4 us (2%)
    pallas_call x1, Pallas kernels, body(): flip_conv, flip_res, incoming_gradient = reducer(conv_in, res_in, edge_rows)  46.4 us
    ppermute x1, starting transfers between devices, passed_along(): return lax.ppermute(array, axis, pairs)  16.8 us
    ppermute x1, waiting for transfers between devices, passed_along(): return lax.ppermute(array, axis, pairs)  10 us
    dot_general x1, matrix products, body(): jnp.einsum('tk,tn->kn', inputs, pre_grad, preferred_element_type=jnp.floa...  2.63 us
    dot_general x1, matrix products, gate_backward(): pre_act = jnp.dot(inputs, w_conv, preferred_element_type=jnp.float32)  2.39 us
    unnamed x16, local copies, waits for them, and re-layouts  1.89 us
  transfers between devices with their start and end apart: 1, of which 1 were waited for; matrix products, arithmetic and copies ran while one was open for 0% of the time, Pallas kernels for 0%

profile of v10, /device:TPU:1, one launch (start us, length us, event | category | flops | bytes accessed | tf_op | source)
XLA Modules:
  0.0 89.3 jit_solution(639154378912191118)
XLA Ops:
  0.6 0.0 copy-start
  0.6 1.2 %slice_bitcast_fusion.1 = (bf16[256,512]{1,0:T(8,128)(2,1)S(1)}, bf16[256,512]{1,0:T(8,128)(2,1)S(1)}) fusion(bf16[1,512,512]{2,1,0:T(8,128)(2,1)} %param.5), kind=kLoop, calls=%fused_computation.27 | loop fusion | bytes 1048576 | tf_op jit(solution)/shard_map/slice | solution.py:281
  1.9 16.8 %collective-permute-start = (bf16[256,512]{1,0:T(8,128)(2,1)S(1)}, bf16[256,512]{1,0:T(8,128)(2,1)S(1)}, u32[]{:S(2)}, u32[]{:S(2)}) collective-permute-start(bf16[256,512]{1,0:T(8,128)(2,1)S(1)} %get-tuple-element.19), channel_id=1, source_target_pairs={{0,32},{32,64},{64,96},{96,128},{128,160},{160,192},{192,224},{224... | collective-permute-start | bytes 786440 | tf_op jit(solution)/shard_map/ppermute | solution.py:15
  19.4 10.0 %collective-permute-done = bf16[256,512]{1,0:T(8,128)(2,1)S(1)} collective-permute-done((bf16[256,512]{1,0:T(8,128)(2,1)S(1)}, bf16[256,512]{1,0:T(8,128)(2,1)S(1)}, u32[]{:S(2)}, u32[]{:S(2)}) %collective-permute-start) | collective-permute-done | bytes 262176 | tf_op jit(solution)/shard_map/ppermute | solution.py:15
  29.4 0.0 copy-done
  29.4 0.0 copy-start.3
  29.4 2.4 %fusion.10 = f32[512,1024]{0,1:T(8,128)S(1)} fusion(bf16[1024,1024]{1,0:T(8,128)(2,1)S(1)} %copy-done, bf16[512,512]{1,0:T(8,128)(2,1)} %bitcast.30, bf16[256,512]{1,0:T(8,128)(2,1)S(1)} %get-tuple-element.20, bf16[256,512]{1,0:T(8,128)(2,1)S(1)} %collective-permute-done), kind=kOutput, calls=%fused_computation.25 | convolution fusion | flops 1076887552 | bytes 5242880 | tf_op jit(solution)/shard_map/dot_general | solution.py:20
  31.8 0.0 copy-done.3
  31.8 0.0 copy-start.6
  31.8 1.4 %convolution_convert_fusion.1 = bf16[512,512]{1,0:T(8,128)(2,1)} fusion(f32[512,1024]{0,1:T(8,128)S(1)} %fusion.10, bf16[1,512,512]{2,1,0:T(8,128)(2,1)S(1)} %copy-done.3, f32[512]{0:T(512)S(1)} %fusion.11), kind=kOutput, calls=%fused_computation.2 | convolution fusion | flops 270270464 | bytes 3147776 | tf_op jit(solution)/shard_map/tk,tn->kn/dot_general | solution.py:291
  33.2 0.0 copy-done.6
  33.2 0.8 multiply_convert_fusion.2
  34.0 1.3 %fusion.3 = f32[512,1024]{1,0:T(8,128)S(1)} fusion(bf16[1024,1024]{1,0:T(8,128)(2,1)S(1)} %copy-done, bf16[512,512]{0,1:T(8,128)(2,1)S(1)} %get-tuple-element.18, bf16[512,512]{0,1:T(8,128)(2,1)S(1)} %get-tuple-element.17), kind=kOutput, calls=%fused_computation.13 | convolution fusion | flops 1075838976 | bytes 5242880 | tf_op jit(solution)/shard_map/dot_general | solution.py:289
  35.4 0.0 copy-start.1
  35.4 0.0 copy-start.2
  35.4 0.7 slice.95.edge_ref
  36.1 0.6 copy-done.1
  36.8 0.1 fusion.6
  36.9 0.0 copy-done.2
  36.9 2.6 %convolution_convert_fusion = bf16[1024,1024]{1,0:T(8,128)(2,1)} fusion(bf16[512,512]{0,1:T(8,128)(2,1)S(1)} %get-tuple-element.18, bf16[512,512]{0,1:T(8,128)(2,1)S(1)} %get-tuple-element.17, bf16[512,512]{1,0:T(8,128)(2,1)S(1)} %bitcast.31, bf16[256,512]{1,0:T(8,128)(2,1)S(1)} %get-tuple-element.20, bf16[256,512]{1,0:T(8,128)(2,1)S(1)} %collective-permute-done), kind=kOutput, calls=%fused_computation | convolution fusion | flops 1080033280 | bytes 4194304 | tf_op jit(solution)/shard_map/tk,tn->kn/dot_general | solution.py:290
  39.6 46.4 %shard_map.76 = (f32[32,64]{1,0:T(8,128)}, f32[16,32]{1,0:T(8,128)}, bf16[256,512]{1,0:T(8,128)(2,1)}) custom-call(bf16[4,2,2,64,1024]{4,3,2,1,0:T(8,128)(2,1)} %bitcast.29, bf16[4,2,2,32,512]{4,3,2,1,0:T(8,128)(2,1)} %bitcast.32, bf16[256,512]{1,0:T(8,128)(2,1)} %slice.95.edge_ref), custom_call_target="tpu_custom_call" | custom-call | tf_op jit(solution)/shard_map/pallas_call | solution.py:306
  86.0 0.0 copy-start.4
  86.0 0.0 copy-start.5
  86.0 1.2 %fusion.5 = bf16[256,512]{1,0:T(8,128)(2,1)S(1)} fusion(f32[512,1024]{1,0:T(8,128)} %copy-done.1, bf16[256,512]{1,0:T(8,128)(2,1)} %get-tuple-element.14, bf16[1,512,512]{2,1,0:T(8,128)(2,1)S(1)} %copy-done.3), kind=kLoop, calls=%fused_computation.16 | loop fusion | flops 655360 | bytes 1310720 | tf_op jit(solution)/shard_map/convert_element_type | solution.py:310
  87.2 0.8 maximum_bitcast_fusion
  88.1 0.0 copy-done.4
  88.1 0.6 copy.14
  88.7 0.0 copy-done.5
  88.7 0.6 copy.15
  (1 shorter events, 0.0 us)
Async XLA Ops:
  0.6 28.8 %copy-start = (bf16[1024,1024]{1,0:T(8,128)(2,1)S(1)}, bf16[1024,1024]{1,0:T(8,128)(2,1)}, u32[]{:S(2)}) copy-start(bf16[1024,1024]{1,0:T(8,128)(2,1)} %param.7) | copy-start | bytes 6291460
  1.9 27.5 %collective-permute-start = (bf16[256,512]{1,0:T(8,128)(2,1)S(1)}, bf16[256,512]{1,0:T(8,128)(2,1)S(1)}, u32[]{:S(2)}, u32[]{:S(2)}) collective-permute-start(bf16[256,512]{1,0:T(8,128)(2,1)S(1)} %get-tuple-element.19), channel_id=1, source_target_pairs={{0,32},{32,64},{64,96},{96,128},{128,160},{160,192},{192,224},{224... | collective-permute-start | bytes 786440 | tf_op jit(solution)/shard_map/ppermute | solution.py:15
  29.4 2.4 %copy-start.3 = (bf16[1,512,512]{2,1,0:T(8,128)(2,1)S(1)}, bf16[1,512,512]{2,1,0:T(8,128)(2,1)}, u32[]{:S(2)}) copy-start(bf16[1,512,512]{2,1,0:T(8,128)(2,1)} %param.6) | copy-start | bytes 1572868
  31.8 1.4 %copy-start.6 = (bf16[512,512]{1,0:T(8,128)(2,1)S(1)}, bf16[512,512]{1,0:T(8,128)(2,1)}, u32[]{:S(2)}) copy-start(bf16[512,512]{1,0:T(8,128)(2,1)} %param.8) | copy-start | bytes 1572868
  35.4 1.4 %copy-start.1 = (f32[512,1024]{1,0:T(8,128)}, f32[512,1024]{1,0:T(8,128)S(1)}, u32[]{:S(2)}) copy-start(f32[512,1024]{1,0:T(8,128)S(1)} %fusion.3) | copy-start | bytes 6291460
  35.4 1.6 %copy-start.2 = (bf16[1,512,512]{2,1,0:T(8,128)(2,1)S(1)}, bf16[1,512,512]{2,1,0:T(8,128)(2,1)}, u32[]{:S(2)}) copy-start(bf16[1,512,512]{2,1,0:T(8,128)(2,1)} %param.5) | copy-start | bytes 1572868
  86.0 2.1 %copy-start.4 = (f32[32,64]{1,0:T(8,128)S(1)}, f32[32,64]{1,0:T(8,128)}, u32[]{:S(2)}) copy-start(f32[32,64]{1,0:T(8,128)} %get-tuple-element.15) | copy-start | bytes 24580
  86.0 2.7 %copy-start.5 = (f32[16,32]{1,0:T(8,128)S(1)}, f32[16,32]{1,0:T(8,128)}, u32[]{:S(2)}) copy-start(f32[16,32]{1,0:T(8,128)} %get-tuple-element.16) | copy-start | bytes 6148

commit v11 on v10

--- a/solution.py
+++ b/solution.py
@@ -38,7 +38,8 @@
     base_xa, base_yb = 1, 1 + nx
     base_ya, base_xb = 1 + nx + ny, 1 + nx + 2 * ny
     base_z = 1 + 2 * nx + 2 * ny
-    n_slots = base_z + nz
+    n_slots = base_z + nz + 1
+    slot_cb = base_z + nz
     n_peers = (nc - 1) + (nx - 1) + (ny - 1) + (nz - 1) + 2
     n_tm = nx * nzh * nc
     mesh_id = pl.DeviceIdType.MESH
@@ -107,21 +108,35 @@
             recv_sem=local_sems.at[1, 2], device_id=before, device_id_type=mesh_id)
         edge.start()
 
-        send(0, conv_ref.at[:, :, pl.ds(other_c, 1)], rc_conv, 0, peers[0])
-        send(1, res_ref.at[:, :, pl.ds(other_c, 1)], rc_res, 0, peers[0])
-        arrive(0, conv_ref.at[:, :, pl.ds(other_c, 1)], rc_conv, 0)
-        arrive(1, res_ref.at[:, :, pl.ds(other_c, 1)], rc_res, 0)
-        for x in range(nx):
-            for zh in range(nzh):
-                own_c = conv_ref[x, zh, pl.ds(me_c, 1)][0].astype(jnp.float32)
-                sx_conv[x, zh] = (own_c + rc_conv[x, zh, 0].astype(jnp.float32)).astype(jnp.bfloat16)
-                own_r = res_ref[x, zh, pl.ds(me_c, 1)][0].astype(jnp.float32)
-                sx_res[x, zh] = (own_r + rc_res[x, zh, 0].astype(jnp.float32)).astype(jnp.bfloat16)
+        def pair_view(ref, lo, size):
+            return ref.at[:, :, pl.ds(other_c, 1), pl.ds(lo, size)]
+
+        def pair_slot(ref, lo, size):
+            return ref.at[:, :, :, pl.ds(lo, size)]
+
+        for lo_c, lo_r, slot in ((0, 0, 0), (hc, hr, slot_cb)):
+            send(0, pair_view(conv_ref, lo_c, hc), pair_slot(rc_conv, lo_c, hc), slot, peers[0])
+            send(1, pair_view(res_ref, lo_r, hr), pair_slot(rc_res, lo_r, hr), slot, peers[0])
+
+        def pair_sum(lo_c, lo_r, slot):
+            arrive(0, pair_view(conv_ref, lo_c, hc), pair_slot(rc_conv, lo_c, hc), slot)
+            arrive(1, pair_view(res_ref, lo_r, hr), pair_slot(rc_res, lo_r, hr), slot)
+            for x in range(nx):
+                for zh in range(nzh):
+                    own_c = conv_ref[x, zh, pl.ds(me_c, 1), pl.ds(lo_c, hc)][0].astype(jnp.float32)
+                    got_c = rc_conv[x, zh, 0, pl.ds(lo_c, hc)].astype(jnp.float32)
+                    sx_conv[x, zh, pl.ds(lo_c, hc)] = (own_c + got_c).astype(jnp.bfloat16)
+                    own_r = res_ref[x, zh, pl.ds(me_c, 1), pl.ds(lo_r, hr)][0].astype(jnp.float32)
+                    got_r = rc_res[x, zh, 0, pl.ds(lo_r, hr)].astype(jnp.float32)
+                    sx_res[x, zh, pl.ds(lo_r, hr)] = (own_r + got_r).astype(jnp.bfloat16)
+
+        pair_sum(0, 0, 0)
 
         for d in range(1, nx):
             tx = lax.rem(me_x + d, nx)
             send(0, sx_conv.at[tx, :, pl.ds(0, hc)], rxa_conv.at[me_x], base_xa + me_x, x_peers[d - 1])
             send(1, sx_res.at[tx, :, pl.ds(0, hr)], rxa_res.at[me_x], base_xa + me_x, x_peers[d - 1])
+        pair_sum(hc, hr, slot_cb)
         for d in range(1, ny):
             ty = lax.rem(me_y + d, ny)
             send(0, sx_conv.at[:, :, pl.ds(hc, hc), pl.ds(ty * cyc, cyc)], ryb_conv.at[me_y],
@@ -296,10 +311,10 @@
         edge_rows = input_gradient[:DILATION_STEP, :channel_count].astype(jnp.bfloat16)
         reducer = make_reducer(sizes, rc, n_conv, rr, n_res, float(all_tokens) ** (-0.5), edge_rows.shape)
         split = count_of_rows - DILATION_STEP
-        head_rows = (
-            cotangent[:split].astype(jnp.float32) + input_gradient[:split, channel_count:]
-            + input_gradient[DILATION_STEP:, :channel_count]
-        ).astype(jnp.bfloat16)
+        head_rows = jnp.concatenate([
+            (cotangent[:split].astype(jnp.float32) + input_gradient[:split, channel_count:]
+             + input_gradient[DILATION_STEP:, :channel_count]).astype(jnp.bfloat16),
+            jnp.zeros((count_of_rows - split, channel_count), jnp.bfloat16)], 0)
         conv_in = term_conv.astype(jnp.bfloat16).reshape(nx, nzh, nc, rc, n_conv)
         res_in = term_res.astype(jnp.bfloat16).reshape(nx, nzh, nc, rr, n_res)
         head_rows, conv_in, res_in, edge_rows = lax.optimization_barrier((head_rows, conv_in, res_in, edge_rows))
@@ -308,7 +323,7 @@
             cotangent[split:].astype(jnp.float32) + input_gradient[split:, channel_count:]
             + incoming_gradient.astype(jnp.float32)
         ).astype(jnp.bfloat16)
-        grad_rows = jnp.concatenate([head_rows, tail_rows], 0)
+        grad_rows = lax.dynamic_update_slice(head_rows, tail_rows, (split, 0))
         return (grad_rows[None], flip_conv.T, flip_res.T)
 
     return body

time: 89.5 us -> 90.5 us (1.011)
  local copies, waits for them, and re-layouts: 3.85 us -> 5.39 us
    unnamed x16 -> x18, local copies, waits for them, and re-layouts: 1.89 us -> 3.4 us
    dynamic_update_slice x0 -> x1, other arithmetic: none -> 1.23 us  [body(): grad_rows = lax.dynamic_update_slice(head_rows, tail_rows, (split, 0))]
    convert_element_type x2 -> x1, other arithmetic: 1.37 us -> 0.14 us  [body(): head_rows = jnp.concatenate([(cotangent[:split].astype(jnp.float32) + inp...]
where the time goes in v11:
time: 90.5 us; the launch traced here: 90.1 us
  Pallas kernels  46.4 us (51%)
  starting transfers between devices  16.8 us (19%)
  waiting for transfers between devices  10 us (11%)
  matrix products  8.62 us (10%)
  local copies, waits for them, and re-layouts  5.39 us (6%)
  between operations  1.42 us (2%)
  other arithmetic  1.37 us (2%)
    pallas_call x1, Pallas kernels, body(): flip_conv, flip_res, incoming_gradient = reducer(conv_in, res_in, edge_rows)  46.4 us
    ppermute x1, starting transfers between devices, passed_along(): return lax.ppermute(array, axis, pairs)  16.8 us
    ppermute x1, waiting for transfers between devices, passed_along(): return lax.ppermute(array, axis, pairs)  10 us
    unnamed x18, local copies, waits for them, and re-layouts  3.4 us
    dot_general x1, matrix products, body(): jnp.einsum('tk,tn->kn', inputs, pre_grad, preferred_element_type=jnp.floa...  2.62 us
    dot_general x1, matrix products, gate_backward(): pre_act = jnp.dot(inputs, w_conv, preferred_element_type=jnp.float32)  2.46 us
  transfers between devices with their start and end apart: 1, of which 1 were waited for; matrix products, arithmetic and copies ran while one was open for 0% of the time, Pallas kernels for 0%

profile of v11, /device:TPU:1, one launch (start us, length us, event | category | flops | bytes accessed | tf_op | source)
XLA Modules:
  0.0 90.1 jit_solution(8605027082373490528)
XLA Ops:
  0.6 0.0 copy-start
  0.6 1.2 %slice_bitcast_fusion.1 = (bf16[256,512]{1,0:T(8,128)(2,1)S(1)}, bf16[256,512]{1,0:T(8,128)(2,1)S(1)}) fusion(bf16[1,512,512]{2,1,0:T(8,128)(2,1)} %param.5), kind=kLoop, calls=%fused_computation.28 | loop fusion | bytes 1048576 | tf_op jit(solution)/shard_map/slice | solution.py:296
  1.9 16.8 %collective-permute-start = (bf16[256,512]{1,0:T(8,128)(2,1)S(1)}, bf16[256,512]{1,0:T(8,128)(2,1)S(1)}, u32[]{:S(2)}, u32[]{:S(2)}) collective-permute-start(bf16[256,512]{1,0:T(8,128)(2,1)S(1)} %get-tuple-element.19), channel_id=1, source_target_pairs={{0,32},{32,64},{64,96},{96,128},{128,160},{160,192},{192,224},{224... | collective-permute-start | bytes 786440 | tf_op jit(solution)/shard_map/ppermute | solution.py:15
  19.4 10.0 %collective-permute-done = bf16[256,512]{1,0:T(8,128)(2,1)S(1)} collective-permute-done((bf16[256,512]{1,0:T(8,128)(2,1)S(1)}, bf16[256,512]{1,0:T(8,128)(2,1)S(1)}, u32[]{:S(2)}, u32[]{:S(2)}) %collective-permute-start) | collective-permute-done | bytes 262176 | tf_op jit(solution)/shard_map/ppermute | solution.py:15
  29.4 0.0 copy-start.6
  29.4 0.0 copy-done
  29.4 0.0 copy-start.3
  29.4 2.5 %fusion.10 = f32[512,1024]{0,1:T(8,128)S(1)} fusion(bf16[1024,1024]{1,0:T(8,128)(2,1)S(1)} %copy-done, bf16[512,512]{1,0:T(8,128)(2,1)} %bitcast.33, bf16[256,512]{1,0:T(8,128)(2,1)S(1)} %get-tuple-element.20, bf16[256,512]{1,0:T(8,128)(2,1)S(1)} %collective-permute-done), kind=kOutput, calls=%fused_computation.24 | convolution fusion | flops 1076887552 | bytes 5242880 | tf_op jit(solution)/shard_map/dot_general | solution.py:20
  31.9 0.0 copy-done.6
  31.9 0.0 copy-done.3
  31.9 0.0 copy-start.5
  31.9 1.4 %convolution_convert_fusion.1 = bf16[512,512]{1,0:T(8,128)(2,1)} fusion(f32[512,1024]{0,1:T(8,128)S(1)} %fusion.10, bf16[1,512,512]{2,1,0:T(8,128)(2,1)S(1)} %copy-done.3, f32[512]{0:T(512)S(1)} %fusion.13), kind=kOutput, calls=%fused_computation.2 | convolution fusion | flops 270270464 | bytes 3147776 | tf_op jit(solution)/shard_map/tk,tn->kn/dot_general | solution.py:306
  33.3 0.0 copy-done.5
  33.3 0.8 multiply_convert_fusion.2
  34.1 1.3 %fusion.3 = f32[512,1024]{1,0:T(8,128)S(1)} fusion(bf16[1024,1024]{1,0:T(8,128)(2,1)S(1)} %copy-done, bf16[512,512]{0,1:T(8,128)(2,1)S(1)} %get-tuple-element.18, bf16[512,512]{0,1:T(8,128)(2,1)S(1)} %get-tuple-element.17), kind=kOutput, calls=%fused_computation.13 | convolution fusion | flops 1075838976 | bytes 5242880 | tf_op jit(solution)/shard_map/dot_general | solution.py:304
  35.4 0.0 copy-start.1
  35.4 0.0 copy-start.2
  35.5 0.0 copy-start.7
  35.5 0.7 slice.99.edge_ref
  36.2 0.6 copy-done.1
  36.9 0.1 fusion.6
  37.0 0.0 copy-done.2
  37.1 0.1 copy-done.7
  37.1 2.6 %convolution_convert_fusion = bf16[1024,1024]{1,0:T(8,128)(2,1)} fusion(bf16[512,512]{0,1:T(8,128)(2,1)S(1)} %get-tuple-element.18, bf16[512,512]{0,1:T(8,128)(2,1)S(1)} %get-tuple-element.17, bf16[512,512]{1,0:T(8,128)(2,1)S(1)} %bitcast.34, bf16[256,512]{1,0:T(8,128)(2,1)S(1)} %get-tuple-element.20, bf16[256,512]{1,0:T(8,128)(2,1)S(1)} %copy-done.7), kind=kOutput, calls=%fused_computation | convolution fusion | flops 1080033280 | bytes 4194304 | tf_op jit(solution)/shard_map/tk,tn->kn/dot_general | solution.py:305
  39.7 46.4 %shard_map.76 = (f32[32,64]{1,0:T(8,128)}, f32[16,32]{1,0:T(8,128)}, bf16[256,512]{1,0:T(8,128)(2,1)}) custom-call(bf16[4,2,2,64,1024]{4,3,2,1,0:T(8,128)(2,1)} %bitcast.32, bf16[4,2,2,32,512]{4,3,2,1,0:T(8,128)(2,1)} %bitcast.36, bf16[256,512]{1,0:T(8,128)(2,1)} %slice.99.edge_ref), custom_call_target="tpu_custom_call" | custom-call | tf_op jit(solution)/shard_map/pallas_call | solution.py:321
  86.2 1.2 %fusion.12 = bf16[1,512,512]{2,1,0:T(8,128)(2,1)S(1)} fusion(bf16[1,512,512]{2,1,0:T(8,128)(2,1)S(1)} %bitcast.35, bf16[256,512]{1,0:T(8,128)(2,1)} %get-tuple-element.14, f32[512,1024]{1,0:T(8,128)} %copy-done.1, bf16[1,512,512]{2,1,0:T(8,128)(2,1)S(1)} %copy-done.3), kind=kLoop, calls=%fused_computation.26 | loop fusion | flops 655360 | bytes 1310720 | tf_op jit(solution)/shard_map/dynamic_update_slice | solution.py:326
  87.4 0.0 copy-start.4
  87.4 1.3 %copy.15 = f32[64,32]{0,1:T(8,128)} copy(f32[64,32]{0,1:T(8,128)} %bitcast.37) | data formatting | bytes 16384
  88.8 1.3 %copy.16 = f32[32,16]{0,1:T(8,128)} copy(f32[32,16]{0,1:T(8,128)} %bitcast.38) | data formatting | bytes 4096
  90.1 0.0 copy-done.4
  (2 shorter events, 0.0 us)
Async XLA Ops:
  0.6 28.8 %copy-start = (bf16[1024,1024]{1,0:T(8,128)(2,1)S(1)}, bf16[1024,1024]{1,0:T(8,128)(2,1)}, u32[]{:S(2)}) copy-start(bf16[1024,1024]{1,0:T(8,128)(2,1)} %param.7) | copy-start | bytes 6291460
  1.9 27.5 %collective-permute-start = (bf16[256,512]{1,0:T(8,128)(2,1)S(1)}, bf16[256,512]{1,0:T(8,128)(2,1)S(1)}, u32[]{:S(2)}, u32[]{:S(2)}) collective-permute-start(bf16[256,512]{1,0:T(8,128)(2,1)S(1)} %get-tuple-element.19), channel_id=1, source_target_pairs={{0,32},{32,64},{64,96},{96,128},{128,160},{160,192},{192,224},{224... | collective-permute-start | bytes 786440 | tf_op jit(solution)/shard_map/ppermute | solution.py:15
  29.4 2.5 %copy-start.6 = (bf16[256,512]{1,0:T(8,128)(2,1)}, bf16[256,512]{1,0:T(8,128)(2,1)S(1)}, u32[]{:S(2)}) copy-start(bf16[256,512]{1,0:T(8,128)(2,1)S(1)} %collective-permute-done) | copy-start | bytes 786436
  29.4 2.5 %copy-start.3 = (bf16[1,512,512]{2,1,0:T(8,128)(2,1)S(1)}, bf16[1,512,512]{2,1,0:T(8,128)(2,1)}, u32[]{:S(2)}) copy-start(bf16[1,512,512]{2,1,0:T(8,128)(2,1)} %param.6) | copy-start | bytes 1572868
  31.9 1.4 %copy-start.5 = (bf16[512,512]{1,0:T(8,128)(2,1)S(1)}, bf16[512,512]{1,0:T(8,128)(2,1)}, u32[]{:S(2)}) copy-start(bf16[512,512]{1,0:T(8,128)(2,1)} %param.8) | copy-start | bytes 1572868
  35.4 1.4 %copy-start.1 = (f32[512,1024]{1,0:T(8,128)}, f32[512,1024]{1,0:T(8,128)S(1)}, u32[]{:S(2)}) copy-start(f32[512,1024]{1,0:T(8,128)S(1)} %fusion.3) | copy-start | bytes 6291460
  35.4 1.6 %copy-start.2 = (bf16[1,512,512]{2,1,0:T(8,128)(2,1)S(1)}, bf16[1,512,512]{2,1,0:T(8,128)(2,1)}, u32[]{:S(2)}) copy-start(bf16[1,512,512]{2,1,0:T(8,128)(2,1)} %param.5) | copy-start | bytes 1572868
  35.5 1.7 %copy-start.7 = (bf16[256,512]{1,0:T(8,128)(2,1)S(1)}, bf16[256,512]{1,0:T(8,128)(2,1)}, u32[]{:S(2)}) copy-start(bf16[256,512]{1,0:T(8,128)(2,1)} %copy-done.6) | copy-start | bytes 786436
  87.4 2.7 %copy-start.4 = (bf16[1,512,512]{2,1,0:T(8,128)(2,1)}, bf16[1,512,512]{2,1,0:T(8,128)(2,1)S(1)}, u32[]{:S(2)}) copy-start(bf16[1,512,512]{2,1,0:T(8,128)(2,1)S(1)} %fusion.12) | copy-start | bytes 1572868

commit v12 on v6

--- a/solution.py
+++ b/solution.py
@@ -38,8 +38,11 @@
     base_xa, base_yb = 1, 1 + nx
     base_ya, base_xb = 1 + nx + ny, 1 + nx + 2 * ny
     base_z = 1 + 2 * nx + 2 * ny
-    n_slots = base_z + nz
-    n_peers = (nc - 1) + (nx - 1) + (ny - 1) + (nz - 1)
+    n_cw, n_ccw = nz // 2 - 1, nz // 2
+    base_ccw = base_z + n_cw
+    n_slots = base_ccw + n_ccw
+    n_peers = (nc - 1) + (nx - 1) + (ny - 1) + 2
+    n_tm = nx * nzh * nc
     mesh_id = pl.DeviceIdType.MESH
 
     def kernel(conv_ref, res_ref, conv_out, res_out,
@@ -47,8 +50,8 @@
                rxa_conv, rxa_res, ryb_conv, ryb_res,
                sa_conv, sa_res, rya_conv, rya_res,
                sb_conv, sb_res, rxb_conv, rxb_res,
-               sz_conv, sz_res, rz_conv, rz_res,
-               send_sems, recv_sems, local_sems):
+               sz_conv, sz_res, cw_in_c, cw_in_r, cw_out_c, cw_out_r,
+               ccw_in_c, ccw_in_r, ccw_out_c, ccw_out_r, send_sems, recv_sems, local_sems):
         me_x = lax.axis_index("x")
         me_zh = lax.axis_index("zh")
         me_c = lax.axis_index("c")
@@ -65,10 +68,9 @@
         peers = [dev(c=other_c)]
         x_peers = [dev(x=lax.rem(me_x + d, nx)) for d in range(1, nx)]
         y_peers = [dev(y=lax.rem(me_y + d, ny)) for d in range(1, ny)]
-        z_peers = []
-        for d in range(1, nz):
-            q = lax.rem(me_z + d, nz)
-            z_peers.append(dev(zh=q // nzl, zl=lax.rem(q, nzl)))
+        right = dev(zh=lax.rem(me_z + 1, nz) // nzl, zl=lax.rem(lax.rem(me_z + 1, nz), nzl))
+        left = dev(zh=lax.rem(me_z + nz - 1, nz) // nzl, zl=lax.rem(lax.rem(me_z + nz - 1, nz), nzl))
+        z_peers = [right, left]
         barrier = pltpu.get_barrier_semaphore()
         for peer in peers + x_peers + y_peers + z_peers:
             pl.semaphore_signal(barrier, inc=1, device_id=peer, device_id_type=mesh_id)
@@ -182,23 +184,31 @@
             flip_c = acc_c[zh].T
             flip_r = acc_r[zh].T
             for zl in range(nzl):
-                sz_conv[zh * nzl + zl] = flip_c[zl * cc:(zl + 1) * cc, :].astype(jnp.bfloat16)
-                sz_res[zh * nzl + zl] = flip_r[zl * cr:(zl + 1) * cr, :].astype(jnp.bfloat16)
-
-        for d in range(1, nz):
-            tz = lax.rem(me_z + d, nz)
-            send(0, sz_conv.at[tz], rz_conv.at[me_z], base_z + me_z, z_peers[d - 1])
-            send(1, sz_res.at[tz], rz_res.at[me_z], base_z + me_z, z_peers[d - 1])
-        for d in range(1, nz):
-            sz = lax.rem(me_z + nz - d, nz)
-            arrive(0, sz_conv.at[sz], rz_conv.at[sz], base_z + sz)
-            arrive(1, sz_res.at[sz], rz_res.at[sz], base_z + sz)
-        acc_c = sz_conv[me_z].astype(jnp.float32)
-        acc_r = sz_res[me_z].astype(jnp.float32)
-        for d in range(1, nz):
-            sz = lax.rem(me_z + nz - d, nz)
-            acc_c = acc_c + rz_conv[sz].astype(jnp.float32)
-            acc_r = acc_r + rz_res[sz].astype(jnp.float32)
+                sz_conv[zh * nzl + zl] = flip_c[zl * cc:(zl + 1) * cc, :]
+                sz_res[zh * nzl + zl] = flip_r[zl * cr:(zl + 1) * cr, :]
+
+        chains = ((n_cw, 1, base_z, right, cw_in_c, cw_in_r, cw_out_c, cw_out_r),
+                  (n_ccw, -1, base_ccw, left, ccw_in_c, ccw_in_r, ccw_out_c, ccw_out_r))
+        for s in range(n_ccw):
+            for steps, sign, base, peer, in_c, in_r, out_c, out_r in chains:
+                if s >= steps:
+                    continue
+                q = lax.rem(me_z + nz + sign * (steps - s), nz)
+                if s == 0:
+                    src_c, src_r = sz_conv.at[q], sz_res.at[q]
+                else:
+                    arrive(0, sz_conv.at[q], in_c.at[s - 1], base + s - 1)
+                    arrive(1, sz_res.at[q], in_r.at[s - 1], base + s - 1)
+                    out_c[s] = sz_conv[q] + in_c[s - 1]
+                    out_r[s] = sz_res[q] + in_r[s - 1]
+                    src_c, src_r = out_c.at[s], out_r.at[s]
+                send(0, src_c, in_c.at[s], base + s, peer)
+                send(1, src_r, in_r.at[s], base + s, peer)
+        for steps, sign, base, peer, in_c, in_r, out_c, out_r in chains:
+            arrive(0, sz_conv.at[me_z], in_c.at[steps - 1], base + steps - 1)
+            arrive(1, sz_res.at[me_z], in_r.at[steps - 1], base + steps - 1)
+        acc_c = sz_conv[me_z] + cw_in_c[n_cw - 1] + ccw_in_c[n_ccw - 1]
+        acc_r = sz_res[me_z] + cw_in_r[n_cw - 1] + ccw_in_r[n_ccw - 1]
         conv_out[...] = acc_c * scale
         res_out[...] = acc_r * scale
         for copy in sends:
@@ -228,13 +238,19 @@
             pltpu.VMEM((nx, nzh, hr, cyr), bf16),
             pltpu.VMEM((nx, nzh, hc, cyc), bf16),
             pltpu.VMEM((nx, nzh, hr, cyr), bf16),
-            pltpu.VMEM((nz, cc, rc), bf16),
-            pltpu.VMEM((nz, cr, rr), bf16),
-            pltpu.VMEM((nz, cc, rc), bf16),
-            pltpu.VMEM((nz, cr, rr), bf16),
+            pltpu.VMEM((nz, cc, rc), f32),
+            pltpu.VMEM((nz, cr, rr), f32),
+            pltpu.VMEM((n_cw, cc, rc), f32),
+            pltpu.VMEM((n_cw, cr, rr), f32),
+            pltpu.VMEM((n_cw, cc, rc), f32),
+            pltpu.VMEM((n_cw, cr, rr), f32),
+            pltpu.VMEM((n_ccw, cc, rc), f32),
+            pltpu.VMEM((n_ccw, cr, rr), f32),
+            pltpu.VMEM((n_ccw, cc, rc), f32),
+            pltpu.VMEM((n_ccw, cr, rr), f32),
             pltpu.SemaphoreType.DMA((2, n_slots)),
             pltpu.SemaphoreType.DMA((2, n_slots)),
-            pltpu.SemaphoreType.DMA((2, 2)),
+            pltpu.SemaphoreType.DMA((2, 3)),
         ],
         compiler_params=pltpu.CompilerParams(collective_id=0, has_side_effects=True),
     )
@@ -261,26 +277,30 @@
         in_length = (start_row + jnp.arange(count_of_rows) < seq_len).astype(jnp.float32)[:, None]
         gated, pre_grad = gate_backward(inputs, cotangent, in_length, w_conv, w_res)
         input_gradient = jnp.dot(pre_grad, w_conv.T, preferred_element_type=jnp.float32)
-        incoming_gradient = passed_along(
-            input_gradient[:DILATION_STEP, :channel_count].astype(jnp.bfloat16), TM, -1, n_tm
-        ).astype(jnp.float32)
-        delayed_gradient = jnp.concatenate(
-            [input_gradient[DILATION_STEP:, :channel_count], incoming_gradient], 0
-        )
-        grad_rows = (
-            cotangent.astype(jnp.float32) + input_gradient[:, channel_count:] + delayed_gradient
-        ).astype(jnp.bfloat16)
         term_conv = jnp.einsum("tk,tn->kn", inputs, pre_grad, preferred_element_type=jnp.float32)
         term_res = jnp.einsum("tk,tn->kn", gated, cotangent, preferred_element_type=jnp.float32)
         kc, n_conv = term_conv.shape
         kr, n_res = term_res.shape
         rc, rr = kc // n_tm, kr // n_tm
         all_tokens = count_of_rows * n_tm * n_rep
+        incoming_gradient = passed_along(
+            input_gradient[:DILATION_STEP, :channel_count].astype(jnp.bfloat16), TM, -1, n_tm
+        )
         reducer = make_reducer(sizes, rc, n_conv, rr, n_res, float(all_tokens) ** (-0.5))
-        flip_conv, flip_res = reducer(
-            term_conv.astype(jnp.bfloat16).reshape(nx, nzh, nc, rc, n_conv),
-            term_res.astype(jnp.bfloat16).reshape(nx, nzh, nc, rr, n_res),
-        )
+        split = count_of_rows - DILATION_STEP
+        head_rows = (
+            cotangent[:split].astype(jnp.float32) + input_gradient[:split, channel_count:]
+            + input_gradient[DILATION_STEP:, :channel_count]
+        ).astype(jnp.bfloat16)
+        conv_in = term_conv.astype(jnp.bfloat16).reshape(nx, nzh, nc, rc, n_conv)
+        res_in = term_res.astype(jnp.bfloat16).reshape(nx, nzh, nc, rr, n_res)
+        head_rows, conv_in, res_in = lax.optimization_barrier((head_rows, conv_in, res_in))
+        flip_conv, flip_res = reducer(conv_in, res_in)
+        tail_rows = (
+            cotangent[split:].astype(jnp.float32) + input_gradient[split:, channel_count:]
+            + incoming_gradient.astype(jnp.float32)
+        ).astype(jnp.bfloat16)
+        grad_rows = jnp.concatenate([head_rows, tail_rows], 0)
         return (grad_rows[None], flip_conv.T, flip_res.T)
 
     return body

time: 91.1 us -> 112 us (1.23)
  the two profiles are of different devices: /device:TPU:1 before, /device:TPU:32 now
where the time goes in v12:
time: 112 us; the launch traced here: 111 us
  Pallas kernels  71.3 us (64%)
  waiting for transfers between devices  21.8 us (19%)
  matrix products  8.6 us (8%)
  local copies, waits for them, and re-layouts  3.89 us (3%)
  starting transfers between devices  3.05 us (3%)
  between operations  1.39 us (1%)
    pallas_call x1, Pallas kernels, body(): flip_conv, flip_res = reducer(conv_in, res_in)  71.3 us
    ppermute x2, waiting for transfers between devices, passed_along(): return lax.ppermute(array, axis, pairs)  21.8 us
    ppermute x2, starting transfers between devices, passed_along(): return lax.ppermute(array, axis, pairs)  3.05 us
    dot_general x1, matrix products, body(): jnp.einsum('tk,tn->kn', inputs, pre_grad, preferred_element_type=jnp.floa...  2.65 us
    unnamed x10, local copies, waits for them, and re-layouts  2.64 us
    dot_general x1, matrix products, gate_backward(): pre_act = jnp.dot(inputs, w_conv, preferred_element_type=jnp.float32)  2.42 us
  transfers between devices with their start and end apart: 2, of which 2 were waited for; matrix products, arithmetic and copies ran while one was open for 4% of the time, Pallas kernels for 0%

profile of v12, /device:TPU:32, one launch (start us, length us, event | category | flops | bytes accessed | tf_op | source)
XLA Modules:
  0.0 111.1 jit_solution(4070295218264808121)
XLA Ops:
  0.6 0.0 copy-start
  0.6 1.2 %slice_bitcast_fusion.1 = (bf16[256,512]{1,0:T(8,128)(2,1)S(1)}, bf16[256,512]{1,0:T(8,128)(2,1)S(1)}) fusion(bf16[1,512,512]{2,1,0:T(8,128)(2,1)} %param.5), kind=kLoop, calls=%fused_computation.27 | loop fusion | bytes 1048576 | tf_op jit(solution)/shard_map/slice | solution.py:271
  1.9 1.8 %collective-permute-start = (bf16[256,512]{1,0:T(8,128)(2,1)S(1)}, bf16[256,512]{1,0:T(8,128)(2,1)S(1)}, u32[]{:S(2)}, u32[]{:S(2)}) collective-permute-start(bf16[256,512]{1,0:T(8,128)(2,1)S(1)} %get-tuple-element.17), channel_id=1, source_target_pairs={{0,32},{32,64},{64,96},{96,128},{128,160},{160,192},{192,224},{224... | collective-permute-start | bytes 786440 | tf_op jit(solution)/shard_map/ppermute | solution.py:15
  4.3 0.5 collective-permute-done
  4.8 0.0 copy-done
  4.8 0.0 copy-start.2
  4.8 0.0 copy-start.3
  4.8 2.4 %fusion.10 = f32[512,1024]{0,1:T(8,128)S(1)} fusion(bf16[1024,1024]{1,0:T(8,128)(2,1)S(1)} %copy-done, bf16[512,512]{1,0:T(8,128)(2,1)} %bitcast.31, bf16[256,512]{1,0:T(8,128)(2,1)S(1)} %get-tuple-element.18, bf16[256,512]{1,0:T(8,128)(2,1)S(1)} %collective-permute-done), kind=kOutput, calls=%fused_computation.25 | convolution fusion | flops 1076887552 | bytes 5242880 | tf_op jit(solution)/shard_map/dot_general | solution.py:20
  7.2 0.0 copy-done.2
  7.2 0.0 copy-done.3
  7.2 0.9 multiply_convert_fusion.2
  8.1 0.0 copy-start.1
  8.1 1.3 %fusion.3 = f32[512,1024]{1,0:T(8,128)S(1)} fusion(bf16[1024,1024]{1,0:T(8,128)(2,1)S(1)} %copy-done, bf16[512,512]{0,1:T(8,128)(2,1)S(1)} %get-tuple-element.14, bf16[512,512]{0,1:T(8,128)(2,1)S(1)} %get-tuple-element.13), kind=kOutput, calls=%fused_computation.13 | convolution fusion | flops 1075838976 | bytes 5242880 | tf_op jit(solution)/shard_map/dot_general | solution.py:279
  9.4 1.3 %collective-permute-start.1 = (bf16[256,512]{1,0:T(8,128)(2,1)S(1)}, bf16[256,512]{1,0:T(8,128)(2,1)S(1)}, u32[]{:S(2)}, u32[]{:S(2)}) collective-permute-start(bf16[256,512]{1,0:T(8,128)(2,1)S(1)} %slice.95), channel_id=1, source_target_pairs={{32,0},{64,32},{96,64},{128,96},{160,128},{192,160},{224,192},{256... | collective-permute-start | bytes 786440 | tf_op jit(solution)/shard_map/ppermute | solution.py:15
  10.7 0.0 copy-done.1
  10.7 2.6 %convolution_convert_fusion = bf16[1024,1024]{1,0:T(8,128)(2,1)} fusion(bf16[512,512]{0,1:T(8,128)(2,1)S(1)} %get-tuple-element.14, bf16[512,512]{0,1:T(8,128)(2,1)S(1)} %get-tuple-element.13, bf16[512,512]{1,0:T(8,128)(2,1)S(1)} %bitcast.32, bf16[256,512]{1,0:T(8,128)(2,1)S(1)} %get-tuple-element.18, bf16[256,512]{1,0:T(8,128)(2,1)S(1)} %collective-permute-done), kind=kOutput, calls=%fused_computation | convolution fusion | flops 1080033280 | bytes 4194304 | tf_op jit(solution)/shard_map/tk,tn->kn/dot_general | solution.py:280
  13.4 1.4 %convolution_convert_fusion.1 = bf16[512,512]{1,0:T(8,128)(2,1)} fusion(f32[512,1024]{0,1:T(8,128)S(1)} %fusion.10, bf16[1,512,512]{2,1,0:T(8,128)(2,1)S(1)} %copy-done.2, f32[512]{0:T(512)S(1)} %fusion.11), kind=kOutput, calls=%fused_computation.2 | convolution fusion | flops 270270464 | bytes 3147776 | tf_op jit(solution)/shard_map/tk,tn->kn/dot_general | solution.py:281
  14.8 21.4 %collective-permute-done.1 = bf16[256,512]{1,0:T(8,128)(2,1)S(1)} collective-permute-done((bf16[256,512]{1,0:T(8,128)(2,1)S(1)}, bf16[256,512]{1,0:T(8,128)(2,1)S(1)}, u32[]{:S(2)}, u32[]{:S(2)}) %collective-permute-start.1) | collective-permute-done | bytes 262176 | tf_op jit(solution)/shard_map/ppermute | solution.py:15
  36.1 0.3 fusion.6
  36.4 71.3 %shard_map.76 = (f32[32,64]{1,0:T(8,128)}, f32[16,32]{1,0:T(8,128)}) custom-call(bf16[4,2,2,64,1024]{4,3,2,1,0:T(8,128)(2,1)} %bitcast.29, bf16[4,2,2,32,512]{4,3,2,1,0:T(8,128)(2,1)} %bitcast.30), custom_call_target="tpu_custom_call" | custom-call | tf_op jit(solution)/shard_map/pallas_call | solution.py:298
  107.7 0.8 maximum_bitcast_fusion
  108.5 1.3 %copy.14 = f32[64,32]{0,1:T(8,128)} copy(f32[64,32]{0,1:T(8,128)} %bitcast.33) | data formatting | bytes 16384
  109.8 1.3 %copy.15 = f32[32,16]{0,1:T(8,128)} copy(f32[32,16]{0,1:T(8,128)} %bitcast.34) | data formatting | bytes 4096
  (2 shorter events, 0.0 us)
Async XLA Ops:
  0.6 4.1 %copy-start = (bf16[1024,1024]{1,0:T(8,128)(2,1)S(1)}, bf16[1024,1024]{1,0:T(8,128)(2,1)}, u32[]{:S(2)}) copy-start(bf16[1024,1024]{1,0:T(8,128)(2,1)} %param.7) | copy-start | bytes 6291460
  1.9 2.9 %collective-permute-start = (bf16[256,512]{1,0:T(8,128)(2,1)S(1)}, bf16[256,512]{1,0:T(8,128)(2,1)S(1)}, u32[]{:S(2)}, u32[]{:S(2)}) collective-permute-start(bf16[256,512]{1,0:T(8,128)(2,1)S(1)} %get-tuple-element.17), channel_id=1, source_target_pairs={{0,32},{32,64},{64,96},{96,128},{128,160},{160,192},{192,224},{224... | collective-permute-start | bytes 786440 | tf_op jit(solution)/shard_map/ppermute | solution.py:15
  4.8 2.4 %copy-start.2 = (bf16[1,512,512]{2,1,0:T(8,128)(2,1)S(1)}, bf16[1,512,512]{2,1,0:T(8,128)(2,1)}, u32[]{:S(2)}) copy-start(bf16[1,512,512]{2,1,0:T(8,128)(2,1)} %param.6) | copy-start | bytes 1572868
  4.8 2.4 %copy-start.3 = (bf16[512,512]{1,0:T(8,128)(2,1)S(1)}, bf16[512,512]{1,0:T(8,128)(2,1)}, u32[]{:S(2)}) copy-start(bf16[512,512]{1,0:T(8,128)(2,1)} %param.8) | copy-start | bytes 1572868
  8.1 2.7 %copy-start.1 = (bf16[1,512,512]{2,1,0:T(8,128)(2,1)S(1)}, bf16[1,512,512]{2,1,0:T(8,128)(2,1)}, u32[]{:S(2)}) copy-start(bf16[1,512,512]{2,1,0:T(8,128)(2,1)} %param.5) | copy-start | bytes 1572868
  9.4 26.7 %collective-permute-start.1 = (bf16[256,512]{1,0:T(8,128)(2,1)S(1)}, bf16[256,512]{1,0:T(8,128)(2,1)S(1)}, u32[]{:S(2)}, u32[]{:S(2)}) collective-permute-start(bf16[256,512]{1,0:T(8,128)(2,1)S(1)} %slice.95), channel_id=1, source_target_pairs={{32,0},{64,32},{96,64},{128,96},{160,128},{192,160},{224,192},{256... | collective-permute-start | bytes 786440 | tf_op jit(solution)/shard_map/ppermute | solution.py:15

commit v13 on v10

--- a/solution.py
+++ b/solution.py
@@ -48,7 +48,7 @@
                rxa_conv, rxa_res, ryb_conv, ryb_res,
                sa_conv, sa_res, rya_conv, rya_res,
                sb_conv, sb_res, rxb_conv, rxb_res,
-               sz_conv, sz_res, rz_conv, rz_res,
+               sz_both, rz_both,
                edge_buf, send_sems, recv_sems, local_sems):
         me_x = lax.axis_index("x")
         me_zh = lax.axis_index("zh")
@@ -195,25 +195,23 @@
             flip_c = acc_c[zh].T
             flip_r = acc_r[zh].T
             for zl in range(nzl):
-                sz_conv[zh * nzl + zl] = flip_c[zl * cc:(zl + 1) * cc, :].astype(jnp.bfloat16)
-                sz_res[zh * nzl + zl] = flip_r[zl * cr:(zl + 1) * cr, :].astype(jnp.bfloat16)
+                q = zh * nzl + zl
+                sz_both[q, :cc, :] = flip_c[zl * cc:(zl + 1) * cc, :].astype(jnp.bfloat16)
+                sz_both[q, cc:, :rr] = flip_r[zl * cr:(zl + 1) * cr, :].astype(jnp.bfloat16)
+                sz_both[q, cc:, rr:] = jnp.zeros((cr, rc - rr), jnp.bfloat16)
 
         for d in range(1, nz):
             tz = lax.rem(me_z + d, nz)
-            send(0, sz_conv.at[tz], rz_conv.at[me_z], base_z + me_z, z_peers[d - 1])
-            send(1, sz_res.at[tz], rz_res.at[me_z], base_z + me_z, z_peers[d - 1])
+            send(0, sz_both.at[tz], rz_both.at[me_z], base_z + me_z, z_peers[d - 1])
         for d in range(1, nz):
             sz = lax.rem(me_z + nz - d, nz)
-            arrive(0, sz_conv.at[sz], rz_conv.at[sz], base_z + sz)
-            arrive(1, sz_res.at[sz], rz_res.at[sz], base_z + sz)
-        acc_c = sz_conv[me_z].astype(jnp.float32)
-        acc_r = sz_res[me_z].astype(jnp.float32)
+            arrive(0, sz_both.at[sz], rz_both.at[sz], base_z + sz)
+        acc = sz_both[me_z].astype(jnp.float32)
         for d in range(1, nz):
             sz = lax.rem(me_z + nz - d, nz)
-            acc_c = acc_c + rz_conv[sz].astype(jnp.float32)
-            acc_r = acc_r + rz_res[sz].astype(jnp.float32)
-        conv_out[...] = acc_c * scale
-        res_out[...] = acc_r * scale
+            acc = acc + rz_both[sz].astype(jnp.float32)
+        conv_out[...] = acc[:cc] * scale
+        res_out[...] = acc[cc:, :rr] * scale
         edge.wait_recv()
 
         @pl.when(t < n_tm - 1)
@@ -253,10 +251,8 @@
             pltpu.VMEM((nx, nzh, hr, cyr), bf16),
             pltpu.VMEM((nx, nzh, hc, cyc), bf16),
             pltpu.VMEM((nx, nzh, hr, cyr), bf16),
-            pltpu.VMEM((nz, cc, rc), bf16),
-            pltpu.VMEM((nz, cr, rr), bf16),
-            pltpu.VMEM((nz, cc, rc), bf16),
-            pltpu.VMEM((nz, cr, rr), bf16),
+            pltpu.VMEM((nz, cc + cr, rc), bf16),
+            pltpu.VMEM((nz, cc + cr, rc), bf16),
             pltpu.VMEM(edge_shape, bf16),
             pltpu.SemaphoreType.DMA((2, n_slots)),
             pltpu.SemaphoreType.DMA((2, n_slots)),

time: 89.5 us -> 89.5 us (level)
  no operation moved by 1% of the time
where the time goes in v13:
time: 89.5 us; the launch traced here: 89.2 us
  Pallas kernels  46.4 us (52%)
  starting transfers between devices  16.8 us (19%)
  waiting for transfers between devices  10 us (11%)
  matrix products  8.57 us (10%)
  local copies, waits for them, and re-layouts  3.85 us (4%)
  other arithmetic  2.2 us (2%)
  between operations  1.4 us (2%)
    pallas_call x1, Pallas kernels, body(): flip_conv, flip_res, incoming_gradient = reducer(conv_in, res_in, edge_rows)  46.4 us
    ppermute x1, starting transfers between devices, passed_along(): return lax.ppermute(array, axis, pairs)  16.8 us
    ppermute x1, waiting for transfers between devices, passed_along(): return lax.ppermute(array, axis, pairs)  10 us
    dot_general x1, matrix products, body(): jnp.einsum('tk,tn->kn', inputs, pre_grad, preferred_element_type=jnp.floa...  2.63 us
    dot_general x1, matrix products, gate_backward(): pre_act = jnp.dot(inputs, w_conv, preferred_element_type=jnp.float32)  2.39 us
    unnamed x16, local copies, waits for them, and re-layouts  1.89 us
  transfers between devices with their start and end apart: 1, of which 1 were waited for; matrix products, arithmetic and copies ran while one was open for 0% of the time, Pallas kernels for 0%

profile of v13, /device:TPU:1, one launch (start us, length us, event | category | flops | bytes accessed | tf_op | source)
XLA Modules:
  0.0 89.2 jit_solution(14711916160419079993)
XLA Ops:
  0.6 0.0 copy-start
  0.6 1.2 %slice_bitcast_fusion.1 = (bf16[256,512]{1,0:T(8,128)(2,1)S(1)}, bf16[256,512]{1,0:T(8,128)(2,1)S(1)}) fusion(bf16[1,512,512]{2,1,0:T(8,128)(2,1)} %param.5), kind=kLoop, calls=%fused_computation.27 | loop fusion | bytes 1048576 | tf_op jit(solution)/shard_map/slice | solution.py:277
  1.9 16.8 %collective-permute-start = (bf16[256,512]{1,0:T(8,128)(2,1)S(1)}, bf16[256,512]{1,0:T(8,128)(2,1)S(1)}, u32[]{:S(2)}, u32[]{:S(2)}) collective-permute-start(bf16[256,512]{1,0:T(8,128)(2,1)S(1)} %get-tuple-element.19), channel_id=1, source_target_pairs={{0,32},{32,64},{64,96},{96,128},{128,160},{160,192},{192,224},{224... | collective-permute-start | bytes 786440 | tf_op jit(solution)/shard_map/ppermute | solution.py:15
  19.4 10.0 %collective-permute-done = bf16[256,512]{1,0:T(8,128)(2,1)S(1)} collective-permute-done((bf16[256,512]{1,0:T(8,128)(2,1)S(1)}, bf16[256,512]{1,0:T(8,128)(2,1)S(1)}, u32[]{:S(2)}, u32[]{:S(2)}) %collective-permute-start) | collective-permute-done | bytes 262176 | tf_op jit(solution)/shard_map/ppermute | solution.py:15
  29.4 0.0 copy-done
  29.4 0.0 copy-start.3
  29.4 2.4 %fusion.10 = f32[512,1024]{0,1:T(8,128)S(1)} fusion(bf16[1024,1024]{1,0:T(8,128)(2,1)S(1)} %copy-done, bf16[512,512]{1,0:T(8,128)(2,1)} %bitcast.30, bf16[256,512]{1,0:T(8,128)(2,1)S(1)} %get-tuple-element.20, bf16[256,512]{1,0:T(8,128)(2,1)S(1)} %collective-permute-done), kind=kOutput, calls=%fused_computation.25 | convolution fusion | flops 1076887552 | bytes 5242880 | tf_op jit(solution)/shard_map/dot_general | solution.py:20
  31.8 0.0 copy-done.3
  31.8 0.0 copy-start.6
  31.8 1.4 %convolution_convert_fusion.1 = bf16[512,512]{1,0:T(8,128)(2,1)} fusion(f32[512,1024]{0,1:T(8,128)S(1)} %fusion.10, bf16[1,512,512]{2,1,0:T(8,128)(2,1)S(1)} %copy-done.3, f32[512]{0:T(512)S(1)} %fusion.11), kind=kOutput, calls=%fused_computation.2 | convolution fusion | flops 270270464 | bytes 3147776 | tf_op jit(solution)/shard_map/tk,tn->kn/dot_general | solution.py:287
  33.2 0.0 copy-done.6
  33.2 0.8 multiply_convert_fusion.2
  34.0 1.3 %fusion.3 = f32[512,1024]{1,0:T(8,128)S(1)} fusion(bf16[1024,1024]{1,0:T(8,128)(2,1)S(1)} %copy-done, bf16[512,512]{0,1:T(8,128)(2,1)S(1)} %get-tuple-element.18, bf16[512,512]{0,1:T(8,128)(2,1)S(1)} %get-tuple-element.17), kind=kOutput, calls=%fused_computation.13 | convolution fusion | flops 1075838976 | bytes 5242880 | tf_op jit(solution)/shard_map/dot_general | solution.py:285
  35.4 0.0 copy-start.1
  35.4 0.0 copy-start.2
  35.4 0.7 slice.95.edge_ref
  36.1 0.6 copy-done.1
  36.8 0.1 fusion.6
  36.9 0.0 copy-done.2
  36.9 2.6 %convolution_convert_fusion = bf16[1024,1024]{1,0:T(8,128)(2,1)} fusion(bf16[512,512]{0,1:T(8,128)(2,1)S(1)} %get-tuple-element.18, bf16[512,512]{0,1:T(8,128)(2,1)S(1)} %get-tuple-element.17, bf16[512,512]{1,0:T(8,128)(2,1)S(1)} %bitcast.31, bf16[256,512]{1,0:T(8,128)(2,1)S(1)} %get-tuple-element.20, bf16[256,512]{1,0:T(8,128)(2,1)S(1)} %collective-permute-done), kind=kOutput, calls=%fused_computation | convolution fusion | flops 1080033280 | bytes 4194304 | tf_op jit(solution)/shard_map/tk,tn->kn/dot_general | solution.py:286
  39.6 46.4 %shard_map.76 = (f32[32,64]{1,0:T(8,128)}, f32[16,32]{1,0:T(8,128)}, bf16[256,512]{1,0:T(8,128)(2,1)}) custom-call(bf16[4,2,2,64,1024]{4,3,2,1,0:T(8,128)(2,1)} %bitcast.29, bf16[4,2,2,32,512]{4,3,2,1,0:T(8,128)(2,1)} %bitcast.32, bf16[256,512]{1,0:T(8,128)(2,1)} %slice.95.edge_ref), custom_call_target="tpu_custom_call" | custom-call | tf_op jit(solution)/shard_map/pallas_call | solution.py:302
  85.9 0.0 copy-start.4
  86.0 0.0 copy-start.5
  86.0 1.2 %fusion.5 = bf16[256,512]{1,0:T(8,128)(2,1)S(1)} fusion(f32[512,1024]{1,0:T(8,128)} %copy-done.1, bf16[256,512]{1,0:T(8,128)(2,1)} %get-tuple-element.14, bf16[1,512,512]{2,1,0:T(8,128)(2,1)S(1)} %copy-done.3), kind=kLoop, calls=%fused_computation.16 | loop fusion | flops 655360 | bytes 1310720 | tf_op jit(solution)/shard_map/convert_element_type | solution.py:306
  87.2 0.8 maximum_bitcast_fusion
  88.0 0.0 copy-done.4
  88.0 0.6 copy.14
  88.6 0.0 copy-done.5
  88.6 0.6 copy.15
  (1 shorter events, 0.0 us)
Async XLA Ops:
  0.6 28.8 %copy-start = (bf16[1024,1024]{1,0:T(8,128)(2,1)S(1)}, bf16[1024,1024]{1,0:T(8,128)(2,1)}, u32[]{:S(2)}) copy-start(bf16[1024,1024]{1,0:T(8,128)(2,1)} %param.7) | copy-start | bytes 6291460
  1.9 27.5 %collective-permute-start = (bf16[256,512]{1,0:T(8,128)(2,1)S(1)}, bf16[256,512]{1,0:T(8,128)(2,1)S(1)}, u32[]{:S(2)}, u32[]{:S(2)}) collective-permute-start(bf16[256,512]{1,0:T(8,128)(2,1)S(1)} %get-tuple-element.19), channel_id=1, source_target_pairs={{0,32},{32,64},{64,96},{96,128},{128,160},{160,192},{192,224},{224... | collective-permute-start | bytes 786440 | tf_op jit(solution)/shard_map/ppermute | solution.py:15
  29.4 2.4 %copy-start.3 = (bf16[1,512,512]{2,1,0:T(8,128)(2,1)S(1)}, bf16[1,512,512]{2,1,0:T(8,128)(2,1)}, u32[]{:S(2)}) copy-start(bf16[1,512,512]{2,1,0:T(8,128)(2,1)} %param.6) | copy-start | bytes 1572868
  31.8 1.4 %copy-start.6 = (bf16[512,512]{1,0:T(8,128)(2,1)S(1)}, bf16[512,512]{1,0:T(8,128)(2,1)}, u32[]{:S(2)}) copy-start(bf16[512,512]{1,0:T(8,128)(2,1)} %param.8) | copy-start | bytes 1572868
  35.4 1.4 %copy-start.1 = (f32[512,1024]{1,0:T(8,128)}, f32[512,1024]{1,0:T(8,128)S(1)}, u32[]{:S(2)}) copy-start(f32[512,1024]{1,0:T(8,128)S(1)} %fusion.3) | copy-start | bytes 6291460
  35.4 1.6 %copy-start.2 = (bf16[1,512,512]{2,1,0:T(8,128)(2,1)S(1)}, bf16[1,512,512]{2,1,0:T(8,128)(2,1)}, u32[]{:S(2)}) copy-start(bf16[1,512,512]{2,1,0:T(8,128)(2,1)} %param.5) | copy-start | bytes 1572868
  85.9 2.1 %copy-start.4 = (f32[32,64]{1,0:T(8,128)S(1)}, f32[32,64]{1,0:T(8,128)}, u32[]{:S(2)}) copy-start(f32[32,64]{1,0:T(8,128)} %get-tuple-element.15) | copy-start | bytes 24580
  86.0 2.7 %copy-start.5 = (f32[16,32]{1,0:T(8,128)S(1)}, f32[16,32]{1,0:T(8,128)}, u32[]{:S(2)}) copy-start(f32[16,32]{1,0:T(8,128)} %get-tuple-element.16) | copy-start | bytes 6148

commit v14 on v13

--- a/solution.py
+++ b/solution.py
@@ -78,7 +78,8 @@
 
         before = tm_dev(lax.rem(t + n_tm - 1, n_tm))
         after = tm_dev(lax.rem(t + 1, n_tm))
-        for peer in peers + x_peers + y_peers + z_peers + [before, after]:
+        far_first = sorted(range(1, nz), key=lambda d: -min(d, nz - d))
+        for peer in [z_peers[d - 1] for d in far_first] + [before, after] + peers + x_peers + y_peers:
             pl.semaphore_signal(barrier, inc=1, device_id=peer, device_id_type=mesh_id)
         pl.semaphore_wait(barrier, n_peers)
 

time: 89.5 us -> 89.4 us (level)
  no operation moved by 1% of the time
where the time goes in v14:
time: 89.4 us; the launch traced here: 89.2 us
  Pallas kernels  46.3 us (52%)
  starting transfers between devices  16.8 us (19%)
  waiting for transfers between devices  10 us (11%)
  matrix products  8.57 us (10%)
  local copies, waits for them, and re-layouts  3.85 us (4%)
  other arithmetic  2.2 us (2%)
  between operations  1.4 us (2%)
    pallas_call x1, Pallas kernels, body(): flip_conv, flip_res, incoming_gradient = reducer(conv_in, res_in, edge_rows)  46.3 us
    ppermute x1, starting transfers between devices, passed_along(): return lax.ppermute(array, axis, pairs)  16.8 us
    ppermute x1, waiting for transfers between devices, passed_along(): return lax.ppermute(array, axis, pairs)  10 us
    dot_general x1, matrix products, body(): jnp.einsum('tk,tn->kn', inputs, pre_grad, preferred_element_type=jnp.floa...  2.63 us
    dot_general x1, matrix products, gate_backward(): pre_act = jnp.dot(inputs, w_conv, preferred_element_type=jnp.float32)  2.39 us
    unnamed x16, local copies, waits for them, and re-layouts  1.89 us
  transfers between devices with their start and end apart: 1, of which 1 were waited for; matrix products, arithmetic and copies ran while one was open for 0% of the time, Pallas kernels for 0%

profile of v14, /device:TPU:1, one launch (start us, length us, event | category | flops | bytes accessed | tf_op | source)
XLA Modules:
  0.0 89.2 jit_solution(8967942660113937875)
XLA Ops:
  0.6 0.0 copy-start
  0.6 1.2 %slice_bitcast_fusion.1 = (bf16[256,512]{1,0:T(8,128)(2,1)S(1)}, bf16[256,512]{1,0:T(8,128)(2,1)S(1)}) fusion(bf16[1,512,512]{2,1,0:T(8,128)(2,1)} %param.5), kind=kLoop, calls=%fused_computation.27 | loop fusion | bytes 1048576 | tf_op jit(solution)/shard_map/slice | solution.py:278
  1.9 16.8 %collective-permute-start = (bf16[256,512]{1,0:T(8,128)(2,1)S(1)}, bf16[256,512]{1,0:T(8,128)(2,1)S(1)}, u32[]{:S(2)}, u32[]{:S(2)}) collective-permute-start(bf16[256,512]{1,0:T(8,128)(2,1)S(1)} %get-tuple-element.19), channel_id=1, source_target_pairs={{0,32},{32,64},{64,96},{96,128},{128,160},{160,192},{192,224},{224... | collective-permute-start | bytes 786440 | tf_op jit(solution)/shard_map/ppermute | solution.py:15
  19.4 10.0 %collective-permute-done = bf16[256,512]{1,0:T(8,128)(2,1)S(1)} collective-permute-done((bf16[256,512]{1,0:T(8,128)(2,1)S(1)}, bf16[256,512]{1,0:T(8,128)(2,1)S(1)}, u32[]{:S(2)}, u32[]{:S(2)}) %collective-permute-start) | collective-permute-done | bytes 262176 | tf_op jit(solution)/shard_map/ppermute | solution.py:15
  29.4 0.0 copy-done
  29.4 0.0 copy-start.3
  29.4 2.4 %fusion.10 = f32[512,1024]{0,1:T(8,128)S(1)} fusion(bf16[1024,1024]{1,0:T(8,128)(2,1)S(1)} %copy-done, bf16[512,512]{1,0:T(8,128)(2,1)} %bitcast.30, bf16[256,512]{1,0:T(8,128)(2,1)S(1)} %get-tuple-element.20, bf16[256,512]{1,0:T(8,128)(2,1)S(1)} %collective-permute-done), kind=kOutput, calls=%fused_computation.25 | convolution fusion | flops 1076887552 | bytes 5242880 | tf_op jit(solution)/shard_map/dot_general | solution.py:20
  31.8 0.0 copy-done.3
  31.8 0.0 copy-start.6
  31.8 1.4 %convolution_convert_fusion.1 = bf16[512,512]{1,0:T(8,128)(2,1)} fusion(f32[512,1024]{0,1:T(8,128)S(1)} %fusion.10, bf16[1,512,512]{2,1,0:T(8,128)(2,1)S(1)} %copy-done.3, f32[512]{0:T(512)S(1)} %fusion.11), kind=kOutput, calls=%fused_computation.2 | convolution fusion | flops 270270464 | bytes 3147776 | tf_op jit(solution)/shard_map/tk,tn->kn/dot_general | solution.py:288
  33.2 0.0 copy-done.6
  33.2 0.8 multiply_convert_fusion.2
  34.0 1.3 %fusion.3 = f32[512,1024]{1,0:T(8,128)S(1)} fusion(bf16[1024,1024]{1,0:T(8,128)(2,1)S(1)} %copy-done, bf16[512,512]{0,1:T(8,128)(2,1)S(1)} %get-tuple-element.18, bf16[512,512]{0,1:T(8,128)(2,1)S(1)} %get-tuple-element.17), kind=kOutput, calls=%fused_computation.13 | convolution fusion | flops 1075838976 | bytes 5242880 | tf_op jit(solution)/shard_map/dot_general | solution.py:286
  35.4 0.0 copy-start.1
  35.4 0.0 copy-start.2
  35.4 0.7 slice.95.edge_ref
  36.1 0.6 copy-done.1
  36.8 0.1 fusion.6
  36.9 0.0 copy-done.2
  36.9 2.6 %convolution_convert_fusion = bf16[1024,1024]{1,0:T(8,128)(2,1)} fusion(bf16[512,512]{0,1:T(8,128)(2,1)S(1)} %get-tuple-element.18, bf16[512,512]{0,1:T(8,128)(2,1)S(1)} %get-tuple-element.17, bf16[512,512]{1,0:T(8,128)(2,1)S(1)} %bitcast.31, bf16[256,512]{1,0:T(8,128)(2,1)S(1)} %get-tuple-element.20, bf16[256,512]{1,0:T(8,128)(2,1)S(1)} %collective-permute-done), kind=kOutput, calls=%fused_computation | convolution fusion | flops 1080033280 | bytes 4194304 | tf_op jit(solution)/shard_map/tk,tn->kn/dot_general | solution.py:287
  39.6 46.3 %shard_map.76 = (f32[32,64]{1,0:T(8,128)}, f32[16,32]{1,0:T(8,128)}, bf16[256,512]{1,0:T(8,128)(2,1)}) custom-call(bf16[4,2,2,64,1024]{4,3,2,1,0:T(8,128)(2,1)} %bitcast.29, bf16[4,2,2,32,512]{4,3,2,1,0:T(8,128)(2,1)} %bitcast.32, bf16[256,512]{1,0:T(8,128)(2,1)} %slice.95.edge_ref), custom_call_target="tpu_custom_call" | custom-call | tf_op jit(solution)/shard_map/pallas_call | solution.py:303
  85.9 0.0 copy-start.4
  85.9 0.0 copy-start.5
  85.9 1.2 %fusion.5 = bf16[256,512]{1,0:T(8,128)(2,1)S(1)} fusion(f32[512,1024]{1,0:T(8,128)} %copy-done.1, bf16[256,512]{1,0:T(8,128)(2,1)} %get-tuple-element.14, bf16[1,512,512]{2,1,0:T(8,128)(2,1)S(1)} %copy-done.3), kind=kLoop, calls=%fused_computation.16 | loop fusion | flops 655360 | bytes 1310720 | tf_op jit(solution)/shard_map/convert_element_type | solution.py:307
  87.2 0.8 maximum_bitcast_fusion
  88.0 0.0 copy-done.4
  88.0 0.6 copy.14
  88.6 0.0 copy-done.5
  88.6 0.6 copy.15
  (1 shorter events, 0.0 us)
Async XLA Ops:
  0.6 28.8 %copy-start = (bf16[1024,1024]{1,0:T(8,128)(2,1)S(1)}, bf16[1024,1024]{1,0:T(8,128)(2,1)}, u32[]{:S(2)}) copy-start(bf16[1024,1024]{1,0:T(8,128)(2,1)} %param.7) | copy-start | bytes 6291460
  1.9 27.5 %collective-permute-start = (bf16[256,512]{1,0:T(8,128)(2,1)S(1)}, bf16[256,512]{1,0:T(8,128)(2,1)S(1)}, u32[]{:S(2)}, u32[]{:S(2)}) collective-permute-start(bf16[256,512]{1,0:T(8,128)(2,1)S(1)} %get-tuple-element.19), channel_id=1, source_target_pairs={{0,32},{32,64},{64,96},{96,128},{128,160},{160,192},{192,224},{224... | collective-permute-start | bytes 786440 | tf_op jit(solution)/shard_map/ppermute | solution.py:15
  29.4 2.4 %copy-start.3 = (bf16[1,512,512]{2,1,0:T(8,128)(2,1)S(1)}, bf16[1,512,512]{2,1,0:T(8,128)(2,1)}, u32[]{:S(2)}) copy-start(bf16[1,512,512]{2,1,0:T(8,128)(2,1)} %param.6) | copy-start | bytes 1572868
  31.8 1.4 %copy-start.6 = (bf16[512,512]{1,0:T(8,128)(2,1)S(1)}, bf16[512,512]{1,0:T(8,128)(2,1)}, u32[]{:S(2)}) copy-start(bf16[512,512]{1,0:T(8,128)(2,1)} %param.8) | copy-start | bytes 1572868
  35.4 1.4 %copy-start.1 = (f32[512,1024]{1,0:T(8,128)}, f32[512,1024]{1,0:T(8,128)S(1)}, u32[]{:S(2)}) copy-start(f32[512,1024]{1,0:T(8,128)S(1)} %fusion.3) | copy-start | bytes 6291460
  35.4 1.6 %copy-start.2 = (bf16[1,512,512]{2,1,0:T(8,128)(2,1)S(1)}, bf16[1,512,512]{2,1,0:T(8,128)(2,1)}, u32[]{:S(2)}) copy-start(bf16[1,512,512]{2,1,0:T(8,128)(2,1)} %param.5) | copy-start | bytes 1572868
  85.9 2.1 %copy-start.4 = (f32[32,64]{1,0:T(8,128)S(1)}, f32[32,64]{1,0:T(8,128)}, u32[]{:S(2)}) copy-start(f32[32,64]{1,0:T(8,128)} %get-tuple-element.15) | copy-start | bytes 24580
  85.9 2.7 %copy-start.5 = (f32[16,32]{1,0:T(8,128)S(1)}, f32[16,32]{1,0:T(8,128)}, u32[]{:S(2)}) copy-start(f32[16,32]{1,0:T(8,128)} %get-tuple-element.16) | copy-start | bytes 6148

commit v15 on v14

--- a/solution.py
+++ b/solution.py
@@ -49,7 +49,7 @@
                sa_conv, sa_res, rya_conv, rya_res,
                sb_conv, sb_res, rxb_conv, rxb_res,
                sz_both, rz_both,
-               edge_buf, send_sems, recv_sems, local_sems):
+               edge_buf, own_conv, own_res, send_sems, recv_sems, local_sems, own_sems):
         me_x = lax.axis_index("x")
         me_zh = lax.axis_index("zh")
         me_c = lax.axis_index("c")
@@ -110,13 +110,19 @@
 
         send(0, conv_ref.at[:, :, pl.ds(other_c, 1)], rc_conv, 0, peers[0])
         send(1, res_ref.at[:, :, pl.ds(other_c, 1)], rc_res, 0, peers[0])
+        own_in = [pltpu.make_async_copy(conv_ref.at[:, :, pl.ds(me_c, 1)], own_conv, own_sems.at[0]),
+                  pltpu.make_async_copy(res_ref.at[:, :, pl.ds(me_c, 1)], own_res, own_sems.at[1])]
+        for copy in own_in:
+            copy.start()
+        for copy in own_in:
+            copy.wait()
         arrive(0, conv_ref.at[:, :, pl.ds(other_c, 1)], rc_conv, 0)
         arrive(1, res_ref.at[:, :, pl.ds(other_c, 1)], rc_res, 0)
         for x in range(nx):
             for zh in range(nzh):
-                own_c = conv_ref[x, zh, pl.ds(me_c, 1)][0].astype(jnp.float32)
+                own_c = own_conv[x, zh, 0].astype(jnp.float32)
                 sx_conv[x, zh] = (own_c + rc_conv[x, zh, 0].astype(jnp.float32)).astype(jnp.bfloat16)
-                own_r = res_ref[x, zh, pl.ds(me_c, 1)][0].astype(jnp.float32)
+                own_r = own_res[x, zh, 0].astype(jnp.float32)
                 sx_res[x, zh] = (own_r + rc_res[x, zh, 0].astype(jnp.float32)).astype(jnp.bfloat16)
 
         for d in range(1, nx):
@@ -233,7 +239,7 @@
         kernel,
         out_shape=(jax.ShapeDtypeStruct((cc, rc), f32), jax.ShapeDtypeStruct((cr, rr), f32),
                    jax.ShapeDtypeStruct(edge_shape, bf16)),
-        in_specs=[vmem, vmem, vmem],
+        in_specs=[pl.BlockSpec(memory_space=pl.ANY), pl.BlockSpec(memory_space=pl.ANY), vmem],
         out_specs=(vmem, vmem, vmem),
         scratch_shapes=[
             pltpu.VMEM((nx, nzh, 1, rc, n_conv), bf16),
@@ -255,9 +261,12 @@
             pltpu.VMEM((nz, cc + cr, rc), bf16),
             pltpu.VMEM((nz, cc + cr, rc), bf16),
             pltpu.VMEM(edge_shape, bf16),
+            pltpu.VMEM((nx, nzh, 1, rc, n_conv), bf16),
+            pltpu.VMEM((nx, nzh, 1, rr, n_res), bf16),
             pltpu.SemaphoreType.DMA((2, n_slots)),
             pltpu.SemaphoreType.DMA((2, n_slots)),
             pltpu.SemaphoreType.DMA((2, 3)),
+            pltpu.SemaphoreType.DMA((2,)),
         ],
         compiler_params=pltpu.CompilerParams(collective_id=0, has_side_effects=True),
     )

time: 89.4 us -> 87.9 us (0.983)
  Pallas kernels: 46.3 us -> 44.8 us
    pallas_call x1, Pallas kernels: 46.3 us -> 44.8 us  [body(): flip_conv, flip_res, incoming_gradient = reducer(conv_in, res_in, edge_rows)]
where the time goes in v15:
time: 87.9 us; the launch traced here: 87.6 us
  Pallas kernels  44.8 us (51%)
  starting transfers between devices  16.8 us (19%)
  waiting for transfers between devices  10 us (11%)
  matrix products  8.57 us (10%)
  local copies, waits for them, and re-layouts  3.85 us (4%)
  other arithmetic  2.2 us (3%)
  between operations  1.4 us (2%)
    pallas_call x1, Pallas kernels, body(): flip_conv, flip_res, incoming_gradient = reducer(conv_in, res_in, edge_rows)  44.8 us
    ppermute x1, starting transfers between devices, passed_along(): return lax.ppermute(array, axis, pairs)  16.8 us
    ppermute x1, waiting for transfers between devices, passed_along(): return lax.ppermute(array, axis, pairs)  10 us
    dot_general x1, matrix products, body(): jnp.einsum('tk,tn->kn', inputs, pre_grad, preferred_element_type=jnp.floa...  2.63 us
    dot_general x1, matrix products, gate_backward(): pre_act = jnp.dot(inputs, w_conv, preferred_element_type=jnp.float32)  2.39 us
    unnamed x16, local copies, waits for them, and re-layouts  1.89 us
  transfers between devices with their start and end apart: 1, of which 1 were waited for; matrix products, arithmetic and copies ran while one was open for 0% of the time, Pallas kernels for 0%

profile of v15, /device:TPU:1, one launch (start us, length us, event | category | flops | bytes accessed | tf_op | source)
XLA Modules:
  0.0 87.6 jit_solution(6675924405476710177)
XLA Ops:
  0.6 0.0 copy-start
  0.6 1.2 %slice_bitcast_fusion.1 = (bf16[256,512]{1,0:T(8,128)(2,1)S(1)}, bf16[256,512]{1,0:T(8,128)(2,1)S(1)}) fusion(bf16[1,512,512]{2,1,0:T(8,128)(2,1)} %param.5), kind=kLoop, calls=%fused_computation.27 | loop fusion | bytes 1048576 | tf_op jit(solution)/shard_map/slice | solution.py:287
  1.9 16.8 %collective-permute-start = (bf16[256,512]{1,0:T(8,128)(2,1)S(1)}, bf16[256,512]{1,0:T(8,128)(2,1)S(1)}, u32[]{:S(2)}, u32[]{:S(2)}) collective-permute-start(bf16[256,512]{1,0:T(8,128)(2,1)S(1)} %get-tuple-element.19), channel_id=1, source_target_pairs={{0,32},{32,64},{64,96},{96,128},{128,160},{160,192},{192,224},{224... | collective-permute-start | bytes 786440 | tf_op jit(solution)/shard_map/ppermute | solution.py:15
  19.4 10.0 %collective-permute-done = bf16[256,512]{1,0:T(8,128)(2,1)S(1)} collective-permute-done((bf16[256,512]{1,0:T(8,128)(2,1)S(1)}, bf16[256,512]{1,0:T(8,128)(2,1)S(1)}, u32[]{:S(2)}, u32[]{:S(2)}) %collective-permute-start) | collective-permute-done | bytes 262176 | tf_op jit(solution)/shard_map/ppermute | solution.py:15
  29.4 0.0 copy-done
  29.4 0.0 copy-start.3
  29.4 2.4 %fusion.10 = f32[512,1024]{0,1:T(8,128)S(1)} fusion(bf16[1024,1024]{1,0:T(8,128)(2,1)S(1)} %copy-done, bf16[512,512]{1,0:T(8,128)(2,1)} %bitcast.30, bf16[256,512]{1,0:T(8,128)(2,1)S(1)} %get-tuple-element.20, bf16[256,512]{1,0:T(8,128)(2,1)S(1)} %collective-permute-done), kind=kOutput, calls=%fused_computation.25 | convolution fusion | flops 1076887552 | bytes 5242880 | tf_op jit(solution)/shard_map/dot_general | solution.py:20
  31.8 0.0 copy-done.3
  31.8 0.0 copy-start.6
  31.8 1.4 %convolution_convert_fusion.1 = bf16[512,512]{1,0:T(8,128)(2,1)} fusion(f32[512,1024]{0,1:T(8,128)S(1)} %fusion.10, bf16[1,512,512]{2,1,0:T(8,128)(2,1)S(1)} %copy-done.3, f32[512]{0:T(512)S(1)} %fusion.11), kind=kOutput, calls=%fused_computation.2 | convolution fusion | flops 270270464 | bytes 3147776 | tf_op jit(solution)/shard_map/tk,tn->kn/dot_general | solution.py:297
  33.2 0.0 copy-done.6
  33.2 0.8 multiply_convert_fusion.2
  34.0 1.3 %fusion.3 = f32[512,1024]{1,0:T(8,128)S(1)} fusion(bf16[1024,1024]{1,0:T(8,128)(2,1)S(1)} %copy-done, bf16[512,512]{0,1:T(8,128)(2,1)S(1)} %get-tuple-element.18, bf16[512,512]{0,1:T(8,128)(2,1)S(1)} %get-tuple-element.17), kind=kOutput, calls=%fused_computation.13 | convolution fusion | flops 1075838976 | bytes 5242880 | tf_op jit(solution)/shard_map/dot_general | solution.py:295
  35.4 0.0 copy-start.1
  35.4 0.0 copy-start.2
  35.4 0.7 slice.95.edge_ref
  36.1 0.6 copy-done.1
  36.8 0.1 fusion.6
  36.9 0.0 copy-done.2
  36.9 2.6 %convolution_convert_fusion = bf16[1024,1024]{1,0:T(8,128)(2,1)} fusion(bf16[512,512]{0,1:T(8,128)(2,1)S(1)} %get-tuple-element.18, bf16[512,512]{0,1:T(8,128)(2,1)S(1)} %get-tuple-element.17, bf16[512,512]{1,0:T(8,128)(2,1)S(1)} %bitcast.31, bf16[256,512]{1,0:T(8,128)(2,1)S(1)} %get-tuple-element.20, bf16[256,512]{1,0:T(8,128)(2,1)S(1)} %collective-permute-done), kind=kOutput, calls=%fused_computation | convolution fusion | flops 1080033280 | bytes 4194304 | tf_op jit(solution)/shard_map/tk,tn->kn/dot_general | solution.py:296
  39.6 44.8 %shard_map.76 = (f32[32,64]{1,0:T(8,128)}, f32[16,32]{1,0:T(8,128)}, bf16[256,512]{1,0:T(8,128)(2,1)}) custom-call(bf16[4,2,2,64,1024]{4,3,2,1,0:T(8,128)(2,1)} %bitcast.29, bf16[4,2,2,32,512]{4,3,2,1,0:T(8,128)(2,1)} %bitcast.32, bf16[256,512]{1,0:T(8,128)(2,1)} %slice.95.edge_ref), custom_call_target="tpu_custom_call" | custom-call | tf_op jit(solution)/shard_map/pallas_call | solution.py:312
  84.4 0.0 copy-start.4
  84.4 0.0 copy-start.5
  84.4 1.2 %fusion.5 = bf16[256,512]{1,0:T(8,128)(2,1)S(1)} fusion(f32[512,1024]{1,0:T(8,128)} %copy-done.1, bf16[256,512]{1,0:T(8,128)(2,1)} %get-tuple-element.14, bf16[1,512,512]{2,1,0:T(8,128)(2,1)S(1)} %copy-done.3), kind=kLoop, calls=%fused_computation.16 | loop fusion | flops 655360 | bytes 1310720 | tf_op jit(solution)/shard_map/convert_element_type | solution.py:316
  85.6 0.8 maximum_bitcast_fusion
  86.4 0.0 copy-done.4
  86.4 0.6 copy.14
  87.0 0.0 copy-done.5
  87.0 0.6 copy.15
  (1 shorter events, 0.0 us)
Async XLA Ops:
  0.6 28.8 %copy-start = (bf16[1024,1024]{1,0:T(8,128)(2,1)S(1)}, bf16[1024,1024]{1,0:T(8,128)(2,1)}, u32[]{:S(2)}) copy-start(bf16[1024,1024]{1,0:T(8,128)(2,1)} %param.7) | copy-start | bytes 6291460
  1.9 27.5 %collective-permute-start = (bf16[256,512]{1,0:T(8,128)(2,1)S(1)}, bf16[256,512]{1,0:T(8,128)(2,1)S(1)}, u32[]{:S(2)}, u32[]{:S(2)}) collective-permute-start(bf16[256,512]{1,0:T(8,128)(2,1)S(1)} %get-tuple-element.19), channel_id=1, source_target_pairs={{0,32},{32,64},{64,96},{96,128},{128,160},{160,192},{192,224},{224... | collective-permute-start | bytes 786440 | tf_op jit(solution)/shard_map/ppermute | solution.py:15
  29.4 2.4 %copy-start.3 = (bf16[1,512,512]{2,1,0:T(8,128)(2,1)S(1)}, bf16[1,512,512]{2,1,0:T(8,128)(2,1)}, u32[]{:S(2)}) copy-start(bf16[1,512,512]{2,1,0:T(8,128)(2,1)} %param.6) | copy-start | bytes 1572868
  31.8 1.4 %copy-start.6 = (bf16[512,512]{1,0:T(8,128)(2,1)S(1)}, bf16[512,512]{1,0:T(8,128)(2,1)}, u32[]{:S(2)}) copy-start(bf16[512,512]{1,0:T(8,128)(2,1)} %param.8) | copy-start | bytes 1572868
  35.4 1.4 %copy-start.1 = (f32[512,1024]{1,0:T(8,128)}, f32[512,1024]{1,0:T(8,128)S(1)}, u32[]{:S(2)}) copy-start(f32[512,1024]{1,0:T(8,128)S(1)} %fusion.3) | copy-start | bytes 6291460
  35.4 1.6 %copy-start.2 = (bf16[1,512,512]{2,1,0:T(8,128)(2,1)S(1)}, bf16[1,512,512]{2,1,0:T(8,128)(2,1)}, u32[]{:S(2)}) copy-start(bf16[1,512,512]{2,1,0:T(8,128)(2,1)} %param.5) | copy-start | bytes 1572868
  84.4 2.1 %copy-start.4 = (f32[32,64]{1,0:T(8,128)S(1)}, f32[32,64]{1,0:T(8,128)}, u32[]{:S(2)}) copy-start(f32[32,64]{1,0:T(8,128)} %get-tuple-element.15) | copy-start | bytes 24580
  84.4 2.7 %copy-start.5 = (f32[16,32]{1,0:T(8,128)S(1)}, f32[16,32]{1,0:T(8,128)}, u32[]{:S(2)}) copy-start(f32[16,32]{1,0:T(8,128)} %get-tuple-element.16) | copy-start | bytes 6148

commit v16 on v15

--- a/solution.py
+++ b/solution.py
@@ -29,7 +29,7 @@
     return (gated, pre_grad)
 
 
-def make_reducer(sizes, rc, n_conv, rr, n_res, scale, edge_shape):
+def make_reducer(sizes, rc, n_conv, rr, n_res, scale, edge_shape, rows_shape):
     nx, nzh, nc, ny, nzl = sizes
     nz = nzh * nzl
     cyc, cyr = n_conv // ny, n_res // ny
@@ -43,13 +43,13 @@
     n_tm = nx * nzh * nc
     mesh_id = pl.DeviceIdType.MESH
 
-    def kernel(conv_ref, res_ref, edge_ref, conv_out, res_out, edge_out,
+    def kernel(conv_ref, res_ref, edge_ref, cot_ref, grad_ref, conv_out, res_out, rows_out,
                rc_conv, rc_res, sx_conv, sx_res,
                rxa_conv, rxa_res, ryb_conv, ryb_res,
                sa_conv, sa_res, rya_conv, rya_res,
                sb_conv, sb_res, rxb_conv, rxb_res,
                sz_both, rz_both,
-               edge_buf, own_conv, own_res, send_sems, recv_sems, local_sems, own_sems):
+               edge_buf, own_conv, own_res, cot_v, cur_v, late_v, send_sems, recv_sems, local_sems, own_sems):
         me_x = lax.axis_index("x")
         me_zh = lax.axis_index("zh")
         me_c = lax.axis_index("c")
@@ -113,6 +113,14 @@
         own_in = [pltpu.make_async_copy(conv_ref.at[:, :, pl.ds(me_c, 1)], own_conv, own_sems.at[0]),
                   pltpu.make_async_copy(res_ref.at[:, :, pl.ds(me_c, 1)], own_res, own_sems.at[1])]
         for copy in own_in:
+            copy.start()
+        step, ch = edge_shape
+        count = cot_v.shape[0]
+        split = count - step
+        row_in = [pltpu.make_async_copy(cot_ref, cot_v, own_sems.at[2]),
+                  pltpu.make_async_copy(grad_ref.at[:, pl.ds(ch, ch)], cur_v, own_sems.at[3]),
+                  pltpu.make_async_copy(grad_ref.at[pl.ds(step, count - step), pl.ds(0, ch)], late_v, own_sems.at[4])]
+        for copy in row_in:
             copy.start()
         for copy in own_in:
             copy.wait()
@@ -135,6 +143,10 @@
                  base_yb + me_y, y_peers[d - 1])
             send(1, sx_res.at[:, :, pl.ds(hr, hr), pl.ds(ty * cyr, cyr)], ryb_res.at[me_y],
                  base_yb + me_y, y_peers[d - 1])
+        for copy in row_in:
+            copy.wait()
+        rows_out[pl.ds(0, split)] = (cot_v[pl.ds(0, split)].astype(jnp.float32) + cur_v[pl.ds(0, split)]
+                                     + late_v[pl.ds(0, split)]).astype(jnp.bfloat16)
         own_b = [keep(0, 0, sx_conv.at[:, :, pl.ds(hc, hc), pl.ds(me_y * cyc, cyc)], ryb_conv.at[me_y]),
                  keep(1, 0, sx_res.at[:, :, pl.ds(hr, hr), pl.ds(me_y * cyr, cyr)], ryb_res.at[me_y])]
 
@@ -221,13 +233,15 @@
         res_out[...] = acc[cc:, :rr] * scale
         edge.wait_recv()
 
+        tail = cot_v[pl.ds(split, step)].astype(jnp.float32) + cur_v[pl.ds(split, step)]
+
         @pl.when(t < n_tm - 1)
         def _():
-            edge_out[...] = edge_buf[...]
+            rows_out[pl.ds(split, step)] = (tail + edge_buf[...].astype(jnp.float32)).astype(jnp.bfloat16)
 
         @pl.when(t == n_tm - 1)
         def _():
-            edge_out[...] = jnp.zeros_like(edge_out)
+            rows_out[pl.ds(split, step)] = tail.astype(jnp.bfloat16)
 
         for copy in sends:
             copy.wait_send()
@@ -238,8 +252,9 @@
     return pl.pallas_call(
         kernel,
         out_shape=(jax.ShapeDtypeStruct((cc, rc), f32), jax.ShapeDtypeStruct((cr, rr), f32),
-                   jax.ShapeDtypeStruct(edge_shape, bf16)),
-        in_specs=[pl.BlockSpec(memory_space=pl.ANY), pl.BlockSpec(memory_space=pl.ANY), vmem],
+                   jax.ShapeDtypeStruct(rows_shape, bf16)),
+        in_specs=[pl.BlockSpec(memory_space=pl.ANY), pl.BlockSpec(memory_space=pl.ANY), vmem,
+                  pl.BlockSpec(memory_space=pl.ANY), pl.BlockSpec(memory_space=pl.ANY)],
         out_specs=(vmem, vmem, vmem),
         scratch_shapes=[
             pltpu.VMEM((nx, nzh, 1, rc, n_conv), bf16),
@@ -263,10 +278,13 @@
             pltpu.VMEM(edge_shape, bf16),
             pltpu.VMEM((nx, nzh, 1, rc, n_conv), bf16),
             pltpu.VMEM((nx, nzh, 1, rr, n_res), bf16),
+            pltpu.VMEM(rows_shape, bf16),
+            pltpu.VMEM(rows_shape, f32),
+            pltpu.VMEM((rows_shape[0] - edge_shape[0], edge_shape[1]), f32),
             pltpu.SemaphoreType.DMA((2, n_slots)),
             pltpu.SemaphoreType.DMA((2, n_slots)),
             pltpu.SemaphoreType.DMA((2, 3)),
-            pltpu.SemaphoreType.DMA((2,)),
+            pltpu.SemaphoreType.DMA((5,)),
         ],
         compiler_params=pltpu.CompilerParams(collective_id=0, has_side_effects=True),
     )
@@ -300,21 +318,11 @@
         rc, rr = kc // n_tm, kr // n_tm
         all_tokens = count_of_rows * n_tm * n_rep
         edge_rows = input_gradient[:DILATION_STEP, :channel_count].astype(jnp.bfloat16)
-        reducer = make_reducer(sizes, rc, n_conv, rr, n_res, float(all_tokens) ** (-0.5), edge_rows.shape)
-        split = count_of_rows - DILATION_STEP
-        head_rows = (
-            cotangent[:split].astype(jnp.float32) + input_gradient[:split, channel_count:]
-            + input_gradient[DILATION_STEP:, :channel_count]
-        ).astype(jnp.bfloat16)
+        reducer = make_reducer(sizes, rc, n_conv, rr, n_res, float(all_tokens) ** (-0.5), edge_rows.shape,
+                               cotangent.shape)
         conv_in = term_conv.astype(jnp.bfloat16).reshape(nx, nzh, nc, rc, n_conv)
         res_in = term_res.astype(jnp.bfloat16).reshape(nx, nzh, nc, rr, n_res)
-        head_rows, conv_in, res_in, edge_rows = lax.optimization_barrier((head_rows, conv_in, res_in, edge_rows))
-        flip_conv, flip_res, incoming_gradient = reducer(conv_in, res_in, edge_rows)
-        tail_rows = (
-            cotangent[split:].astype(jnp.float32) + input_gradient[split:, channel_count:]
-            + incoming_gradient.astype(jnp.float32)
-        ).astype(jnp.bfloat16)
-        grad_rows = jnp.concatenate([head_rows, tail_rows], 0)
+        flip_conv, flip_res, grad_rows = reducer(conv_in, res_in, edge_rows, cotangent, input_gradient)
         return (grad_rows[None], flip_conv.T, flip_res.T)
 
     return body

time: 87.9 us -> 89.7 us (1.020)
  local copies, waits for them, and re-layouts: 3.85 us -> 7.78 us
  other arithmetic: 2.2 us -> 0.01 us
    unnamed x16 -> x13, local copies, waits for them, and re-layouts: 1.89 us -> 5.81 us
    convert_element_type x2 -> x0, other arithmetic: 1.37 us -> none  [the longest x1 1.22 us: body(): tail_rows = (cotangent[split:].astype(jnp.float32) + input_gradient[split...]
where the time goes in v16:
time: 89.7 us; the launch traced here: 89.3 us
  Pallas kernels  44.8 us (50%)
  starting transfers between devices  16.8 us (19%)
  waiting for transfers between devices  10 us (11%)
  matrix products  8.58 us (10%)
  local copies, waits for them, and re-layouts  7.78 us (9%)
  between operations  1.37 us (2%)
    pallas_call x1, Pallas kernels, body(): reducer(conv_in, res_in, edge_rows, cotangent, input_gradient)  44.8 us
    ppermute x1, starting transfers between devices, passed_along(): return lax.ppermute(array, axis, pairs)  16.8 us
    ppermute x1, waiting for transfers between devices, passed_along(): return lax.ppermute(array, axis, pairs)  10 us
    unnamed x13, local copies, waits for them, and re-layouts  5.81 us
    dot_general x1, matrix products, body(): jnp.einsum('tk,tn->kn', inputs, pre_grad, preferred_element_type=jnp.floa...  2.65 us
    dot_general x1, matrix products, gate_backward(): pre_act = jnp.dot(inputs, w_conv, preferred_element_type=jnp.float32)  2.39 us
  transfers between devices with their start and end apart: 1, of which 1 were waited for; matrix products, arithmetic and copies ran while one was open for 0% of the time, Pallas kernels for 0%

profile of v16, /device:TPU:1, one launch (start us, length us, event | category | flops | bytes accessed | tf_op | source)
XLA Modules:
  0.0 89.3 jit_solution(1210737195897854309)
XLA Ops:
  0.6 0.0 copy-start
  0.6 1.2 %slice_bitcast_fusion.1 = (bf16[256,512]{1,0:T(8,128)(2,1)S(1)}, bf16[256,512]{1,0:T(8,128)(2,1)S(1)}) fusion(bf16[1,512,512]{2,1,0:T(8,128)(2,1)} %param.5), kind=kLoop, calls=%fused_computation.18 | loop fusion | bytes 1048576 | tf_op jit(solution)/shard_map/slice | solution.py:305
  1.9 16.8 %collective-permute-start = (bf16[256,512]{1,0:T(8,128)(2,1)S(1)}, bf16[256,512]{1,0:T(8,128)(2,1)S(1)}, u32[]{:S(2)}, u32[]{:S(2)}) collective-permute-start(bf16[256,512]{1,0:T(8,128)(2,1)S(1)} %get-tuple-element.11), channel_id=1, source_target_pairs={{0,32},{32,64},{64,96},{96,128},{128,160},{160,192},{192,224},{224... | collective-permute-start | bytes 786440 | tf_op jit(solution)/shard_map/ppermute | solution.py:15
  19.4 10.0 %collective-permute-done = bf16[256,512]{1,0:T(8,128)(2,1)S(1)} collective-permute-done((bf16[256,512]{1,0:T(8,128)(2,1)S(1)}, bf16[256,512]{1,0:T(8,128)(2,1)S(1)}, u32[]{:S(2)}, u32[]{:S(2)}) %collective-permute-start) | collective-permute-done | bytes 262176 | tf_op jit(solution)/shard_map/ppermute | solution.py:15
  29.4 0.0 copy-done
  29.4 0.0 copy-start.3
  29.4 2.4 %fusion.5 = f32[512,1024]{0,1:T(8,128)S(1)} fusion(bf16[1024,1024]{1,0:T(8,128)(2,1)S(1)} %copy-done, bf16[512,512]{1,0:T(8,128)(2,1)} %bitcast.23, bf16[256,512]{1,0:T(8,128)(2,1)S(1)} %get-tuple-element.12, bf16[256,512]{1,0:T(8,128)(2,1)S(1)} %collective-permute-done), kind=kOutput, calls=%fused_computation.16 | convolution fusion | flops 1076887552 | bytes 5242880 | tf_op jit(solution)/shard_map/dot_general | solution.py:20
  31.8 0.0 copy-done.3
  31.8 0.0 copy-start.4
  31.8 1.4 %convolution_convert_fusion.1 = bf16[512,512]{1,0:T(8,128)(2,1)} fusion(f32[512,1024]{0,1:T(8,128)S(1)} %fusion.5, f32[512]{0:T(512)S(1)} %fusion.6, bf16[1,512,512]{2,1,0:T(8,128)(2,1)S(1)} %copy-done.3), kind=kOutput, calls=%fused_computation.2 | convolution fusion | flops 270270464 | bytes 3147776 | tf_op jit(solution)/shard_map/tk,tn->kn/dot_general | solution.py:315
  33.2 0.0 copy-done.4
  33.2 0.8 multiply_convert_fusion.2
  34.0 0.0 copy-start.2
  34.1 1.3 %fusion.3.grad_ref = f32[512,1024]{1,0:T(8,128)S(1)} fusion(bf16[1024,1024]{1,0:T(8,128)(2,1)S(1)} %copy-done, bf16[512,512]{0,1:T(8,128)(2,1)S(1)} %get-tuple-element.10, bf16[512,512]{0,1:T(8,128)(2,1)S(1)} %get-tuple-element.9), kind=kOutput, calls=%fused_computation.13 | convolution fusion | flops 1075838976 | bytes 5242880 | tf_op jit(solution)/shard_map/dot_general | solution.py:313
  35.4 0.0 copy-start.1
  35.4 1.3 %copy-done.1 = f32[512,1024]{1,0:T(8,128)} copy-done((f32[512,1024]{1,0:T(8,128)}, f32[512,1024]{1,0:T(8,128)S(1)}, u32[]{:S(2)}) %copy-start.1) | copy-done | bytes 2097176
  36.7 0.8 slice.57.edge_ref
  37.4 0.0 copy-done.2
  37.4 2.6 %convolution_convert_fusion = bf16[1024,1024]{1,0:T(8,128)(2,1)} fusion(bf16[512,512]{0,1:T(8,128)(2,1)S(1)} %get-tuple-element.10, bf16[512,512]{0,1:T(8,128)(2,1)S(1)} %get-tuple-element.9, bf16[512,512]{1,0:T(8,128)(2,1)S(1)} %bitcast.24, bf16[256,512]{1,0:T(8,128)(2,1)S(1)} %get-tuple-element.12, bf16[256,512]{1,0:T(8,128)(2,1)S(1)} %collective-permute-done), kind=kOutput, calls=%fused_computation | convolution fusion | flops 1080033280 | bytes 4194304 | tf_op jit(solution)/shard_map/tk,tn->kn/dot_general | solution.py:314
  40.1 44.8 %shard_map.76 = (f32[32,64]{1,0:T(8,128)}, f32[16,32]{1,0:T(8,128)}, bf16[512,512]{1,0:T(8,128)(2,1)}) custom-call(bf16[4,2,2,64,1024]{4,3,2,1,0:T(8,128)(2,1)} %bitcast.22, bf16[4,2,2,32,512]{4,3,2,1,0:T(8,128)(2,1)} %bitcast.27, bf16[256,512]{1,0:T(8,128)(2,1)} %slice.57.edge_ref, bf16[512,512]{1,0:T(8,128)(2,1)} %bitcast.26, f32[512,1024]{1,0:T(8,128)} %copy-done.1), custom_call_target="tpu_custom_call" | custom-call | tf_op jit(solution)/shard_map/pallas_call | solution.py:325
  84.9 1.9 %copy.15 = bf16[1,512,512]{2,1,0:T(8,128)(2,1)} copy(bf16[1,512,512]{2,1,0:T(8,128)(2,1)} %bitcast.25) | data formatting | bytes 1048576
  86.7 1.3 %copy.16 = f32[64,32]{0,1:T(8,128)} copy(f32[64,32]{0,1:T(8,128)} %bitcast.28) | data formatting | bytes 16384
  88.0 1.3 %copy.17 = f32[32,16]{0,1:T(8,128)} copy(f32[32,16]{0,1:T(8,128)} %bitcast.29) | data formatting | bytes 4096
  (1 shorter events, 0.0 us)
Async XLA Ops:
  0.6 28.8 %copy-start = (bf16[1024,1024]{1,0:T(8,128)(2,1)S(1)}, bf16[1024,1024]{1,0:T(8,128)(2,1)}, u32[]{:S(2)}) copy-start(bf16[1024,1024]{1,0:T(8,128)(2,1)} %param.7) | copy-start | bytes 6291460
  1.9 27.5 %collective-permute-start = (bf16[256,512]{1,0:T(8,128)(2,1)S(1)}, bf16[256,512]{1,0:T(8,128)(2,1)S(1)}, u32[]{:S(2)}, u32[]{:S(2)}) collective-permute-start(bf16[256,512]{1,0:T(8,128)(2,1)S(1)} %get-tuple-element.11), channel_id=1, source_target_pairs={{0,32},{32,64},{64,96},{96,128},{128,160},{160,192},{192,224},{224... | collective-permute-start | bytes 786440 | tf_op jit(solution)/shard_map/ppermute | solution.py:15
  29.4 2.4 %copy-start.3 = (bf16[1,512,512]{2,1,0:T(8,128)(2,1)S(1)}, bf16[1,512,512]{2,1,0:T(8,128)(2,1)}, u32[]{:S(2)}) copy-start(bf16[1,512,512]{2,1,0:T(8,128)(2,1)} %param.6) | copy-start | bytes 1572868
  31.8 1.4 %copy-start.4 = (bf16[512,512]{1,0:T(8,128)(2,1)S(1)}, bf16[512,512]{1,0:T(8,128)(2,1)}, u32[]{:S(2)}) copy-start(bf16[512,512]{1,0:T(8,128)(2,1)} %param.8) | copy-start | bytes 1572868
  34.0 3.4 %copy-start.2 = (bf16[1,512,512]{2,1,0:T(8,128)(2,1)S(1)}, bf16[1,512,512]{2,1,0:T(8,128)(2,1)}, u32[]{:S(2)}) copy-start(bf16[1,512,512]{2,1,0:T(8,128)(2,1)} %param.5) | copy-start | bytes 1572868
  35.4 1.3 %copy-start.1 = (f32[512,1024]{1,0:T(8,128)}, f32[512,1024]{1,0:T(8,128)S(1)}, u32[]{:S(2)}) copy-start(f32[512,1024]{1,0:T(8,128)S(1)} %fusion.3.grad_ref) | copy-start | bytes 6291460

commit v17 on v15

--- a/solution.py
+++ b/solution.py
@@ -302,10 +302,10 @@
         edge_rows = input_gradient[:DILATION_STEP, :channel_count].astype(jnp.bfloat16)
         reducer = make_reducer(sizes, rc, n_conv, rr, n_res, float(all_tokens) ** (-0.5), edge_rows.shape)
         split = count_of_rows - DILATION_STEP
-        head_rows = (
-            cotangent[:split].astype(jnp.float32) + input_gradient[:split, channel_count:]
-            + input_gradient[DILATION_STEP:, :channel_count]
-        ).astype(jnp.bfloat16)
+        head_rows = jnp.concatenate([
+            (cotangent[:split].astype(jnp.float32) + input_gradient[:split, channel_count:]
+             + input_gradient[DILATION_STEP:, :channel_count]).astype(jnp.bfloat16),
+            jnp.zeros((count_of_rows - split, channel_count), jnp.bfloat16)], 0)
         conv_in = term_conv.astype(jnp.bfloat16).reshape(nx, nzh, nc, rc, n_conv)
         res_in = term_res.astype(jnp.bfloat16).reshape(nx, nzh, nc, rr, n_res)
         head_rows, conv_in, res_in, edge_rows = lax.optimization_barrier((head_rows, conv_in, res_in, edge_rows))
@@ -314,7 +314,7 @@
             cotangent[split:].astype(jnp.float32) + input_gradient[split:, channel_count:]
             + incoming_gradient.astype(jnp.float32)
         ).astype(jnp.bfloat16)
-        grad_rows = jnp.concatenate([head_rows, tail_rows], 0)
+        grad_rows = lax.dynamic_update_slice(head_rows, tail_rows, (split, 0))
         return (grad_rows[None], flip_conv.T, flip_res.T)
 
     return body

time: 87.9 us -> 88.6 us (level)
  local copies, waits for them, and re-layouts: 3.85 us -> 5.39 us
    unnamed x16 -> x18, local copies, waits for them, and re-layouts: 1.89 us -> 3.4 us
    dynamic_update_slice x0 -> x1, other arithmetic: none -> 1.23 us  [body(): grad_rows = lax.dynamic_update_slice(head_rows, tail_rows, (split, 0))]
    convert_element_type x2 -> x1, other arithmetic: 1.37 us -> 0.14 us  [body(): head_rows = jnp.concatenate([(cotangent[:split].astype(jnp.float32) + inp...]
where the time goes in v17:
time: 88.6 us; the launch traced here: 88.2 us
  Pallas kernels  44.5 us (50%)
  starting transfers between devices  16.8 us (19%)
  waiting for transfers between devices  10 us (11%)
  matrix products  8.62 us (10%)
  local copies, waits for them, and re-layouts  5.39 us (6%)
  between operations  1.42 us (2%)
  other arithmetic  1.37 us (2%)
    pallas_call x1, Pallas kernels, body(): flip_conv, flip_res, incoming_gradient = reducer(conv_in, res_in, edge_rows)  44.5 us
    ppermute x1, starting transfers between devices, passed_along(): return lax.ppermute(array, axis, pairs)  16.8 us
    ppermute x1, waiting for transfers between devices, passed_along(): return lax.ppermute(array, axis, pairs)  10 us
    unnamed x18, local copies, waits for them, and re-layouts  3.4 us
    dot_general x1, matrix products, body(): jnp.einsum('tk,tn->kn', inputs, pre_grad, preferred_element_type=jnp.floa...  2.62 us
    dot_general x1, matrix products, gate_backward(): pre_act = jnp.dot(inputs, w_conv, preferred_element_type=jnp.float32)  2.46 us
  transfers between devices with their start and end apart: 1, of which 1 were waited for; matrix products, arithmetic and copies ran while one was open for 0% of the time, Pallas kernels for 0%

profile of v17, /device:TPU:1, one launch (start us, length us, event | category | flops | bytes accessed | tf_op | source)
XLA Modules:
  0.0 88.2 jit_solution(16983308728681126989)
XLA Ops:
  0.6 0.0 copy-start
  0.6 1.2 %slice_bitcast_fusion.1 = (bf16[256,512]{1,0:T(8,128)(2,1)S(1)}, bf16[256,512]{1,0:T(8,128)(2,1)S(1)}) fusion(bf16[1,512,512]{2,1,0:T(8,128)(2,1)} %param.5), kind=kLoop, calls=%fused_computation.28 | loop fusion | bytes 1048576 | tf_op jit(solution)/shard_map/slice | solution.py:287
  1.9 16.8 %collective-permute-start = (bf16[256,512]{1,0:T(8,128)(2,1)S(1)}, bf16[256,512]{1,0:T(8,128)(2,1)S(1)}, u32[]{:S(2)}, u32[]{:S(2)}) collective-permute-start(bf16[256,512]{1,0:T(8,128)(2,1)S(1)} %get-tuple-element.19), channel_id=1, source_target_pairs={{0,32},{32,64},{64,96},{96,128},{128,160},{160,192},{192,224},{224... | collective-permute-start | bytes 786440 | tf_op jit(solution)/shard_map/ppermute | solution.py:15
  19.4 10.0 %collective-permute-done = bf16[256,512]{1,0:T(8,128)(2,1)S(1)} collective-permute-done((bf16[256,512]{1,0:T(8,128)(2,1)S(1)}, bf16[256,512]{1,0:T(8,128)(2,1)S(1)}, u32[]{:S(2)}, u32[]{:S(2)}) %collective-permute-start) | collective-permute-done | bytes 262176 | tf_op jit(solution)/shard_map/ppermute | solution.py:15
  29.4 0.0 copy-start.6
  29.4 0.0 copy-done
  29.4 0.0 copy-start.3
  29.4 2.5 %fusion.10 = f32[512,1024]{0,1:T(8,128)S(1)} fusion(bf16[1024,1024]{1,0:T(8,128)(2,1)S(1)} %copy-done, bf16[512,512]{1,0:T(8,128)(2,1)} %bitcast.33, bf16[256,512]{1,0:T(8,128)(2,1)S(1)} %get-tuple-element.20, bf16[256,512]{1,0:T(8,128)(2,1)S(1)} %collective-permute-done), kind=kOutput, calls=%fused_computation.24 | convolution fusion | flops 1076887552 | bytes 5242880 | tf_op jit(solution)/shard_map/dot_general | solution.py:20
  31.9 0.0 copy-done.6
  31.9 0.0 copy-done.3
  31.9 0.0 copy-start.5
  31.9 1.4 %convolution_convert_fusion.1 = bf16[512,512]{1,0:T(8,128)(2,1)} fusion(f32[512,1024]{0,1:T(8,128)S(1)} %fusion.10, bf16[1,512,512]{2,1,0:T(8,128)(2,1)S(1)} %copy-done.3, f32[512]{0:T(512)S(1)} %fusion.13), kind=kOutput, calls=%fused_computation.2 | convolution fusion | flops 270270464 | bytes 3147776 | tf_op jit(solution)/shard_map/tk,tn->kn/dot_general | solution.py:297
  33.3 0.0 copy-done.5
  33.3 0.8 multiply_convert_fusion.2
  34.1 1.3 %fusion.3 = f32[512,1024]{1,0:T(8,128)S(1)} fusion(bf16[1024,1024]{1,0:T(8,128)(2,1)S(1)} %copy-done, bf16[512,512]{0,1:T(8,128)(2,1)S(1)} %get-tuple-element.18, bf16[512,512]{0,1:T(8,128)(2,1)S(1)} %get-tuple-element.17), kind=kOutput, calls=%fused_computation.13 | convolution fusion | flops 1075838976 | bytes 5242880 | tf_op jit(solution)/shard_map/dot_general | solution.py:295
  35.4 0.0 copy-start.1
  35.4 0.0 copy-start.2
  35.5 0.0 copy-start.7
  35.5 0.7 slice.99.edge_ref
  36.2 0.6 copy-done.1
  36.9 0.1 fusion.6
  37.0 0.0 copy-done.2
  37.1 0.1 copy-done.7
  37.1 2.6 %convolution_convert_fusion = bf16[1024,1024]{1,0:T(8,128)(2,1)} fusion(bf16[512,512]{0,1:T(8,128)(2,1)S(1)} %get-tuple-element.18, bf16[512,512]{0,1:T(8,128)(2,1)S(1)} %get-tuple-element.17, bf16[512,512]{1,0:T(8,128)(2,1)S(1)} %bitcast.34, bf16[256,512]{1,0:T(8,128)(2,1)S(1)} %get-tuple-element.20, bf16[256,512]{1,0:T(8,128)(2,1)S(1)} %copy-done.7), kind=kOutput, calls=%fused_computation | convolution fusion | flops 1080033280 | bytes 4194304 | tf_op jit(solution)/shard_map/tk,tn->kn/dot_general | solution.py:296
  39.7 44.5 %shard_map.76 = (f32[32,64]{1,0:T(8,128)}, f32[16,32]{1,0:T(8,128)}, bf16[256,512]{1,0:T(8,128)(2,1)}) custom-call(bf16[4,2,2,64,1024]{4,3,2,1,0:T(8,128)(2,1)} %bitcast.32, bf16[4,2,2,32,512]{4,3,2,1,0:T(8,128)(2,1)} %bitcast.36, bf16[256,512]{1,0:T(8,128)(2,1)} %slice.99.edge_ref), custom_call_target="tpu_custom_call" | custom-call | tf_op jit(solution)/shard_map/pallas_call | solution.py:312
  84.3 1.2 %fusion.12 = bf16[1,512,512]{2,1,0:T(8,128)(2,1)S(1)} fusion(bf16[1,512,512]{2,1,0:T(8,128)(2,1)S(1)} %bitcast.35, bf16[256,512]{1,0:T(8,128)(2,1)} %get-tuple-element.14, f32[512,1024]{1,0:T(8,128)} %copy-done.1, bf16[1,512,512]{2,1,0:T(8,128)(2,1)S(1)} %copy-done.3), kind=kLoop, calls=%fused_computation.26 | loop fusion | flops 655360 | bytes 1310720 | tf_op jit(solution)/shard_map/dynamic_update_slice | solution.py:317
  85.5 0.0 copy-start.4
  85.5 1.3 %copy.15 = f32[64,32]{0,1:T(8,128)} copy(f32[64,32]{0,1:T(8,128)} %bitcast.37) | data formatting | bytes 16384
  86.9 1.3 %copy.16 = f32[32,16]{0,1:T(8,128)} copy(f32[32,16]{0,1:T(8,128)} %bitcast.38) | data formatting | bytes 4096
  88.2 0.0 copy-done.4
  (2 shorter events, 0.0 us)
Async XLA Ops:
  0.6 28.8 %copy-start = (bf16[1024,1024]{1,0:T(8,128)(2,1)S(1)}, bf16[1024,1024]{1,0:T(8,128)(2,1)}, u32[]{:S(2)}) copy-start(bf16[1024,1024]{1,0:T(8,128)(2,1)} %param.7) | copy-start | bytes 6291460
  1.9 27.5 %collective-permute-start = (bf16[256,512]{1,0:T(8,128)(2,1)S(1)}, bf16[256,512]{1,0:T(8,128)(2,1)S(1)}, u32[]{:S(2)}, u32[]{:S(2)}) collective-permute-start(bf16[256,512]{1,0:T(8,128)(2,1)S(1)} %get-tuple-element.19), channel_id=1, source_target_pairs={{0,32},{32,64},{64,96},{96,128},{128,160},{160,192},{192,224},{224... | collective-permute-start | bytes 786440 | tf_op jit(solution)/shard_map/ppermute | solution.py:15
  29.4 2.5 %copy-start.6 = (bf16[256,512]{1,0:T(8,128)(2,1)}, bf16[256,512]{1,0:T(8,128)(2,1)S(1)}, u32[]{:S(2)}) copy-start(bf16[256,512]{1,0:T(8,128)(2,1)S(1)} %collective-permute-done) | copy-start | bytes 786436
  29.4 2.5 %copy-start.3 = (bf16[1,512,512]{2,1,0:T(8,128)(2,1)S(1)}, bf16[1,512,512]{2,1,0:T(8,128)(2,1)}, u32[]{:S(2)}) copy-start(bf16[1,512,512]{2,1,0:T(8,128)(2,1)} %param.6) | copy-start | bytes 1572868
  31.9 1.4 %copy-start.5 = (bf16[512,512]{1,0:T(8,128)(2,1)S(1)}, bf16[512,512]{1,0:T(8,128)(2,1)}, u32[]{:S(2)}) copy-start(bf16[512,512]{1,0:T(8,128)(2,1)} %param.8) | copy-start | bytes 1572868
  35.4 1.4 %copy-start.1 = (f32[512,1024]{1,0:T(8,128)}, f32[512,1024]{1,0:T(8,128)S(1)}, u32[]{:S(2)}) copy-start(f32[512,1024]{1,0:T(8,128)S(1)} %fusion.3) | copy-start | bytes 6291460
  35.4 1.6 %copy-start.2 = (bf16[1,512,512]{2,1,0:T(8,128)(2,1)S(1)}, bf16[1,512,512]{2,1,0:T(8,128)(2,1)}, u32[]{:S(2)}) copy-start(bf16[1,512,512]{2,1,0:T(8,128)(2,1)} %param.5) | copy-start | bytes 1572868
  35.5 1.7 %copy-start.7 = (bf16[256,512]{1,0:T(8,128)(2,1)S(1)}, bf16[256,512]{1,0:T(8,128)(2,1)}, u32[]{:S(2)}) copy-start(bf16[256,512]{1,0:T(8,128)(2,1)} %copy-done.6) | copy-start | bytes 786436
  85.5 2.7 %copy-start.4 = (bf16[1,512,512]{2,1,0:T(8,128)(2,1)}, bf16[1,512,512]{2,1,0:T(8,128)(2,1)S(1)}, u32[]{:S(2)}) copy-start(bf16[1,512,512]{2,1,0:T(8,128)(2,1)S(1)} %fusion.12) | copy-start | bytes 1572868

commit v18 on v15

--- a/solution.py
+++ b/solution.py
@@ -272,6 +272,78 @@
     )
 
 
+def make_halo(sizes):
+    nx, nzh, nc, ny, nzl = sizes
+    n_tm = nx * nzh * nc
+    mesh_id = pl.DeviceIdType.MESH
+
+    def kernel(block_ref, out_ref, buf, send_sem, recv_sem):
+        me_y = lax.axis_index("y")
+        me_zl = lax.axis_index("zl")
+        t = (lax.axis_index("x") * nzh + lax.axis_index("zh")) * nc + lax.axis_index("c")
+
+        def dev(u):
+            return (u // (nzh * nc), lax.rem(u // nc, nzh), lax.rem(u, nc), me_y, me_zl)
+
+        nxt = jnp.minimum(t + 1, n_tm - 1)
+        prv = jnp.maximum(t - 1, 0)
+        has_next = t < n_tm - 1
+        has_prev = t > 0
+        rows, step = block_ref.shape[1], out_ref.shape[0]
+        src_ref = block_ref.at[0, pl.ds(rows - step, step)]
+        barrier = pltpu.get_barrier_semaphore()
+
+        @pl.when(has_next)
+        def _():
+            pl.semaphore_signal(barrier, inc=1, device_id=dev(nxt), device_id_type=mesh_id)
+
+        @pl.when(has_prev)
+        def _():
+            pl.semaphore_signal(barrier, inc=1, device_id=dev(prv), device_id_type=mesh_id)
+
+        pl.semaphore_wait(barrier, (1 - (t + 1) // n_tm) + (t + n_tm - 1) // n_tm)
+
+        copy = pltpu.make_async_remote_copy(
+            src_ref=src_ref, dst_ref=buf, send_sem=send_sem, recv_sem=recv_sem,
+            device_id=dev(nxt), device_id_type=mesh_id)
+
+        @pl.when(has_next)
+        def _():
+            copy.start()
+
+        @pl.when(has_prev)
+        def _():
+            copy.wait_recv()
+            out_ref[...] = buf[...]
+
+        @pl.when(t == 0)
+        def _():
+            out_ref[...] = jnp.zeros_like(out_ref)
+
+        @pl.when(has_next)
+        def _():
+            copy.wait_send()
+
+    vmem = pl.BlockSpec(memory_space=pltpu.VMEM)
+
+    def call(block, step):
+        shape = (step, block.shape[2])
+        return pl.pallas_call(
+            kernel,
+            out_shape=jax.ShapeDtypeStruct(shape, block.dtype),
+            in_specs=[pl.BlockSpec(memory_space=pl.ANY)],
+            out_specs=vmem,
+            scratch_shapes=[
+                pltpu.VMEM(shape, block.dtype),
+                pltpu.SemaphoreType.DMA(()),
+                pltpu.SemaphoreType.DMA(()),
+            ],
+            compiler_params=pltpu.CompilerParams(collective_id=1, has_side_effects=True),
+        )(block)
+
+    return call
+
+
 def make_body(sizes):
     nx, nzh, nc, ny, nzl = sizes
     n_tm = nx * nzh * nc
@@ -285,7 +357,7 @@
         channel_count = sequence_rows.shape[1]
         start_row = lax.axis_index(TM) * count_of_rows
         trailing_rows = sequence_rows[count_of_rows - DILATION_STEP :]
-        arrived = passed_along(trailing_rows, TM, 1, n_tm)
+        arrived = make_halo(sizes)(samples, DILATION_STEP)
         prior_samples = jnp.concatenate(
             [arrived, sequence_rows[: count_of_rows - DILATION_STEP]], 0
         )

time: 87.9 us -> 88.6 us (level)
  Pallas kernels: 44.8 us -> 72.1 us
  starting transfers between devices: 16.8 us -> 0 us
  waiting for transfers between devices: 10 us -> 0 us
    pallas_call x0 -> x1, Pallas kernels: none -> 20.1 us  [call(): pl.pallas_call(kernel, out_shape=jax.ShapeDtypeStruct(shape, block.dtype)...]
    ppermute x1 -> x0, starting transfers between devices: 16.8 us -> none  [passed_along(): return lax.ppermute(array, axis, pairs)]
    ppermute x1 -> x0, waiting for transfers between devices: 10 us -> none  [passed_along(): return lax.ppermute(array, axis, pairs)]
    pallas_call x1, Pallas kernels: 44.8 us -> 51.9 us  [body(): flip_conv, flip_res, incoming_gradient = reducer(conv_in, res_in, edge_rows)]
    unnamed x16 -> x18, local copies, waits for them, and re-layouts: 1.89 us -> 2.08 us
  transfers between devices with their start and end apart: 1 -> 0, of which waited for: 1 -> 0; matrix products, arithmetic and copies ran while one was open for 0% -> 0% of each run, Pallas kernels for 0% -> 0%
where the time goes in v18:
time: 88.6 us; the launch traced here: 88.3 us
  Pallas kernels  72.1 us (81%)
  matrix products  8.63 us (10%)
  local copies, waits for them, and re-layouts  3.86 us (4%)
  other arithmetic  2.2 us (2%)
  between operations  1.55 us (2%)
    pallas_call x1, Pallas kernels, body(): flip_conv, flip_res, incoming_gradient = reducer(conv_in, res_in, edge_rows)  51.9 us
    pallas_call x1, Pallas kernels, call(): pl.pallas_call(kernel, out_shape=jax.ShapeDtypeStruct(shape, block.dtype)...  20.1 us
    dot_general x1, matrix products, body(): jnp.einsum('tk,tn->kn', inputs, pre_grad, preferred_element_type=jnp.floa...  2.62 us
    dot_general x1, matrix products, gate_backward(): pre_act = jnp.dot(inputs, w_conv, preferred_element_type=jnp.float32)  2.47 us
    unnamed x18, local copies, waits for them, and re-layouts  2.08 us

profile of v18, /device:TPU:1, one launch (start us, length us, event | category | flops | bytes accessed | tf_op | source)
XLA Modules:
  0.0 88.3 jit_solution(9894203914303760775)
XLA Ops:
  0.6 0.0 copy-start
  1.5 20.1 %shard_map.76 = bf16[256,512]{1,0:T(8,128)(2,1)} custom-call(bf16[1,512,512]{2,1,0:T(8,128)(2,1)} %block_ref.1), custom_call_target="tpu_custom_call" | custom-call | tf_op jit(solution)/shard_map/pallas_call | solution.py:331
  21.6 1.0 %slice_bitcast_fusion = bf16[256,512]{1,0:T(8,128)(2,1)S(1)} fusion(bf16[1,512,512]{2,1,0:T(8,128)(2,1)} %block_ref.1), kind=kLoop, calls=%fused_computation.26 | loop fusion | bytes 524288 | tf_op jit(solution)/shard_map/slice | solution.py:362
  22.6 0.0 copy-done
  22.6 0.0 copy-start.3
  22.6 2.5 %fusion.10 = f32[512,1024]{0,1:T(8,128)S(1)} fusion(bf16[1024,1024]{1,0:T(8,128)(2,1)S(1)} %copy-done, bf16[512,512]{1,0:T(8,128)(2,1)} %bitcast.28, bf16[256,512]{1,0:T(8,128)(2,1)S(1)} %slice_bitcast_fusion, bf16[256,512]{1,0:T(8,128)(2,1)} %shard_map.76), kind=kOutput, calls=%fused_computation.25 | convolution fusion | flops 1076887552 | bytes 5242880 | tf_op jit(solution)/shard_map/dot_general | solution.py:20
  25.1 0.0 copy-done.3
  25.1 0.0 copy-start.7
  25.1 1.4 %convolution_convert_fusion.1 = bf16[512,512]{1,0:T(8,128)(2,1)} fusion(f32[512,1024]{0,1:T(8,128)S(1)} %fusion.10, bf16[1,512,512]{2,1,0:T(8,128)(2,1)S(1)} %copy-done.3, f32[512]{0:T(512)S(1)} %fusion.11), kind=kOutput, calls=%fused_computation.2 | convolution fusion | flops 270270464 | bytes 3147776 | tf_op jit(solution)/shard_map/tk,tn->kn/dot_general | solution.py:369
  26.5 0.0 copy-done.7
  26.5 0.0 copy-start.2
  26.5 0.0 copy-start.4
  26.5 0.8 multiply_convert_fusion.2
  27.3 0.2 copy-done.2
  27.5 0.1 copy-done.4
  27.6 2.6 %convolution_convert_fusion = bf16[1024,1024]{1,0:T(8,128)(2,1)} fusion(bf16[512,512]{0,1:T(8,128)(2,1)S(1)} %get-tuple-element.18, bf16[512,512]{0,1:T(8,128)(2,1)S(1)} %get-tuple-element.17, bf16[512,512]{1,0:T(8,128)(2,1)S(1)} %bitcast.29, bf16[256,512]{1,0:T(8,128)(2,1)S(1)} %slice_bitcast_fusion, bf16[256,512]{1,0:T(8,128)(2,1)S(1)} %copy-done.4), kind=kOutput, calls=%fused_computation | convolution fusion | flops 1080033280 | bytes 4194304 | tf_op jit(solution)/shard_map/tk,tn->kn/dot_general | solution.py:368
  30.2 1.3 %fusion.3 = f32[512,1024]{1,0:T(8,128)S(1)} fusion(bf16[1024,1024]{1,0:T(8,128)(2,1)S(1)} %copy-done, bf16[512,512]{0,1:T(8,128)(2,1)S(1)} %get-tuple-element.18, bf16[512,512]{0,1:T(8,128)(2,1)S(1)} %get-tuple-element.17), kind=kOutput, calls=%fused_computation.13 | convolution fusion | flops 1075838976 | bytes 5242880 | tf_op jit(solution)/shard_map/dot_general | solution.py:367
  31.5 0.0 copy-start.1
  31.5 0.8 slice.86.edge_ref
  32.3 0.6 copy-done.1
  32.9 0.1 fusion.6
  33.1 51.9 %shard_map.77 = (f32[32,64]{1,0:T(8,128)}, f32[16,32]{1,0:T(8,128)}, bf16[256,512]{1,0:T(8,128)(2,1)}) custom-call(bf16[4,2,2,64,1024]{4,3,2,1,0:T(8,128)(2,1)} %bitcast.27, bf16[4,2,2,32,512]{4,3,2,1,0:T(8,128)(2,1)} %bitcast.30, bf16[256,512]{1,0:T(8,128)(2,1)} %slice.86.edge_ref), custom_call_target="tpu_custom_call" | custom-call | tf_op jit(solution)/shard_map/pallas_call | solution.py:384
  85.1 0.0 copy-start.5
  85.1 0.0 copy-start.6
  85.1 1.2 %fusion.5 = bf16[256,512]{1,0:T(8,128)(2,1)S(1)} fusion(f32[512,1024]{1,0:T(8,128)} %copy-done.1, bf16[256,512]{1,0:T(8,128)(2,1)} %get-tuple-element.14, bf16[1,512,512]{2,1,0:T(8,128)(2,1)S(1)} %copy-done.3), kind=kLoop, calls=%fused_computation.16 | loop fusion | flops 655360 | bytes 1310720 | tf_op jit(solution)/shard_map/convert_element_type | solution.py:388
  86.3 0.8 maximum_bitcast_fusion
  87.1 0.0 copy-done.5
  87.1 0.6 copy.14
  87.7 0.0 copy-done.6
  87.7 0.6 copy.15
  (1 shorter events, 0.0 us)
Async XLA Ops:
  0.6 22.0 %copy-start = (bf16[1024,1024]{1,0:T(8,128)(2,1)S(1)}, bf16[1024,1024]{1,0:T(8,128)(2,1)}, u32[]{:S(2)}) copy-start(bf16[1024,1024]{1,0:T(8,128)(2,1)} %param.7) | copy-start | bytes 6291460
  22.6 2.5 %copy-start.3 = (bf16[1,512,512]{2,1,0:T(8,128)(2,1)S(1)}, bf16[1,512,512]{2,1,0:T(8,128)(2,1)}, u32[]{:S(2)}) copy-start(bf16[1,512,512]{2,1,0:T(8,128)(2,1)} %param.6) | copy-start | bytes 1572868
  25.1 1.4 %copy-start.7 = (bf16[512,512]{1,0:T(8,128)(2,1)S(1)}, bf16[512,512]{1,0:T(8,128)(2,1)}, u32[]{:S(2)}) copy-start(bf16[512,512]{1,0:T(8,128)(2,1)} %param.8) | copy-start | bytes 1572868
  26.5 1.0 %copy-start.2 = (bf16[1,512,512]{2,1,0:T(8,128)(2,1)S(1)}, bf16[1,512,512]{2,1,0:T(8,128)(2,1)}, u32[]{:S(2)}) copy-start(bf16[1,512,512]{2,1,0:T(8,128)(2,1)} %block_ref.1) | copy-start | bytes 1572868
  26.5 1.1 %copy-start.4 = (bf16[256,512]{1,0:T(8,128)(2,1)S(1)}, bf16[256,512]{1,0:T(8,128)(2,1)}, u32[]{:S(2)}) copy-start(bf16[256,512]{1,0:T(8,128)(2,1)} %shard_map.76) | copy-start | bytes 786436
  31.5 1.4 %copy-start.1 = (f32[512,1024]{1,0:T(8,128)}, f32[512,1024]{1,0:T(8,128)S(1)}, u32[]{:S(2)}) copy-start(f32[512,1024]{1,0:T(8,128)S(1)} %fusion.3) | copy-start | bytes 6291460
  85.1 2.1 %copy-start.5 = (f32[32,64]{1,0:T(8,128)S(1)}, f32[32,64]{1,0:T(8,128)}, u32[]{:S(2)}) copy-start(f32[32,64]{1,0:T(8,128)} %get-tuple-element.15) | copy-start | bytes 24580
  85.1 2.7 %copy-start.6 = (f32[16,32]{1,0:T(8,128)S(1)}, f32[16,32]{1,0:T(8,128)}, u32[]{:S(2)}) copy-start(f32[16,32]{1,0:T(8,128)} %get-tuple-element.16) | copy-start | bytes 6148

commit v19 on v15

--- a/solution.py
+++ b/solution.py
@@ -104,7 +104,7 @@
             return copy
 
         edge = pltpu.make_async_remote_copy(
-            src_ref=edge_ref, dst_ref=edge_buf, send_sem=local_sems.at[0, 2],
+            src_ref=edge_ref.at[pl.ds(0, edge_shape[0]), pl.ds(0, edge_shape[1])], dst_ref=edge_buf, send_sem=local_sems.at[0, 2],
             recv_sem=local_sems.at[1, 2], device_id=before, device_id_type=mesh_id)
         edge.start()
 
@@ -238,8 +238,8 @@
     return pl.pallas_call(
         kernel,
         out_shape=(jax.ShapeDtypeStruct((cc, rc), f32), jax.ShapeDtypeStruct((cr, rr), f32),
-                   jax.ShapeDtypeStruct(edge_shape, bf16)),
-        in_specs=[pl.BlockSpec(memory_space=pl.ANY), pl.BlockSpec(memory_space=pl.ANY), vmem],
+                   jax.ShapeDtypeStruct(edge_shape, f32)),
+        in_specs=[pl.BlockSpec(memory_space=pl.ANY)] * 3,
         out_specs=(vmem, vmem, vmem),
         scratch_shapes=[
             pltpu.VMEM((nx, nzh, 1, rc, n_conv), bf16),
@@ -260,7 +260,7 @@
             pltpu.VMEM((nx, nzh, hr, cyr), bf16),
             pltpu.VMEM((nz, cc + cr, rc), bf16),
             pltpu.VMEM((nz, cc + cr, rc), bf16),
-            pltpu.VMEM(edge_shape, bf16),
+            pltpu.VMEM(edge_shape, f32),
             pltpu.VMEM((nx, nzh, 1, rc, n_conv), bf16),
             pltpu.VMEM((nx, nzh, 1, rr, n_res), bf16),
             pltpu.SemaphoreType.DMA((2, n_slots)),
@@ -299,8 +299,8 @@
         kr, n_res = term_res.shape
         rc, rr = kc // n_tm, kr // n_tm
         all_tokens = count_of_rows * n_tm * n_rep
-        edge_rows = input_gradient[:DILATION_STEP, :channel_count].astype(jnp.bfloat16)
-        reducer = make_reducer(sizes, rc, n_conv, rr, n_res, float(all_tokens) ** (-0.5), edge_rows.shape)
+        edge_shape = (DILATION_STEP, channel_count)
+        reducer = make_reducer(sizes, rc, n_conv, rr, n_res, float(all_tokens) ** (-0.5), edge_shape)
         split = count_of_rows - DILATION_STEP
         head_rows = (
             cotangent[:split].astype(jnp.float32) + input_gradient[:split, channel_count:]
@@ -308,8 +308,8 @@
         ).astype(jnp.bfloat16)
         conv_in = term_conv.astype(jnp.bfloat16).reshape(nx, nzh, nc, rc, n_conv)
         res_in = term_res.astype(jnp.bfloat16).reshape(nx, nzh, nc, rr, n_res)
-        head_rows, conv_in, res_in, edge_rows = lax.optimization_barrier((head_rows, conv_in, res_in, edge_rows))
-        flip_conv, flip_res, incoming_gradient = reducer(conv_in, res_in, edge_rows)
+        head_rows, conv_in, res_in = lax.optimization_barrier((head_rows, conv_in, res_in))
+        flip_conv, flip_res, incoming_gradient = reducer(conv_in, res_in, input_gradient)
         tail_rows = (
             cotangent[split:].astype(jnp.float32) + input_gradient[split:, channel_count:]
             + incoming_gradient.astype(jnp.float32)

time: 87.9 us -> 92.1 us (1.048)
  Pallas kernels: 44.8 us -> 48.9 us
    pallas_call x1, Pallas kernels: 44.8 us -> 48.9 us  [body(): reducer(conv_in, res_in, input_gradient)]
where the time goes in v19:
time: 92.1 us; the launch traced here: 91.9 us
  Pallas kernels  48.9 us (53%)
  starting transfers between devices  16.8 us (18%)
  waiting for transfers between devices  10 us (11%)
  matrix products  8.57 us (9%)
  local copies, waits for them, and re-layouts  3.78 us (4%)
  other arithmetic  2.32 us (3%)
  between operations  1.4 us (2%)
    pallas_call x1, Pallas kernels, body(): reducer(conv_in, res_in, input_gradient)  48.9 us
    ppermute x1, starting transfers between devices, passed_along(): return lax.ppermute(array, axis, pairs)  16.8 us
    ppermute x1, waiting for transfers between devices, passed_along(): return lax.ppermute(array, axis, pairs)  10 us
    dot_general x1, matrix products, body(): jnp.einsum('tk,tn->kn', inputs, pre_grad, preferred_element_type=jnp.floa...  2.63 us
    unnamed x16, local copies, waits for them, and re-layouts  2.56 us
    dot_general x1, matrix products, gate_backward(): pre_act = jnp.dot(inputs, w_conv, preferred_element_type=jnp.float32)  2.39 us
  transfers between devices with their start and end apart: 1, of which 1 were waited for; matrix products, arithmetic and copies ran while one was open for 0% of the time, Pallas kernels for 0%

profile of v19, /device:TPU:1, one launch (start us, length us, event | category | flops | bytes accessed | tf_op | source)
XLA Modules:
  0.0 91.9 jit_solution(11037242971380935164)
XLA Ops:
  0.6 0.0 copy-start
  0.6 1.2 %slice_bitcast_fusion.1 = (bf16[256,512]{1,0:T(8,128)(2,1)S(1)}, bf16[256,512]{1,0:T(8,128)(2,1)S(1)}) fusion(bf16[1,512,512]{2,1,0:T(8,128)(2,1)} %param.5), kind=kLoop, calls=%fused_computation.26 | loop fusion | bytes 1048576 | tf_op jit(solution)/shard_map/slice | solution.py:287
  1.9 16.8 %collective-permute-start = (bf16[256,512]{1,0:T(8,128)(2,1)S(1)}, bf16[256,512]{1,0:T(8,128)(2,1)S(1)}, u32[]{:S(2)}, u32[]{:S(2)}) collective-permute-start(bf16[256,512]{1,0:T(8,128)(2,1)S(1)} %get-tuple-element.17), channel_id=1, source_target_pairs={{0,32},{32,64},{64,96},{96,128},{128,160},{160,192},{192,224},{224... | collective-permute-start | bytes 786440 | tf_op jit(solution)/shard_map/ppermute | solution.py:15
  19.4 10.0 %collective-permute-done = bf16[256,512]{1,0:T(8,128)(2,1)S(1)} collective-permute-done((bf16[256,512]{1,0:T(8,128)(2,1)S(1)}, bf16[256,512]{1,0:T(8,128)(2,1)S(1)}, u32[]{:S(2)}, u32[]{:S(2)}) %collective-permute-start) | collective-permute-done | bytes 262176 | tf_op jit(solution)/shard_map/ppermute | solution.py:15
  29.4 0.0 copy-done
  29.4 0.0 copy-start.3
  29.4 2.4 %fusion.10 = f32[512,1024]{0,1:T(8,128)S(1)} fusion(bf16[1024,1024]{1,0:T(8,128)(2,1)S(1)} %copy-done, bf16[512,512]{1,0:T(8,128)(2,1)} %bitcast.31, bf16[256,512]{1,0:T(8,128)(2,1)S(1)} %get-tuple-element.18, bf16[256,512]{1,0:T(8,128)(2,1)S(1)} %collective-permute-done), kind=kOutput, calls=%fused_computation.24 | convolution fusion | flops 1076887552 | bytes 5242880 | tf_op jit(solution)/shard_map/dot_general | solution.py:20
  31.8 0.0 copy-done.3
  31.8 0.0 copy-start.6
  31.8 1.4 %convolution_convert_fusion.1 = bf16[512,512]{1,0:T(8,128)(2,1)} fusion(f32[512,1024]{0,1:T(8,128)S(1)} %fusion.10, bf16[1,512,512]{2,1,0:T(8,128)(2,1)S(1)} %copy-done.3, f32[512]{0:T(512)S(1)} %fusion.11), kind=kOutput, calls=%fused_computation.2 | convolution fusion | flops 270270464 | bytes 3147776 | tf_op jit(solution)/shard_map/tk,tn->kn/dot_general | solution.py:297
  33.2 0.0 copy-done.6
  33.2 0.8 multiply_convert_fusion.2
  34.0 0.0 copy-start.2
  34.1 1.3 %fusion.3.edge_ref = f32[512,1024]{1,0:T(8,128)S(1)} fusion(bf16[1024,1024]{1,0:T(8,128)(2,1)S(1)} %copy-done, bf16[512,512]{0,1:T(8,128)(2,1)S(1)} %get-tuple-element.16, bf16[512,512]{0,1:T(8,128)(2,1)S(1)} %get-tuple-element.15), kind=kOutput, calls=%fused_computation.13 | convolution fusion | flops 1075838976 | bytes 5242880 | tf_op jit(solution)/shard_map/dot_general | solution.py:295
  35.4 0.0 copy-start.1
  35.4 1.3 %copy-done.1 = f32[512,1024]{1,0:T(8,128)} copy-done((f32[512,1024]{1,0:T(8,128)}, f32[512,1024]{1,0:T(8,128)S(1)}, u32[]{:S(2)}) %copy-start.1) | copy-done | bytes 2097176
  36.7 0.1 fusion.6
  36.9 0.0 copy-done.2
  36.9 2.6 %convolution_convert_fusion = bf16[1024,1024]{1,0:T(8,128)(2,1)} fusion(bf16[512,512]{0,1:T(8,128)(2,1)S(1)} %get-tuple-element.16, bf16[512,512]{0,1:T(8,128)(2,1)S(1)} %get-tuple-element.15, bf16[512,512]{1,0:T(8,128)(2,1)S(1)} %bitcast.32, bf16[256,512]{1,0:T(8,128)(2,1)S(1)} %get-tuple-element.18, bf16[256,512]{1,0:T(8,128)(2,1)S(1)} %collective-permute-done), kind=kOutput, calls=%fused_computation | convolution fusion | flops 1080033280 | bytes 4194304 | tf_op jit(solution)/shard_map/tk,tn->kn/dot_general | solution.py:296
  39.5 48.9 %shard_map.76 = (f32[32,64]{1,0:T(8,128)}, f32[16,32]{1,0:T(8,128)}, f32[256,512]{1,0:T(8,128)}) custom-call(bf16[4,2,2,64,1024]{4,3,2,1,0:T(8,128)(2,1)} %bitcast.29, bf16[4,2,2,32,512]{4,3,2,1,0:T(8,128)(2,1)} %bitcast.30, f32[512,1024]{1,0:T(8,128)} %copy-done.1), custom_call_target="tpu_custom_call" | custom-call | tf_op jit(solution)/shard_map/pallas_call | solution.py:312
  88.4 0.0 copy-start.4
  88.5 0.0 copy-start.5
  88.5 1.3 %fusion.5 = bf16[256,512]{1,0:T(8,128)(2,1)S(1)} fusion(f32[256,512]{1,0:T(8,128)} %get-tuple-element.12, f32[512,1024]{1,0:T(8,128)} %copy-done.1, bf16[1,512,512]{2,1,0:T(8,128)(2,1)S(1)} %copy-done.3), kind=kLoop, calls=%fused_computation.16 | loop fusion | flops 524288 | bytes 1572864 | tf_op jit(solution)/shard_map/convert_element_type | solution.py:316
  89.8 0.8 maximum_bitcast_fusion
  90.6 0.0 copy-done.4
  90.6 0.6 copy.14
  91.3 0.0 copy-done.5
  91.3 0.6 copy.15
  (1 shorter events, 0.0 us)
Async XLA Ops:
  0.6 28.8 %copy-start = (bf16[1024,1024]{1,0:T(8,128)(2,1)S(1)}, bf16[1024,1024]{1,0:T(8,128)(2,1)}, u32[]{:S(2)}) copy-start(bf16[1024,1024]{1,0:T(8,128)(2,1)} %param.7) | copy-start | bytes 6291460
  1.9 27.5 %collective-permute-start = (bf16[256,512]{1,0:T(8,128)(2,1)S(1)}, bf16[256,512]{1,0:T(8,128)(2,1)S(1)}, u32[]{:S(2)}, u32[]{:S(2)}) collective-permute-start(bf16[256,512]{1,0:T(8,128)(2,1)S(1)} %get-tuple-element.17), channel_id=1, source_target_pairs={{0,32},{32,64},{64,96},{96,128},{128,160},{160,192},{192,224},{224... | collective-permute-start | bytes 786440 | tf_op jit(solution)/shard_map/ppermute | solution.py:15
  29.4 2.4 %copy-start.3 = (bf16[1,512,512]{2,1,0:T(8,128)(2,1)S(1)}, bf16[1,512,512]{2,1,0:T(8,128)(2,1)}, u32[]{:S(2)}) copy-start(bf16[1,512,512]{2,1,0:T(8,128)(2,1)} %param.6) | copy-start | bytes 1572868
  31.8 1.4 %copy-start.6 = (bf16[512,512]{1,0:T(8,128)(2,1)S(1)}, bf16[512,512]{1,0:T(8,128)(2,1)}, u32[]{:S(2)}) copy-start(bf16[512,512]{1,0:T(8,128)(2,1)} %param.8) | copy-start | bytes 1572868
  34.0 2.8 %copy-start.2 = (bf16[1,512,512]{2,1,0:T(8,128)(2,1)S(1)}, bf16[1,512,512]{2,1,0:T(8,128)(2,1)}, u32[]{:S(2)}) copy-start(bf16[1,512,512]{2,1,0:T(8,128)(2,1)} %param.5) | copy-start | bytes 1572868
  35.4 1.3 %copy-start.1 = (f32[512,1024]{1,0:T(8,128)}, f32[512,1024]{1,0:T(8,128)S(1)}, u32[]{:S(2)}) copy-start(f32[512,1024]{1,0:T(8,128)S(1)} %fusion.3.edge_ref) | copy-start | bytes 6291460
  88.4 2.2 %copy-start.4 = (f32[32,64]{1,0:T(8,128)S(1)}, f32[32,64]{1,0:T(8,128)}, u32[]{:S(2)}) copy-start(f32[32,64]{1,0:T(8,128)} %get-tuple-element.13) | copy-start | bytes 24580
  88.5 2.8 %copy-start.5 = (f32[16,32]{1,0:T(8,128)S(1)}, f32[16,32]{1,0:T(8,128)}, u32[]{:S(2)}) copy-start(f32[16,32]{1,0:T(8,128)} %get-tuple-element.14) | copy-start | bytes 6148

commit v20 on v15

--- a/solution.py
+++ b/solution.py
@@ -239,7 +239,7 @@
         kernel,
         out_shape=(jax.ShapeDtypeStruct((cc, rc), f32), jax.ShapeDtypeStruct((cr, rr), f32),
                    jax.ShapeDtypeStruct(edge_shape, bf16)),
-        in_specs=[pl.BlockSpec(memory_space=pl.ANY), pl.BlockSpec(memory_space=pl.ANY), vmem],
+        in_specs=[pl.BlockSpec(memory_space=pl.ANY)] * 3,
         out_specs=(vmem, vmem, vmem),
         scratch_shapes=[
             pltpu.VMEM((nx, nzh, 1, rc, n_conv), bf16),

time: 87.9 us -> 87.3 us (level)
  Pallas kernels: 44.8 us -> 43.7 us
    pallas_call x1, Pallas kernels: 44.8 us -> 43.7 us  [body(): flip_conv, flip_res, incoming_gradient = reducer(conv_in, res_in, edge_rows)]
where the time goes in v20:
time: 87.3 us; the launch traced here: 86.5 us
  Pallas kernels  43.7 us (50%)
  starting transfers between devices  16.8 us (19%)
  waiting for transfers between devices  10 us (11%)
  matrix products  8.57 us (10%)
  local copies, waits for them, and re-layouts  3.85 us (4%)
  other arithmetic  2.2 us (3%)
  between operations  1.4 us (2%)
    pallas_call x1, Pallas kernels, body(): flip_conv, flip_res, incoming_gradient = reducer(conv_in, res_in, edge_rows)  43.7 us
    ppermute x1, starting transfers between devices, passed_along(): return lax.ppermute(array, axis, pairs)  16.8 us
    ppermute x1, waiting for transfers between devices, passed_along(): return lax.ppermute(array, axis, pairs)  10 us
    dot_general x1, matrix products, body(): jnp.einsum('tk,tn->kn', inputs, pre_grad, preferred_element_type=jnp.floa...  2.63 us
    dot_general x1, matrix products, gate_backward(): pre_act = jnp.dot(inputs, w_conv, preferred_element_type=jnp.float32)  2.39 us
    unnamed x16, local copies, waits for them, and re-layouts  1.89 us
  transfers between devices with their start and end apart: 1, of which 1 were waited for; matrix products, arithmetic and copies ran while one was open for 0% of the time, Pallas kernels for 0%

profile of v20, /device:TPU:1, one launch (start us, length us, event | category | flops | bytes accessed | tf_op | source)
XLA Modules:
  0.0 86.5 jit_solution(8635816013768901683)
XLA Ops:
  0.6 0.0 copy-start
  0.6 1.2 %slice_bitcast_fusion.1 = (bf16[256,512]{1,0:T(8,128)(2,1)S(1)}, bf16[256,512]{1,0:T(8,128)(2,1)S(1)}) fusion(bf16[1,512,512]{2,1,0:T(8,128)(2,1)} %param.5), kind=kLoop, calls=%fused_computation.27 | loop fusion | bytes 1048576 | tf_op jit(solution)/shard_map/slice | solution.py:287
  1.9 16.8 %collective-permute-start = (bf16[256,512]{1,0:T(8,128)(2,1)S(1)}, bf16[256,512]{1,0:T(8,128)(2,1)S(1)}, u32[]{:S(2)}, u32[]{:S(2)}) collective-permute-start(bf16[256,512]{1,0:T(8,128)(2,1)S(1)} %get-tuple-element.19), channel_id=1, source_target_pairs={{0,32},{32,64},{64,96},{96,128},{128,160},{160,192},{192,224},{224... | collective-permute-start | bytes 786440 | tf_op jit(solution)/shard_map/ppermute | solution.py:15
  19.4 10.0 %collective-permute-done = bf16[256,512]{1,0:T(8,128)(2,1)S(1)} collective-permute-done((bf16[256,512]{1,0:T(8,128)(2,1)S(1)}, bf16[256,512]{1,0:T(8,128)(2,1)S(1)}, u32[]{:S(2)}, u32[]{:S(2)}) %collective-permute-start) | collective-permute-done | bytes 262176 | tf_op jit(solution)/shard_map/ppermute | solution.py:15
  29.4 0.0 copy-done
  29.4 0.0 copy-start.3
  29.4 2.4 %fusion.10 = f32[512,1024]{0,1:T(8,128)S(1)} fusion(bf16[1024,1024]{1,0:T(8,128)(2,1)S(1)} %copy-done, bf16[512,512]{1,0:T(8,128)(2,1)} %bitcast.30, bf16[256,512]{1,0:T(8,128)(2,1)S(1)} %get-tuple-element.20, bf16[256,512]{1,0:T(8,128)(2,1)S(1)} %collective-permute-done), kind=kOutput, calls=%fused_computation.25 | convolution fusion | flops 1076887552 | bytes 5242880 | tf_op jit(solution)/shard_map/dot_general | solution.py:20
  31.8 0.0 copy-done.3
  31.8 0.0 copy-start.6
  31.8 1.4 %convolution_convert_fusion.1 = bf16[512,512]{1,0:T(8,128)(2,1)} fusion(f32[512,1024]{0,1:T(8,128)S(1)} %fusion.10, bf16[1,512,512]{2,1,0:T(8,128)(2,1)S(1)} %copy-done.3, f32[512]{0:T(512)S(1)} %fusion.11), kind=kOutput, calls=%fused_computation.2 | convolution fusion | flops 270270464 | bytes 3147776 | tf_op jit(solution)/shard_map/tk,tn->kn/dot_general | solution.py:297
  33.2 0.0 copy-done.6
  33.2 0.8 multiply_convert_fusion.2
  34.0 1.3 %fusion.3 = f32[512,1024]{1,0:T(8,128)S(1)} fusion(bf16[1024,1024]{1,0:T(8,128)(2,1)S(1)} %copy-done, bf16[512,512]{0,1:T(8,128)(2,1)S(1)} %get-tuple-element.18, bf16[512,512]{0,1:T(8,128)(2,1)S(1)} %get-tuple-element.17), kind=kOutput, calls=%fused_computation.13 | convolution fusion | flops 1075838976 | bytes 5242880 | tf_op jit(solution)/shard_map/dot_general | solution.py:295
  35.4 0.0 copy-start.1
  35.4 0.0 copy-start.2
  35.4 0.7 slice.95.edge_ref
  36.1 0.6 copy-done.1
  36.8 0.1 fusion.6
  36.9 0.0 copy-done.2
  36.9 2.6 %convolution_convert_fusion = bf16[1024,1024]{1,0:T(8,128)(2,1)} fusion(bf16[512,512]{0,1:T(8,128)(2,1)S(1)} %get-tuple-element.18, bf16[512,512]{0,1:T(8,128)(2,1)S(1)} %get-tuple-element.17, bf16[512,512]{1,0:T(8,128)(2,1)S(1)} %bitcast.31, bf16[256,512]{1,0:T(8,128)(2,1)S(1)} %get-tuple-element.20, bf16[256,512]{1,0:T(8,128)(2,1)S(1)} %collective-permute-done), kind=kOutput, calls=%fused_computation | convolution fusion | flops 1080033280 | bytes 4194304 | tf_op jit(solution)/shard_map/tk,tn->kn/dot_general | solution.py:296
  39.6 43.7 %shard_map.76 = (f32[32,64]{1,0:T(8,128)}, f32[16,32]{1,0:T(8,128)}, bf16[256,512]{1,0:T(8,128)(2,1)}) custom-call(bf16[4,2,2,64,1024]{4,3,2,1,0:T(8,128)(2,1)} %bitcast.29, bf16[4,2,2,32,512]{4,3,2,1,0:T(8,128)(2,1)} %bitcast.32, bf16[256,512]{1,0:T(8,128)(2,1)} %slice.95.edge_ref), custom_call_target="tpu_custom_call" | custom-call | tf_op jit(solution)/shard_map/pallas_call | solution.py:312
  83.2 0.0 copy-start.4
  83.3 0.0 copy-start.5
  83.3 1.2 %fusion.5 = bf16[256,512]{1,0:T(8,128)(2,1)S(1)} fusion(f32[512,1024]{1,0:T(8,128)} %copy-done.1, bf16[256,512]{1,0:T(8,128)(2,1)} %get-tuple-element.14, bf16[1,512,512]{2,1,0:T(8,128)(2,1)S(1)} %copy-done.3), kind=kLoop, calls=%fused_computation.16 | loop fusion | flops 655360 | bytes 1310720 | tf_op jit(solution)/shard_map/convert_element_type | solution.py:316
  84.5 0.8 maximum_bitcast_fusion
  85.3 0.0 copy-done.4
  85.3 0.6 copy.14
  85.9 0.0 copy-done.5
  85.9 0.6 copy.15
  (1 shorter events, 0.0 us)
Async XLA Ops:
  0.6 28.8 %copy-start = (bf16[1024,1024]{1,0:T(8,128)(2,1)S(1)}, bf16[1024,1024]{1,0:T(8,128)(2,1)}, u32[]{:S(2)}) copy-start(bf16[1024,1024]{1,0:T(8,128)(2,1)} %param.7) | copy-start | bytes 6291460
  1.9 27.5 %collective-permute-start = (bf16[256,512]{1,0:T(8,128)(2,1)S(1)}, bf16[256,512]{1,0:T(8,128)(2,1)S(1)}, u32[]{:S(2)}, u32[]{:S(2)}) collective-permute-start(bf16[256,512]{1,0:T(8,128)(2,1)S(1)} %get-tuple-element.19), channel_id=1, source_target_pairs={{0,32},{32,64},{64,96},{96,128},{128,160},{160,192},{192,224},{224... | collective-permute-start | bytes 786440 | tf_op jit(solution)/shard_map/ppermute | solution.py:15
  29.4 2.4 %copy-start.3 = (bf16[1,512,512]{2,1,0:T(8,128)(2,1)S(1)}, bf16[1,512,512]{2,1,0:T(8,128)(2,1)}, u32[]{:S(2)}) copy-start(bf16[1,512,512]{2,1,0:T(8,128)(2,1)} %param.6) | copy-start | bytes 1572868
  31.8 1.4 %copy-start.6 = (bf16[512,512]{1,0:T(8,128)(2,1)S(1)}, bf16[512,512]{1,0:T(8,128)(2,1)}, u32[]{:S(2)}) copy-start(bf16[512,512]{1,0:T(8,128)(2,1)} %param.8) | copy-start | bytes 1572868
  35.4 1.4 %copy-start.1 = (f32[512,1024]{1,0:T(8,128)}, f32[512,1024]{1,0:T(8,128)S(1)}, u32[]{:S(2)}) copy-start(f32[512,1024]{1,0:T(8,128)S(1)} %fusion.3) | copy-start | bytes 6291460
  35.4 1.6 %copy-start.2 = (bf16[1,512,512]{2,1,0:T(8,128)(2,1)S(1)}, bf16[1,512,512]{2,1,0:T(8,128)(2,1)}, u32[]{:S(2)}) copy-start(bf16[1,512,512]{2,1,0:T(8,128)(2,1)} %param.5) | copy-start | bytes 1572868
  83.2 2.1 %copy-start.4 = (f32[32,64]{1,0:T(8,128)S(1)}, f32[32,64]{1,0:T(8,128)}, u32[]{:S(2)}) copy-start(f32[32,64]{1,0:T(8,128)} %get-tuple-element.15) | copy-start | bytes 24580
  83.3 2.7 %copy-start.5 = (f32[16,32]{1,0:T(8,128)S(1)}, f32[16,32]{1,0:T(8,128)}, u32[]{:S(2)}) copy-start(f32[16,32]{1,0:T(8,128)} %get-tuple-element.16) | copy-start | bytes 6148

commit v21 on v20

--- a/solution.py
+++ b/solution.py
@@ -49,7 +49,7 @@
                sa_conv, sa_res, rya_conv, rya_res,
                sb_conv, sb_res, rxb_conv, rxb_res,
                sz_both, rz_both,
-               edge_buf, own_conv, own_res, send_sems, recv_sems, local_sems, own_sems):
+               edge_buf, own_conv, own_res, conv_v, res_v, send_sems, recv_sems, local_sems, own_sems):
         me_x = lax.axis_index("x")
         me_zh = lax.axis_index("zh")
         me_c = lax.axis_index("c")
@@ -217,17 +217,21 @@
         for d in range(1, nz):
             sz = lax.rem(me_z + nz - d, nz)
             acc = acc + rz_both[sz].astype(jnp.float32)
-        conv_out[...] = acc[:cc] * scale
-        res_out[...] = acc[cc:, :rr] * scale
+        conv_v[...] = acc[:cc] * scale
+        res_v[...] = acc[cc:, :rr] * scale
         edge.wait_recv()
-
-        @pl.when(t < n_tm - 1)
-        def _():
-            edge_out[...] = edge_buf[...]
 
         @pl.when(t == n_tm - 1)
         def _():
-            edge_out[...] = jnp.zeros_like(edge_out)
+            edge_buf[...] = jnp.zeros_like(edge_buf)
+
+        outs = [pltpu.make_async_copy(conv_v, conv_out, own_sems.at[2]),
+                pltpu.make_async_copy(res_v, res_out, own_sems.at[3]),
+                pltpu.make_async_copy(edge_buf, edge_out, own_sems.at[4])]
+        for copy in outs:
+            copy.start()
+        for copy in outs:
+            copy.wait()
 
         for copy in sends:
             copy.wait_send()
@@ -240,7 +244,7 @@
         out_shape=(jax.ShapeDtypeStruct((cc, rc), f32), jax.ShapeDtypeStruct((cr, rr), f32),
                    jax.ShapeDtypeStruct(edge_shape, bf16)),
         in_specs=[pl.BlockSpec(memory_space=pl.ANY)] * 3,
-        out_specs=(vmem, vmem, vmem),
+        out_specs=(pl.BlockSpec(memory_space=pl.ANY),) * 3,
         scratch_shapes=[
             pltpu.VMEM((nx, nzh, 1, rc, n_conv), bf16),
             pltpu.VMEM((nx, nzh, 1, rr, n_res), bf16),
@@ -263,10 +267,12 @@
             pltpu.VMEM(edge_shape, bf16),
             pltpu.VMEM((nx, nzh, 1, rc, n_conv), bf16),
             pltpu.VMEM((nx, nzh, 1, rr, n_res), bf16),
+            pltpu.VMEM((cc, rc), f32),
+            pltpu.VMEM((cr, rr), f32),
             pltpu.SemaphoreType.DMA((2, n_slots)),
             pltpu.SemaphoreType.DMA((2, n_slots)),
             pltpu.SemaphoreType.DMA((2, 3)),
-            pltpu.SemaphoreType.DMA((2,)),
+            pltpu.SemaphoreType.DMA((5,)),
         ],
         compiler_params=pltpu.CompilerParams(collective_id=0, has_side_effects=True),
     )

time: 87.3 us -> 87.3 us (level)
  no operation moved by 1% of the time
where the time goes in v21:
time: 87.3 us; the launch traced here: 86.5 us
  Pallas kernels  43.7 us (50%)
  starting transfers between devices  16.8 us (19%)
  waiting for transfers between devices  10 us (11%)
  matrix products  8.57 us (10%)
  local copies, waits for them, and re-layouts  3.85 us (4%)
  other arithmetic  2.2 us (3%)
  between operations  1.4 us (2%)
    pallas_call x1, Pallas kernels, body(): flip_conv, flip_res, incoming_gradient = reducer(conv_in, res_in, edge_rows)  43.7 us
    ppermute x1, starting transfers between devices, passed_along(): return lax.ppermute(array, axis, pairs)  16.8 us
    ppermute x1, waiting for transfers between devices, passed_along(): return lax.ppermute(array, axis, pairs)  10 us
    dot_general x1, matrix products, body(): jnp.einsum('tk,tn->kn', inputs, pre_grad, preferred_element_type=jnp.floa...  2.63 us
    dot_general x1, matrix products, gate_backward(): pre_act = jnp.dot(inputs, w_conv, preferred_element_type=jnp.float32)  2.39 us
    unnamed x16, local copies, waits for them, and re-layouts  1.89 us
  transfers between devices with their start and end apart: 1, of which 1 were waited for; matrix products, arithmetic and copies ran while one was open for 0% of the time, Pallas kernels for 0%

profile of v21, /device:TPU:1, one launch (start us, length us, event | category | flops | bytes accessed | tf_op | source)
XLA Modules:
  0.0 86.5 jit_solution(11864465490873763182)
XLA Ops:
  0.6 0.0 copy-start
  0.6 1.2 %slice_bitcast_fusion.1 = (bf16[256,512]{1,0:T(8,128)(2,1)S(1)}, bf16[256,512]{1,0:T(8,128)(2,1)S(1)}) fusion(bf16[1,512,512]{2,1,0:T(8,128)(2,1)} %param.5), kind=kLoop, calls=%fused_computation.27 | loop fusion | bytes 1048576 | tf_op jit(solution)/shard_map/slice | solution.py:293
  1.9 16.8 %collective-permute-start = (bf16[256,512]{1,0:T(8,128)(2,1)S(1)}, bf16[256,512]{1,0:T(8,128)(2,1)S(1)}, u32[]{:S(2)}, u32[]{:S(2)}) collective-permute-start(bf16[256,512]{1,0:T(8,128)(2,1)S(1)} %get-tuple-element.19), channel_id=1, source_target_pairs={{0,32},{32,64},{64,96},{96,128},{128,160},{160,192},{192,224},{224... | collective-permute-start | bytes 786440 | tf_op jit(solution)/shard_map/ppermute | solution.py:15
  19.4 10.0 %collective-permute-done = bf16[256,512]{1,0:T(8,128)(2,1)S(1)} collective-permute-done((bf16[256,512]{1,0:T(8,128)(2,1)S(1)}, bf16[256,512]{1,0:T(8,128)(2,1)S(1)}, u32[]{:S(2)}, u32[]{:S(2)}) %collective-permute-start) | collective-permute-done | bytes 262176 | tf_op jit(solution)/shard_map/ppermute | solution.py:15
  29.4 0.0 copy-done
  29.4 0.0 copy-start.3
  29.4 2.4 %fusion.10 = f32[512,1024]{0,1:T(8,128)S(1)} fusion(bf16[1024,1024]{1,0:T(8,128)(2,1)S(1)} %copy-done, bf16[512,512]{1,0:T(8,128)(2,1)} %bitcast.30, bf16[256,512]{1,0:T(8,128)(2,1)S(1)} %get-tuple-element.20, bf16[256,512]{1,0:T(8,128)(2,1)S(1)} %collective-permute-done), kind=kOutput, calls=%fused_computation.25 | convolution fusion | flops 1076887552 | bytes 5242880 | tf_op jit(solution)/shard_map/dot_general | solution.py:20
  31.8 0.0 copy-done.3
  31.8 0.0 copy-start.6
  31.8 1.4 %convolution_convert_fusion.1 = bf16[512,512]{1,0:T(8,128)(2,1)} fusion(f32[512,1024]{0,1:T(8,128)S(1)} %fusion.10, bf16[1,512,512]{2,1,0:T(8,128)(2,1)S(1)} %copy-done.3, f32[512]{0:T(512)S(1)} %fusion.11), kind=kOutput, calls=%fused_computation.2 | convolution fusion | flops 270270464 | bytes 3147776 | tf_op jit(solution)/shard_map/tk,tn->kn/dot_general | solution.py:303
  33.2 0.0 copy-done.6
  33.2 0.8 multiply_convert_fusion.2
  34.0 1.3 %fusion.3 = f32[512,1024]{1,0:T(8,128)S(1)} fusion(bf16[1024,1024]{1,0:T(8,128)(2,1)S(1)} %copy-done, bf16[512,512]{0,1:T(8,128)(2,1)S(1)} %get-tuple-element.18, bf16[512,512]{0,1:T(8,128)(2,1)S(1)} %get-tuple-element.17), kind=kOutput, calls=%fused_computation.13 | convolution fusion | flops 1075838976 | bytes 5242880 | tf_op jit(solution)/shard_map/dot_general | solution.py:301
  35.4 0.0 copy-start.1
  35.4 0.0 copy-start.2
  35.4 0.7 slice.95.edge_ref
  36.1 0.6 copy-done.1
  36.8 0.1 fusion.6
  36.9 0.0 copy-done.2
  36.9 2.6 %convolution_convert_fusion = bf16[1024,1024]{1,0:T(8,128)(2,1)} fusion(bf16[512,512]{0,1:T(8,128)(2,1)S(1)} %get-tuple-element.18, bf16[512,512]{0,1:T(8,128)(2,1)S(1)} %get-tuple-element.17, bf16[512,512]{1,0:T(8,128)(2,1)S(1)} %bitcast.31, bf16[256,512]{1,0:T(8,128)(2,1)S(1)} %get-tuple-element.20, bf16[256,512]{1,0:T(8,128)(2,1)S(1)} %collective-permute-done), kind=kOutput, calls=%fused_computation | convolution fusion | flops 1080033280 | bytes 4194304 | tf_op jit(solution)/shard_map/tk,tn->kn/dot_general | solution.py:302
  39.6 43.7 %shard_map.76 = (f32[32,64]{1,0:T(8,128)}, f32[16,32]{1,0:T(8,128)}, bf16[256,512]{1,0:T(8,128)(2,1)}) custom-call(bf16[4,2,2,64,1024]{4,3,2,1,0:T(8,128)(2,1)} %bitcast.29, bf16[4,2,2,32,512]{4,3,2,1,0:T(8,128)(2,1)} %bitcast.32, bf16[256,512]{1,0:T(8,128)(2,1)} %slice.95.edge_ref), custom_call_target="tpu_custom_call" | custom-call | tf_op jit(solution)/shard_map/pallas_call | solution.py:318
  83.3 0.0 copy-start.4
  83.3 0.0 copy-start.5
  83.3 1.2 %fusion.5 = bf16[256,512]{1,0:T(8,128)(2,1)S(1)} fusion(f32[512,1024]{1,0:T(8,128)} %copy-done.1, bf16[256,512]{1,0:T(8,128)(2,1)} %get-tuple-element.14, bf16[1,512,512]{2,1,0:T(8,128)(2,1)S(1)} %copy-done.3), kind=kLoop, calls=%fused_computation.16 | loop fusion | flops 655360 | bytes 1310720 | tf_op jit(solution)/shard_map/convert_element_type | solution.py:322
  84.5 0.8 maximum_bitcast_fusion
  85.3 0.0 copy-done.4
  85.3 0.6 copy.14
  85.9 0.0 copy-done.5
  85.9 0.6 copy.15
  (1 shorter events, 0.0 us)
Async XLA Ops:
  0.6 28.8 %copy-start = (bf16[1024,1024]{1,0:T(8,128)(2,1)S(1)}, bf16[1024,1024]{1,0:T(8,128)(2,1)}, u32[]{:S(2)}) copy-start(bf16[1024,1024]{1,0:T(8,128)(2,1)} %param.7) | copy-start | bytes 6291460
  1.9 27.5 %collective-permute-start = (bf16[256,512]{1,0:T(8,128)(2,1)S(1)}, bf16[256,512]{1,0:T(8,128)(2,1)S(1)}, u32[]{:S(2)}, u32[]{:S(2)}) collective-permute-start(bf16[256,512]{1,0:T(8,128)(2,1)S(1)} %get-tuple-element.19), channel_id=1, source_target_pairs={{0,32},{32,64},{64,96},{96,128},{128,160},{160,192},{192,224},{224... | collective-permute-start | bytes 786440 | tf_op jit(solution)/shard_map/ppermute | solution.py:15
  29.4 2.4 %copy-start.3 = (bf16[1,512,512]{2,1,0:T(8,128)(2,1)S(1)}, bf16[1,512,512]{2,1,0:T(8,128)(2,1)}, u32[]{:S(2)}) copy-start(bf16[1,512,512]{2,1,0:T(8,128)(2,1)} %param.6) | copy-start | bytes 1572868
  31.8 1.4 %copy-start.6 = (bf16[512,512]{1,0:T(8,128)(2,1)S(1)}, bf16[512,512]{1,0:T(8,128)(2,1)}, u32[]{:S(2)}) copy-start(bf16[512,512]{1,0:T(8,128)(2,1)} %param.8) | copy-start | bytes 1572868
  35.4 1.4 %copy-start.1 = (f32[512,1024]{1,0:T(8,128)}, f32[512,1024]{1,0:T(8,128)S(1)}, u32[]{:S(2)}) copy-start(f32[512,1024]{1,0:T(8,128)S(1)} %fusion.3) | copy-start | bytes 6291460
  35.4 1.6 %copy-start.2 = (bf16[1,512,512]{2,1,0:T(8,128)(2,1)S(1)}, bf16[1,512,512]{2,1,0:T(8,128)(2,1)}, u32[]{:S(2)}) copy-start(bf16[1,512,512]{2,1,0:T(8,128)(2,1)} %param.5) | copy-start | bytes 1572868
  83.3 2.1 %copy-start.4 = (f32[32,64]{1,0:T(8,128)S(1)}, f32[32,64]{1,0:T(8,128)}, u32[]{:S(2)}) copy-start(f32[32,64]{1,0:T(8,128)} %get-tuple-element.15) | copy-start | bytes 24580
  83.3 2.7 %copy-start.5 = (f32[16,32]{1,0:T(8,128)S(1)}, f32[16,32]{1,0:T(8,128)}, u32[]{:S(2)}) copy-start(f32[16,32]{1,0:T(8,128)} %get-tuple-element.16) | copy-start | bytes 6148

commit v22 on v19

--- a/solution.py
+++ b/solution.py
@@ -49,7 +49,7 @@
                sa_conv, sa_res, rya_conv, rya_res,
                sb_conv, sb_res, rxb_conv, rxb_res,
                sz_both, rz_both,
-               edge_buf, own_conv, own_res, send_sems, recv_sems, local_sems, own_sems):
+               edge_buf, own_conv, own_res, edge_f32, edge_src, send_sems, recv_sems, local_sems, own_sems):
         me_x = lax.axis_index("x")
         me_zh = lax.axis_index("zh")
         me_c = lax.axis_index("c")
@@ -103,8 +103,13 @@
             copy.start()
             return copy
 
+        edge_in = pltpu.make_async_copy(
+            edge_ref.at[pl.ds(0, edge_shape[0]), pl.ds(0, edge_shape[1])], edge_f32, own_sems.at[2])
+        edge_in.start()
+        edge_in.wait()
+        edge_src[...] = edge_f32[...].astype(jnp.bfloat16)
         edge = pltpu.make_async_remote_copy(
-            src_ref=edge_ref.at[pl.ds(0, edge_shape[0]), pl.ds(0, edge_shape[1])], dst_ref=edge_buf, send_sem=local_sems.at[0, 2],
+            src_ref=edge_src, dst_ref=edge_buf, send_sem=local_sems.at[0, 2],
             recv_sem=local_sems.at[1, 2], device_id=before, device_id_type=mesh_id)
         edge.start()
 
@@ -238,7 +243,7 @@
     return pl.pallas_call(
         kernel,
         out_shape=(jax.ShapeDtypeStruct((cc, rc), f32), jax.ShapeDtypeStruct((cr, rr), f32),
-                   jax.ShapeDtypeStruct(edge_shape, f32)),
+                   jax.ShapeDtypeStruct(edge_shape, bf16)),
         in_specs=[pl.BlockSpec(memory_space=pl.ANY)] * 3,
         out_specs=(vmem, vmem, vmem),
         scratch_shapes=[
@@ -260,13 +265,15 @@
             pltpu.VMEM((nx, nzh, hr, cyr), bf16),
             pltpu.VMEM((nz, cc + cr, rc), bf16),
             pltpu.VMEM((nz, cc + cr, rc), bf16),
-            pltpu.VMEM(edge_shape, f32),
+            pltpu.VMEM(edge_shape, bf16),
             pltpu.VMEM((nx, nzh, 1, rc, n_conv), bf16),
             pltpu.VMEM((nx, nzh, 1, rr, n_res), bf16),
+            pltpu.VMEM(edge_shape, f32),
+            pltpu.VMEM(edge_shape, bf16),
             pltpu.SemaphoreType.DMA((2, n_slots)),
             pltpu.SemaphoreType.DMA((2, n_slots)),
             pltpu.SemaphoreType.DMA((2, 3)),
-            pltpu.SemaphoreType.DMA((2,)),
+            pltpu.SemaphoreType.DMA((3,)),
         ],
         compiler_params=pltpu.CompilerParams(collective_id=0, has_side_effects=True),
     )

time: 92.1 us -> 88.3 us (0.959)
  Pallas kernels: 48.9 us -> 44.7 us
    pallas_call x1, Pallas kernels: 48.9 us -> 44.7 us  [body(): reducer(conv_in, res_in, input_gradient)]
where the time goes in v22:
time: 88.3 us; the launch traced here: 87.5 us
  Pallas kernels  44.7 us (51%)
  starting transfers between devices  16.8 us (19%)
  waiting for transfers between devices  10 us (11%)
  matrix products  8.57 us (10%)
  local copies, waits for them, and re-layouts  3.78 us (4%)
  other arithmetic  2.2 us (2%)
  between operations  1.4 us (2%)
    pallas_call x1, Pallas kernels, body(): reducer(conv_in, res_in, input_gradient)  44.7 us
    ppermute x1, starting transfers between devices, passed_along(): return lax.ppermute(array, axis, pairs)  16.8 us
    ppermute x1, waiting for transfers between devices, passed_along(): return lax.ppermute(array, axis, pairs)  10 us
    dot_general x1, matrix products, body(): jnp.einsum('tk,tn->kn', inputs, pre_grad, preferred_element_type=jnp.floa...  2.63 us
    unnamed x16, local copies, waits for them, and re-layouts  2.56 us
    dot_general x1, matrix products, gate_backward(): pre_act = jnp.dot(inputs, w_conv, preferred_element_type=jnp.float32)  2.39 us
  transfers between devices with their start and end apart: 1, of which 1 were waited for; matrix products, arithmetic and copies ran while one was open for 0% of the time, Pallas kernels for 0%

profile of v22, /device:TPU:1, one launch (start us, length us, event | category | flops | bytes accessed | tf_op | source)
XLA Modules:
  0.0 87.5 jit_solution(3729190878902162539)
XLA Ops:
  0.6 0.0 copy-start
  0.6 1.2 %slice_bitcast_fusion.1 = (bf16[256,512]{1,0:T(8,128)(2,1)S(1)}, bf16[256,512]{1,0:T(8,128)(2,1)S(1)}) fusion(bf16[1,512,512]{2,1,0:T(8,128)(2,1)} %param.5), kind=kLoop, calls=%fused_computation.26 | loop fusion | bytes 1048576 | tf_op jit(solution)/shard_map/slice | solution.py:294
  1.9 16.8 %collective-permute-start = (bf16[256,512]{1,0:T(8,128)(2,1)S(1)}, bf16[256,512]{1,0:T(8,128)(2,1)S(1)}, u32[]{:S(2)}, u32[]{:S(2)}) collective-permute-start(bf16[256,512]{1,0:T(8,128)(2,1)S(1)} %get-tuple-element.17), channel_id=1, source_target_pairs={{0,32},{32,64},{64,96},{96,128},{128,160},{160,192},{192,224},{224... | collective-permute-start | bytes 786440 | tf_op jit(solution)/shard_map/ppermute | solution.py:15
  19.4 10.0 %collective-permute-done = bf16[256,512]{1,0:T(8,128)(2,1)S(1)} collective-permute-done((bf16[256,512]{1,0:T(8,128)(2,1)S(1)}, bf16[256,512]{1,0:T(8,128)(2,1)S(1)}, u32[]{:S(2)}, u32[]{:S(2)}) %collective-permute-start) | collective-permute-done | bytes 262176 | tf_op jit(solution)/shard_map/ppermute | solution.py:15
  29.4 0.0 copy-done
  29.4 0.0 copy-start.3
  29.4 2.4 %fusion.10 = f32[512,1024]{0,1:T(8,128)S(1)} fusion(bf16[1024,1024]{1,0:T(8,128)(2,1)S(1)} %copy-done, bf16[512,512]{1,0:T(8,128)(2,1)} %bitcast.31, bf16[256,512]{1,0:T(8,128)(2,1)S(1)} %get-tuple-element.18, bf16[256,512]{1,0:T(8,128)(2,1)S(1)} %collective-permute-done), kind=kOutput, calls=%fused_computation.24 | convolution fusion | flops 1076887552 | bytes 5242880 | tf_op jit(solution)/shard_map/dot_general | solution.py:20
  31.8 0.0 copy-done.3
  31.8 0.0 copy-start.6
  31.8 1.4 %convolution_convert_fusion.1 = bf16[512,512]{1,0:T(8,128)(2,1)} fusion(f32[512,1024]{0,1:T(8,128)S(1)} %fusion.10, bf16[1,512,512]{2,1,0:T(8,128)(2,1)S(1)} %copy-done.3, f32[512]{0:T(512)S(1)} %fusion.11), kind=kOutput, calls=%fused_computation.2 | convolution fusion | flops 270270464 | bytes 3147776 | tf_op jit(solution)/shard_map/tk,tn->kn/dot_general | solution.py:304
  33.2 0.0 copy-done.6
  33.2 0.8 multiply_convert_fusion.2
  34.0 0.0 copy-start.2
  34.1 1.3 %fusion.3.edge_ref = f32[512,1024]{1,0:T(8,128)S(1)} fusion(bf16[1024,1024]{1,0:T(8,128)(2,1)S(1)} %copy-done, bf16[512,512]{0,1:T(8,128)(2,1)S(1)} %get-tuple-element.16, bf16[512,512]{0,1:T(8,128)(2,1)S(1)} %get-tuple-element.15), kind=kOutput, calls=%fused_computation.13 | convolution fusion | flops 1075838976 | bytes 5242880 | tf_op jit(solution)/shard_map/dot_general | solution.py:302
  35.4 0.0 copy-start.1
  35.4 1.3 %copy-done.1 = f32[512,1024]{1,0:T(8,128)} copy-done((f32[512,1024]{1,0:T(8,128)}, f32[512,1024]{1,0:T(8,128)S(1)}, u32[]{:S(2)}) %copy-start.1) | copy-done | bytes 2097176
  36.7 0.1 fusion.6
  36.9 0.0 copy-done.2
  36.9 2.6 %convolution_convert_fusion = bf16[1024,1024]{1,0:T(8,128)(2,1)} fusion(bf16[512,512]{0,1:T(8,128)(2,1)S(1)} %get-tuple-element.16, bf16[512,512]{0,1:T(8,128)(2,1)S(1)} %get-tuple-element.15, bf16[512,512]{1,0:T(8,128)(2,1)S(1)} %bitcast.32, bf16[256,512]{1,0:T(8,128)(2,1)S(1)} %get-tuple-element.18, bf16[256,512]{1,0:T(8,128)(2,1)S(1)} %collective-permute-done), kind=kOutput, calls=%fused_computation | convolution fusion | flops 1080033280 | bytes 4194304 | tf_op jit(solution)/shard_map/tk,tn->kn/dot_general | solution.py:303
  39.5 44.7 %shard_map.76 = (f32[32,64]{1,0:T(8,128)}, f32[16,32]{1,0:T(8,128)}, bf16[256,512]{1,0:T(8,128)(2,1)}) custom-call(bf16[4,2,2,64,1024]{4,3,2,1,0:T(8,128)(2,1)} %bitcast.29, bf16[4,2,2,32,512]{4,3,2,1,0:T(8,128)(2,1)} %bitcast.30, f32[512,1024]{1,0:T(8,128)} %copy-done.1), custom_call_target="tpu_custom_call" | custom-call | tf_op jit(solution)/shard_map/pallas_call | solution.py:319
  84.2 0.0 copy-start.4
  84.2 0.0 copy-start.5
  84.2 1.2 %fusion.5 = bf16[256,512]{1,0:T(8,128)(2,1)S(1)} fusion(f32[512,1024]{1,0:T(8,128)} %copy-done.1, bf16[256,512]{1,0:T(8,128)(2,1)} %get-tuple-element.12, bf16[1,512,512]{2,1,0:T(8,128)(2,1)S(1)} %copy-done.3), kind=kLoop, calls=%fused_computation.16 | loop fusion | flops 655360 | bytes 1310720 | tf_op jit(solution)/shard_map/convert_element_type | solution.py:323
  85.4 0.8 maximum_bitcast_fusion
  86.2 0.0 copy-done.4
  86.3 0.6 copy.14
  86.9 0.0 copy-done.5
  86.9 0.6 copy.15
  (1 shorter events, 0.0 us)
Async XLA Ops:
  0.6 28.8 %copy-start = (bf16[1024,1024]{1,0:T(8,128)(2,1)S(1)}, bf16[1024,1024]{1,0:T(8,128)(2,1)}, u32[]{:S(2)}) copy-start(bf16[1024,1024]{1,0:T(8,128)(2,1)} %param.7) | copy-start | bytes 6291460
  1.9 27.5 %collective-permute-start = (bf16[256,512]{1,0:T(8,128)(2,1)S(1)}, bf16[256,512]{1,0:T(8,128)(2,1)S(1)}, u32[]{:S(2)}, u32[]{:S(2)}) collective-permute-start(bf16[256,512]{1,0:T(8,128)(2,1)S(1)} %get-tuple-element.17), channel_id=1, source_target_pairs={{0,32},{32,64},{64,96},{96,128},{128,160},{160,192},{192,224},{224... | collective-permute-start | bytes 786440 | tf_op jit(solution)/shard_map/ppermute | solution.py:15
  29.4 2.4 %copy-start.3 = (bf16[1,512,512]{2,1,0:T(8,128)(2,1)S(1)}, bf16[1,512,512]{2,1,0:T(8,128)(2,1)}, u32[]{:S(2)}) copy-start(bf16[1,512,512]{2,1,0:T(8,128)(2,1)} %param.6) | copy-start | bytes 1572868
  31.8 1.4 %copy-start.6 = (bf16[512,512]{1,0:T(8,128)(2,1)S(1)}, bf16[512,512]{1,0:T(8,128)(2,1)}, u32[]{:S(2)}) copy-start(bf16[512,512]{1,0:T(8,128)(2,1)} %param.8) | copy-start | bytes 1572868
  34.0 2.8 %copy-start.2 = (bf16[1,512,512]{2,1,0:T(8,128)(2,1)S(1)}, bf16[1,512,512]{2,1,0:T(8,128)(2,1)}, u32[]{:S(2)}) copy-start(bf16[1,512,512]{2,1,0:T(8,128)(2,1)} %param.5) | copy-start | bytes 1572868
  35.4 1.3 %copy-start.1 = (f32[512,1024]{1,0:T(8,128)}, f32[512,1024]{1,0:T(8,128)S(1)}, u32[]{:S(2)}) copy-start(f32[512,1024]{1,0:T(8,128)S(1)} %fusion.3.edge_ref) | copy-start | bytes 6291460
  84.2 2.1 %copy-start.4 = (f32[32,64]{1,0:T(8,128)S(1)}, f32[32,64]{1,0:T(8,128)}, u32[]{:S(2)}) copy-start(f32[32,64]{1,0:T(8,128)} %get-tuple-element.13) | copy-start | bytes 24580
  84.2 2.7 %copy-start.5 = (f32[16,32]{1,0:T(8,128)S(1)}, f32[16,32]{1,0:T(8,128)}, u32[]{:S(2)}) copy-start(f32[16,32]{1,0:T(8,128)} %get-tuple-element.14) | copy-start | bytes 6148

commit v23 on v20

--- a/solution.py
+++ b/solution.py
@@ -106,7 +106,6 @@
         edge = pltpu.make_async_remote_copy(
             src_ref=edge_ref, dst_ref=edge_buf, send_sem=local_sems.at[0, 2],
             recv_sem=local_sems.at[1, 2], device_id=before, device_id_type=mesh_id)
-        edge.start()
 
         send(0, conv_ref.at[:, :, pl.ds(other_c, 1)], rc_conv, 0, peers[0])
         send(1, res_ref.at[:, :, pl.ds(other_c, 1)], rc_res, 0, peers[0])
@@ -118,6 +117,7 @@
             copy.wait()
         arrive(0, conv_ref.at[:, :, pl.ds(other_c, 1)], rc_conv, 0)
         arrive(1, res_ref.at[:, :, pl.ds(other_c, 1)], rc_res, 0)
+        edge.start()
         for x in range(nx):
             for zh in range(nzh):
                 own_c = own_conv[x, zh, 0].astype(jnp.float32)

time: 87.3 us -> 90 us (1.031)
  the two profiles are of different devices: /device:TPU:1 before, /device:TPU:3 now
where the time goes in v23:
time: 90 us; the launch traced here: 89.8 us
  Pallas kernels  47.8 us (53%)
  starting transfers between devices  16 us (18%)
  waiting for transfers between devices  10 us (11%)
  matrix products  8.57 us (10%)
  local copies, waits for them, and re-layouts  3.85 us (4%)
  other arithmetic  2.2 us (2%)
  between operations  1.4 us (2%)
    pallas_call x1, Pallas kernels, body(): flip_conv, flip_res, incoming_gradient = reducer(conv_in, res_in, edge_rows)  47.8 us
    ppermute x1, starting transfers between devices, passed_along(): return lax.ppermute(array, axis, pairs)  16 us
    ppermute x1, waiting for transfers between devices, passed_along(): return lax.ppermute(array, axis, pairs)  10 us
    dot_general x1, matrix products, body(): jnp.einsum('tk,tn->kn', inputs, pre_grad, preferred_element_type=jnp.floa...  2.63 us
    dot_general x1, matrix products, gate_backward(): pre_act = jnp.dot(inputs, w_conv, preferred_element_type=jnp.float32)  2.39 us
    unnamed x16, local copies, waits for them, and re-layouts  1.89 us
  transfers between devices with their start and end apart: 1, of which 1 were waited for; matrix products, arithmetic and copies ran while one was open for 0% of the time, Pallas kernels for 0%

profile of v23, /device:TPU:3, one launch (start us, length us, event | category | flops | bytes accessed | tf_op | source)
XLA Modules:
  0.0 89.8 jit_solution(15653094625230542691)
XLA Ops:
  0.6 0.0 copy-start
  0.6 1.2 %slice_bitcast_fusion.1 = (bf16[256,512]{1,0:T(8,128)(2,1)S(1)}, bf16[256,512]{1,0:T(8,128)(2,1)S(1)}) fusion(bf16[1,512,512]{2,1,0:T(8,128)(2,1)} %param.5), kind=kLoop, calls=%fused_computation.27 | loop fusion | bytes 1048576 | tf_op jit(solution)/shard_map/slice | solution.py:287
  1.9 16.0 %collective-permute-start = (bf16[256,512]{1,0:T(8,128)(2,1)S(1)}, bf16[256,512]{1,0:T(8,128)(2,1)S(1)}, u32[]{:S(2)}, u32[]{:S(2)}) collective-permute-start(bf16[256,512]{1,0:T(8,128)(2,1)S(1)} %get-tuple-element.19), channel_id=1, source_target_pairs={{0,32},{32,64},{64,96},{96,128},{128,160},{160,192},{192,224},{224... | collective-permute-start | bytes 786440 | tf_op jit(solution)/shard_map/ppermute | solution.py:15
  18.5 10.0 %collective-permute-done = bf16[256,512]{1,0:T(8,128)(2,1)S(1)} collective-permute-done((bf16[256,512]{1,0:T(8,128)(2,1)S(1)}, bf16[256,512]{1,0:T(8,128)(2,1)S(1)}, u32[]{:S(2)}, u32[]{:S(2)}) %collective-permute-start) | collective-permute-done | bytes 262176 | tf_op jit(solution)/shard_map/ppermute | solution.py:15
  28.6 0.0 copy-done
  28.6 0.0 copy-start.3
  28.6 2.4 %fusion.10 = f32[512,1024]{0,1:T(8,128)S(1)} fusion(bf16[1024,1024]{1,0:T(8,128)(2,1)S(1)} %copy-done, bf16[512,512]{1,0:T(8,128)(2,1)} %bitcast.30, bf16[256,512]{1,0:T(8,128)(2,1)S(1)} %get-tuple-element.20, bf16[256,512]{1,0:T(8,128)(2,1)S(1)} %collective-permute-done), kind=kOutput, calls=%fused_computation.25 | convolution fusion | flops 1076887552 | bytes 5242880 | tf_op jit(solution)/shard_map/dot_general | solution.py:20
  31.0 0.0 copy-done.3
  31.0 0.0 copy-start.6
  31.0 1.4 %convolution_convert_fusion.1 = bf16[512,512]{1,0:T(8,128)(2,1)} fusion(f32[512,1024]{0,1:T(8,128)S(1)} %fusion.10, bf16[1,512,512]{2,1,0:T(8,128)(2,1)S(1)} %copy-done.3, f32[512]{0:T(512)S(1)} %fusion.11), kind=kOutput, calls=%fused_computation.2 | convolution fusion | flops 270270464 | bytes 3147776 | tf_op jit(solution)/shard_map/tk,tn->kn/dot_general | solution.py:297
  32.4 0.0 copy-done.6
  32.4 0.8 multiply_convert_fusion.2
  33.2 1.3 %fusion.3 = f32[512,1024]{1,0:T(8,128)S(1)} fusion(bf16[1024,1024]{1,0:T(8,128)(2,1)S(1)} %copy-done, bf16[512,512]{0,1:T(8,128)(2,1)S(1)} %get-tuple-element.18, bf16[512,512]{0,1:T(8,128)(2,1)S(1)} %get-tuple-element.17), kind=kOutput, calls=%fused_computation.13 | convolution fusion | flops 1075838976 | bytes 5242880 | tf_op jit(solution)/shard_map/dot_general | solution.py:295
  34.5 0.0 copy-start.1
  34.5 0.0 copy-start.2
  34.6 0.7 slice.95.edge_ref
  35.3 0.6 copy-done.1
  36.0 0.1 fusion.6
  36.1 0.0 copy-done.2
  36.1 2.6 %convolution_convert_fusion = bf16[1024,1024]{1,0:T(8,128)(2,1)} fusion(bf16[512,512]{0,1:T(8,128)(2,1)S(1)} %get-tuple-element.18, bf16[512,512]{0,1:T(8,128)(2,1)S(1)} %get-tuple-element.17, bf16[512,512]{1,0:T(8,128)(2,1)S(1)} %bitcast.31, bf16[256,512]{1,0:T(8,128)(2,1)S(1)} %get-tuple-element.20, bf16[256,512]{1,0:T(8,128)(2,1)S(1)} %collective-permute-done), kind=kOutput, calls=%fused_computation | convolution fusion | flops 1080033280 | bytes 4194304 | tf_op jit(solution)/shard_map/tk,tn->kn/dot_general | solution.py:296
  38.7 47.8 %shard_map.76 = (f32[32,64]{1,0:T(8,128)}, f32[16,32]{1,0:T(8,128)}, bf16[256,512]{1,0:T(8,128)(2,1)}) custom-call(bf16[4,2,2,64,1024]{4,3,2,1,0:T(8,128)(2,1)} %bitcast.29, bf16[4,2,2,32,512]{4,3,2,1,0:T(8,128)(2,1)} %bitcast.32, bf16[256,512]{1,0:T(8,128)(2,1)} %slice.95.edge_ref), custom_call_target="tpu_custom_call" | custom-call | tf_op jit(solution)/shard_map/pallas_call | solution.py:312
  86.5 0.0 copy-start.4
  86.5 0.0 copy-start.5
  86.5 1.2 %fusion.5 = bf16[256,512]{1,0:T(8,128)(2,1)S(1)} fusion(f32[512,1024]{1,0:T(8,128)} %copy-done.1, bf16[256,512]{1,0:T(8,128)(2,1)} %get-tuple-element.14, bf16[1,512,512]{2,1,0:T(8,128)(2,1)S(1)} %copy-done.3), kind=kLoop, calls=%fused_computation.16 | loop fusion | flops 655360 | bytes 1310720 | tf_op jit(solution)/shard_map/convert_element_type | solution.py:316
  87.8 0.8 maximum_bitcast_fusion
  88.6 0.0 copy-done.4
  88.6 0.6 copy.14
  89.2 0.0 copy-done.5
  89.2 0.6 copy.15
  (1 shorter events, 0.0 us)
Async XLA Ops:
  0.6 27.9 %copy-start = (bf16[1024,1024]{1,0:T(8,128)(2,1)S(1)}, bf16[1024,1024]{1,0:T(8,128)(2,1)}, u32[]{:S(2)}) copy-start(bf16[1024,1024]{1,0:T(8,128)(2,1)} %param.7) | copy-start | bytes 6291460
  1.9 26.7 %collective-permute-start = (bf16[256,512]{1,0:T(8,128)(2,1)S(1)}, bf16[256,512]{1,0:T(8,128)(2,1)S(1)}, u32[]{:S(2)}, u32[]{:S(2)}) collective-permute-start(bf16[256,512]{1,0:T(8,128)(2,1)S(1)} %get-tuple-element.19), channel_id=1, source_target_pairs={{0,32},{32,64},{64,96},{96,128},{128,160},{160,192},{192,224},{224... | collective-permute-start | bytes 786440 | tf_op jit(solution)/shard_map/ppermute | solution.py:15
  28.6 2.4 %copy-start.3 = (bf16[1,512,512]{2,1,0:T(8,128)(2,1)S(1)}, bf16[1,512,512]{2,1,0:T(8,128)(2,1)}, u32[]{:S(2)}) copy-start(bf16[1,512,512]{2,1,0:T(8,128)(2,1)} %param.6) | copy-start | bytes 1572868
  31.0 1.4 %copy-start.6 = (bf16[512,512]{1,0:T(8,128)(2,1)S(1)}, bf16[512,512]{1,0:T(8,128)(2,1)}, u32[]{:S(2)}) copy-start(bf16[512,512]{1,0:T(8,128)(2,1)} %param.8) | copy-start | bytes 1572868
  34.5 1.4 %copy-start.1 = (f32[512,1024]{1,0:T(8,128)}, f32[512,1024]{1,0:T(8,128)S(1)}, u32[]{:S(2)}) copy-start(f32[512,1024]{1,0:T(8,128)S(1)} %fusion.3) | copy-start | bytes 6291460
  34.5 1.6 %copy-start.2 = (bf16[1,512,512]{2,1,0:T(8,128)(2,1)S(1)}, bf16[1,512,512]{2,1,0:T(8,128)(2,1)}, u32[]{:S(2)}) copy-start(bf16[1,512,512]{2,1,0:T(8,128)(2,1)} %param.5) | copy-start | bytes 1572868
  86.5 2.1 %copy-start.4 = (f32[32,64]{1,0:T(8,128)S(1)}, f32[32,64]{1,0:T(8,128)}, u32[]{:S(2)}) copy-start(f32[32,64]{1,0:T(8,128)} %get-tuple-element.15) | copy-start | bytes 24580
  86.5 2.7 %copy-start.5 = (f32[16,32]{1,0:T(8,128)S(1)}, f32[16,32]{1,0:T(8,128)}, u32[]{:S(2)}) copy-start(f32[16,32]{1,0:T(8,128)} %get-tuple-element.16) | copy-start | bytes 6148
